TPU v7x, 512 devices: a whole 4x4x16 slice. The times are simulated.
512 devices in a mesh: row: 16 (over y, z_hi, core), col: 32 (over x, z_lo).
Axes of the slice: x: 4, y: 4, z: 16 (z_hi: 2, z_lo: 8; z = z_hi * 8 + z_lo), core: 2. Of those that a mesh axis runs over, the one named last changes fastest.
Arguments:
- latent: bfloat16 [16, 64, 128, 320], P(None, 'row', 'col'), may hold values from -6 to 6
- conv_weight: bfloat16 [2, 3, 3, 320, 320], replicated, may hold values from -0.109375 to 0.109375
- conv_gain: float32 [2, 320], replicated, may hold values from 0.25 to 1.75
- qkv_weight: bfloat16 [3, 2048, 320], P(None, 'col'), may hold values from -0.3125 to 0.3125
- qk_gain: bfloat16 [2, 2048], P(None, 'col'), may hold values from 0.6 to 9, as said below
- out_weight: bfloat16 [2048, 320], P('col'), may hold values from -0.5 to 0.5
Outputs:
- features: bfloat16 [16, 64, 128, 320], P(None, 'row', 'col')
- mixed: bfloat16 [16, 32, 64, 320], P('row', None, 'col')
Inputs may be any that keep to these rules, and one draw needn't show every extreme that they name: `qk_gain`: positive gains.
All inputs are finite; a program needn't handle non-finite values.
Results may differ from a plain program's by a relative error of at most 0.035.
Values may be sent and summed in bfloat16 or wider, within the bound.
No kernel may reach another device: no remote copies, remote signals or barrier semaphores. Data moves between devices by JAX's collectives and lax.ppermute only.
A program may use at most 64 MiB of HBM per device.

v0:
```python
import math

import jax
import jax.numpy as jnp
from jax import lax
from jax.sharding import PartitionSpec as P


def with_halo(array, sides, width):
    for axis, dim in sides:
        size, length = (lax.axis_size(axis), array.shape[dim])
        up = [(i, (i + 1) % size) for i in range(size)]
        down = [(j, i) for i, j in up]
        last = lax.slice_in_dim(array, length - width, length, axis=dim)
        leading = lax.slice_in_dim(array, 0, width, axis=dim)
        before = lax.ppermute(last, axis, up)
        after = lax.ppermute(leading, axis, down)
        array = jnp.concatenate([before, array, after], axis=dim)
    return array


def from_partner(array, axis, bit):
    return lax.ppermute(array, axis, [(i, i ^ 1 << bit) for i in range(lax.axis_size(axis))])


def rms_silu(hidden, gain_row):
    factor = lax.rsqrt(jnp.mean(hidden * hidden, axis=-1, keepdims=True) + 1e-06)
    return jax.nn.silu(hidden * factor * gain_row).astype(jnp.bfloat16)


def conv_taps(padded, kernels, out_rows, out_cols):
    image_count = padded.shape[0]
    channels = padded.shape[-1]
    total = jnp.zeros((image_count * out_rows * out_cols, kernels.shape[-1]), jnp.float32)
    for row_tap in range(3):
        for col_tap in range(3):
            window = padded[:, row_tap : row_tap + out_rows, col_tap : col_tap + out_cols]
            total = total + jnp.dot(
                window.reshape(image_count * out_rows * out_cols, channels),
                kernels[row_tap, col_tap],
                preferred_element_type=jnp.float32,
            )
    return total.reshape(image_count, out_rows, out_cols, kernels.shape[-1])


def head_norm(projected, gain_row):
    factor = lax.rsqrt(jnp.mean(projected * projected, axis=-1, keepdims=True) + 1e-06)
    return (projected * factor * gain_row.astype(jnp.float32)).astype(jnp.bfloat16)


def project(source, matrix):
    return lax.dot_general(
        source, matrix, (((1,), (1,)), ((), ())), preferred_element_type=jnp.float32
    )


def shards(latent, conv_weight, conv_gain, qkv_weight, qk_gain, out_weight):
    image_count, rows_tile, cols_tile, channels = latent.shape
    layer_count = conv_weight.shape[0]
    col_count = lax.axis_size("col")
    half_bit = lax.axis_index("col") % 2
    hidden = latent
    for layer_index in range(layer_count):
        activation = rms_silu(hidden.astype(jnp.float32), conv_gain[layer_index])
        padded = with_halo(activation, (("row", 1), ("col", 2)), 1)
        conv_sum = conv_taps(padded, conv_weight[layer_index], rows_tile, cols_tile)
        hidden = (hidden.astype(jnp.float32) + conv_sum).astype(jnp.bfloat16)
    tok_rows = rows_tile // 2
    tok_cols = cols_tile // 2
    pooled = (
        hidden.astype(jnp.float32)
        .reshape(image_count, tok_rows, 2, tok_cols, 2, channels)
        .mean(axis=(2, 4))
        .astype(jnp.bfloat16)
    )
    own_strip = lax.all_to_all(pooled, "row", split_axis=0, concat_axis=1, tiled=True)[0]
    image_tok = lax.all_gather(own_strip, "col", axis=1, tiled=True)
    partner_parts = from_partner((qkv_weight, qk_gain, out_weight), "col", 0)

    def join_halves(own_part, far_part, dim):
        lower_part = jnp.where(half_bit == 0, own_part, far_part)
        upper_part = jnp.where(half_bit == 0, far_part, own_part)
        return jnp.concatenate((lower_part, upper_part), dim)

    head_weight = join_halves(qkv_weight, partner_parts[0], 1)
    head_gain = join_halves(qk_gain, partner_parts[1], 1)
    head_out = join_halves(out_weight, partner_parts[2], 0)
    head_dim = head_weight.shape[1]
    scale = head_dim ** (-0.5)
    all_rows = image_tok.shape[0]
    all_tokens = image_tok.reshape(-1, channels)
    split_view = image_tok.reshape(all_rows, col_count, 2, tok_cols // 2, channels)
    own_tokens = lax.dynamic_index_in_dim(split_view, half_bit, 2, keepdims=False).reshape(
        -1, channels
    )
    own_count = own_tokens.shape[0]
    query_norm = head_norm(project(own_tokens, head_weight[0]), head_gain[0])
    key_norm = head_norm(project(all_tokens, head_weight[1]), head_gain[1])
    value_rows = project(all_tokens, head_weight[2]).astype(jnp.bfloat16)
    block_rows = math.gcd(own_count, 512)

    def one_block(query_block):
        scores = project(query_block, key_norm) * scale
        shifted = jnp.exp(scores - jnp.max(scores, axis=1, keepdims=True))
        return jnp.dot(
            shifted.astype(jnp.bfloat16), value_rows, preferred_element_type=jnp.float32
        ) / jnp.sum(shifted, axis=1, keepdims=True)

    attended = lax.map(one_block, query_norm.reshape(own_count // block_rows, block_rows, head_dim))
    attended = attended.reshape(own_count, head_dim).astype(jnp.bfloat16)
    head_terms = jnp.dot(attended, head_out, preferred_element_type=jnp.float32)
    head_terms = head_terms.reshape(all_rows, col_count, tok_cols // 2, channels)
    returned = lax.all_to_all(
        head_terms.astype(jnp.bfloat16), "col", split_axis=1, concat_axis=1, tiled=True
    ).astype(head_terms.dtype)
    summed = returned.reshape(all_rows, col_count // 2, 2, tok_cols // 2, channels).sum(axis=1)
    summed = summed.reshape(all_rows, tok_cols, channels)
    mixed = (own_strip.astype(jnp.float32) + summed).astype(jnp.bfloat16)
    return (hidden, mixed[None])


def solution(mesh):
    placed = (
        P(None, "row", "col", None),
        P(),
        P(),
        P(None, "col", None),
        P(None, "col"),
        P("col", None),
    )
    return jax.shard_map(
        shards,
        mesh=mesh,
        in_specs=placed,
        out_specs=(P(None, "row", "col", None), P("row", None, "col", None)),
        check_vma=False,
    )
```

profile of v0, /device:TPU:16, one launch (start us, length us, event | category | flops | bytes accessed | tf_op | source)
XLA Modules:
  0.0 428.6 jit_solution(16978137172392012358)
XLA Ops:
  7.2 0.8 slice_reduce_fusion
  8.0 1.1 fusion.23
  9.1 1.2 fusion.28
  10.4 1.9 collective-permute-start
  12.4 15.0 %collective-permute-start.1 = (bf16[16,1,4,320]{3,2,1,0:T(4,128)(2,1)S(1)}, bf16[16,1,4,320]{3,2,1,0:T(4,128)(2,1)S(1)}, u32[]{:S(2)}, u32[]{:S(2)}) collective-permute-start(bf16[16,1,4,320]{3,2,1,0:T(4,128)(2,1)S(1)} %get-tuple-element.121), channel_id=1, source_target_pairs={{32,0},{64,32},{96,64},{128,96},{160,128},{192,160},{224,192},{256... | collective-permute-start | bytes 122888 | tf_op jit(solution)/shard_map/ppermute | solution.py:17
  27.4 4.1 slice_bitcast_fusion
  31.5 0.8 reshape.165
  32.5 0.9 fusion.66
  33.5 2.9 collective-permute-start.2
  36.4 12.6 %collective-permute-start.3 = (bf16[16,6,1,320]{3,2,1,0:T(2,128)(2,1)}, bf16[16,6,1,320]{3,2,1,0:T(2,128)(2,1)S(1)}, u32[]{:S(2)}, u32[]{:S(2)}) collective-permute-start(bf16[16,6,1,320]{3,2,1,0:T(2,128)(2,1)} %get-tuple-element.113), channel_id=1, source_target_pairs={{1,0},{2,1},{3,2},{4,3},{5,4},{6,5},{7,6},{8,7},{9,8},{10,9},{11,1... | collective-permute-start | bytes 184328 | tf_op jit(solution)/shard_map/ppermute | solution.py:17
  49.3 1.2 fusion.40
  50.5 0.8 reshape.168
  51.3 0.6 collective-permute-done.3
  51.9 0.6 maximum_maximum_fusion
  52.5 1.1 fusion.63
  53.6 1.7 reshape.161
  55.3 0.8 reshape.163
  56.1 0.8 reshape.164
  57.1 1.4 fusion.39
  58.5 1.3 convolution_add_fusion.13
  59.9 1.3 convolution_add_fusion.12
  63.8 8.6 %collective-permute-start.4 = (bf16[16,1,4,320]{3,2,1,0:T(4,128)(2,1)S(1)}, bf16[16,1,4,320]{3,2,1,0:T(4,128)(2,1)S(1)}, u32[]{:S(2)}, u32[]{:S(2)}) collective-permute-start(bf16[16,1,4,320]{3,2,1,0:T(4,128)(2,1)S(1)} %get-tuple-element.116), channel_id=1, source_target_pairs={{0,32},{32,64},{64,96},{96,128},{128,160},{160,192},{192,224},{224... | collective-permute-start | bytes 122888 | tf_op jit(solution)/shard_map/ppermute | solution.py:16
  72.4 6.6 %collective-permute-start.5 = (bf16[16,1,4,320]{3,2,1,0:T(4,128)(2,1)S(1)}, bf16[16,1,4,320]{3,2,1,0:T(4,128)(2,1)S(1)}, u32[]{:S(2)}, u32[]{:S(2)}) collective-permute-start(bf16[16,1,4,320]{3,2,1,0:T(4,128)(2,1)S(1)} %get-tuple-element.117), channel_id=1, source_target_pairs={{32,0},{64,32},{96,64},{128,96},{160,128},{192,160},{224,192},{256... | collective-permute-start | bytes 122888 | tf_op jit(solution)/shard_map/ppermute | solution.py:17
  79.0 0.8 reshape.175
  79.7 1.0 collective-permute-done.5
  81.2 0.9 fusion.65
  82.2 1.9 collective-permute-start.6
  84.1 13.2 %collective-permute-start.7 = (bf16[16,6,1,320]{3,2,1,0:T(2,128)(2,1)}, bf16[16,6,1,320]{3,2,1,0:T(2,128)(2,1)}, u32[]{:S(2)}, u32[]{:S(2)}) collective-permute-start(bf16[16,6,1,320]{3,2,1,0:T(2,128)(2,1)} %get-tuple-element.109), channel_id=1, source_target_pairs={{1,0},{2,1},{3,2},{4,3},{5,4},{6,5},{7,6},{8,7},{9,8},{10,9},{11,1... | collective-permute-start | bytes 184328 | tf_op jit(solution)/shard_map/ppermute | solution.py:17
  97.6 0.8 reshape.178
  98.5 0.7 copy-done.17
  99.2 0.9 collective-permute-done.7
  100.0 1.7 maximum_maximum_fusion.1
  101.8 0.9 fusion.61
  102.7 1.7 reshape.171
  104.3 1.0 fusion.62
  105.3 1.7 reshape.173
  107.1 1.7 reshape.174
  108.8 1.0 reshape.176
  109.8 0.8 reshape.177
  110.6 1.1 reshape.179
  112.3 1.3 convolution_add_fusion.5
  116.2 31.2 %all_to_all.14 = bf16[16,2,2,320]{3,1,2,0:T(2,128)(2,1)S(1)} all-to-all(bf16[16,2,2,320]{3,1,2,0:T(2,128)(2,1)S(1)} %copy.78), channel_id=1, replica_groups=mesh['row'=16,'col'=32] {'row'}, dimensions={0} | all-to-all | bytes 81920 | tf_op jit(solution)/shard_map/all_to_all | solution.py:76
  147.5 0.6 copy.82
  148.1 1.9 collective-permute-start.8
  150.1 3.9 collective-permute-start.9
  154.2 1.9 collective-permute-start.10
  156.2 4.3 collective-permute-done.10
  160.5 0.7 broadcast_select_fusion.3
  161.2 210.3 %all-gather.2.cloned.1.call-done = bf16[32,64,320]{2,0,1:T(8,128)(2,1)} async-done(((bf16[32,2,320]{2,0,1:T(8,128)(2,1)}), bf16[32,64,320]{2,0,1:T(8,128)(2,1)}) %all-gather.2.cloned.1.call-update) | async-done | bytes 1310736 | tf_op jit(solution)/shard_map/all_gather | solution.py:77
  371.4 1.9 copy.84
  373.4 0.6 multiply_reduce_fusion.1
  374.1 0.6 convolution_convert_fusion
  375.8 0.5 multiply_reduce_fusion.2
  376.6 5.1 %while.10 = (s32[]{:T(128)}, bf16[2,512,128]{2,1,0:T(8,128)(2,1)S(1)}, bf16[2,512,128]{2,1,0:T(8,128)(2,1)S(1)}, bf16[2048,128]{1,0:T(8,128)(2,1)S(1)}, bf16[2048,128]{1,0:T(8,128)(2,1)S(1)}, /*index=5*/s32[]{:T(128)}) while((s32[]{:T(128)}, bf16[2,512,128]{2,1,0:T(8,128)(2,1)S(1)}, bf16[2,512,128]{2,1,0:T(8,128)(2,1)S(1)}, ...), condition=%wide.region_8.9_spmd, body=%wide.region_5.8_spmd.sunk | while | flops 545324032 | bytes 14035021 | solution.py:109
  376.6 0.8 multiply_reduce_fusion.4
  377.4 0.8 fusion.101
  378.2 0.9 fusion.102
  379.1 0.8 multiply_reduce_fusion.4
  379.9 0.8 fusion.101
  380.7 0.9 fusion.102
  382.1 1.2 copy.89
  383.3 11.4 %all-to-all-start.1 = ((bf16[32,32,1,320]{3,0,2,1:T(8,128)(2,1)}), bf16[32,32,1,320]{3,0,2,1:T(8,128)(2,1)S(1)}, u32[]{:S(2)}, u32[]{:S(2)}) async-start(bf16[32,32,1,320]{3,0,2,1:T(8,128)(2,1)} %copy.89), calls=%async_computation.1 | async-start | bytes 1572864 | tf_op jit(solution)/shard_map/all_to_all | solution.py:113
  394.8 26.2 %all-to-all-done.1 = bf16[32,32,1,320]{3,0,2,1:T(8,128)(2,1)S(1)} async-done(((bf16[32,32,1,320]{3,0,2,1:T(8,128)(2,1)}), bf16[32,32,1,320]{3,0,2,1:T(8,128)(2,1)S(1)}, u32[]{:S(2)}, u32[]{:S(2)}) %all-to-all-start.1) | async-done | bytes 655392 | tf_op jit(solution)/shard_map/all_to_all | solution.py:113
  421.1 0.7 copy.91
  (106 shorter events, 9.8 us)
Async XLA Ops:
  7.2 364.3 %all-gather.2.cloned.1.call-start = ((), (), s32[]{:S(2)}) async-start(), calls=%async_computation.2 | async-start | bytes 1622016 | tf_op jit(solution)/shard_map/all_gather | solution.py:77
  10.4 21.9 %collective-permute-start = (bf16[16,1,4,320]{3,2,1,0:T(4,128)(2,1)S(1)}, bf16[16,1,4,320]{3,2,1,0:T(4,128)(2,1)S(1)}, u32[]{:S(2)}, u32[]{:S(2)}) collective-permute-start(bf16[16,1,4,320]{3,2,1,0:T(4,128)(2,1)S(1)} %get-tuple-element.120), channel_id=1, source_target_pairs={{0,32},{32,64},{64,96},{96,128},{128,160},{160,192},{192,224},{224... | collective-permute-start | bytes 122888 | tf_op jit(solution)/shard_map/ppermute | solution.py:16
  12.4 20.0 %collective-permute-start.1 = (bf16[16,1,4,320]{3,2,1,0:T(4,128)(2,1)S(1)}, bf16[16,1,4,320]{3,2,1,0:T(4,128)(2,1)S(1)}, u32[]{:S(2)}, u32[]{:S(2)}) collective-permute-start(bf16[16,1,4,320]{3,2,1,0:T(4,128)(2,1)S(1)} %get-tuple-element.121), channel_id=1, source_target_pairs={{32,0},{64,32},{96,64},{128,96},{160,128},{192,160},{224,192},{256... | collective-permute-start | bytes 122888 | tf_op jit(solution)/shard_map/ppermute | solution.py:17
  33.5 17.8 %collective-permute-start.2 = (bf16[16,6,1,320]{3,2,1,0:T(2,128)(2,1)}, bf16[16,6,1,320]{3,2,1,0:T(2,128)(2,1)S(1)}, u32[]{:S(2)}, u32[]{:S(2)}) collective-permute-start(bf16[16,6,1,320]{3,2,1,0:T(2,128)(2,1)} %get-tuple-element.112), channel_id=1, source_target_pairs={{0,1},{1,2},{2,3},{3,4},{4,5},{5,6},{6,7},{7,8},{8,9},{9,10},{10,1... | collective-permute-start | bytes 184328 | tf_op jit(solution)/shard_map/ppermute | solution.py:16
  36.4 15.5 %collective-permute-start.3 = (bf16[16,6,1,320]{3,2,1,0:T(2,128)(2,1)}, bf16[16,6,1,320]{3,2,1,0:T(2,128)(2,1)S(1)}, u32[]{:S(2)}, u32[]{:S(2)}) collective-permute-start(bf16[16,6,1,320]{3,2,1,0:T(2,128)(2,1)} %get-tuple-element.113), channel_id=1, source_target_pairs={{1,0},{2,1},{3,2},{4,3},{5,4},{6,5},{7,6},{8,7},{9,8},{10,9},{11,1... | collective-permute-start | bytes 184328 | tf_op jit(solution)/shard_map/ppermute | solution.py:17
  57.0 4.5 %copy-start.5 = (bf16[256,320]{1,0:T(8,128)(2,1)S(1)}, bf16[256,320]{1,0:T(8,128)(2,1)}, u32[]{:S(2)}) copy-start(bf16[256,320]{1,0:T(8,128)(2,1)} %reshape.165) | copy-start | bytes 491524
  57.1 4.1 copy-start
  57.1 4.1 copy-start.11
  61.3 1.3 copy-start.7
  62.2 0.9 copy-start.2
  63.8 16.0 %collective-permute-start.4 = (bf16[16,1,4,320]{3,2,1,0:T(4,128)(2,1)S(1)}, bf16[16,1,4,320]{3,2,1,0:T(4,128)(2,1)S(1)}, u32[]{:S(2)}, u32[]{:S(2)}) collective-permute-start(bf16[16,1,4,320]{3,2,1,0:T(4,128)(2,1)S(1)} %get-tuple-element.116), channel_id=1, source_target_pairs={{0,32},{32,64},{64,96},{96,128},{128,160},{160,192},{192,224},{224... | collective-permute-start | bytes 122888 | tf_op jit(solution)/shard_map/ppermute | solution.py:16
  72.4 8.3 %collective-permute-start.5 = (bf16[16,1,4,320]{3,2,1,0:T(4,128)(2,1)S(1)}, bf16[16,1,4,320]{3,2,1,0:T(4,128)(2,1)S(1)}, u32[]{:S(2)}, u32[]{:S(2)}) collective-permute-start(bf16[16,1,4,320]{3,2,1,0:T(4,128)(2,1)S(1)} %get-tuple-element.117), channel_id=1, source_target_pairs={{32,0},{64,32},{96,64},{128,96},{160,128},{192,160},{224,192},{256... | collective-permute-start | bytes 122888 | tf_op jit(solution)/shard_map/ppermute | solution.py:17
  79.7 17.5 %copy-start.12 = (bf16[16,1,4,320]{3,2,1,0:T(4,128)(2,1)}, bf16[16,1,4,320]{3,2,1,0:T(4,128)(2,1)S(1)}, u32[]{:S(2)}) copy-start(bf16[16,1,4,320]{3,2,1,0:T(4,128)(2,1)S(1)} %collective-permute-done.4) | copy-start | bytes 122884
  80.7 16.6 %copy-start.13 = (bf16[16,1,4,320]{3,2,1,0:T(4,128)(2,1)}, bf16[16,1,4,320]{3,2,1,0:T(4,128)(2,1)S(1)}, u32[]{:S(2)}) copy-start(bf16[16,1,4,320]{3,2,1,0:T(4,128)(2,1)S(1)} %collective-permute-done.5) | copy-start | bytes 122884
  82.2 16.3 %collective-permute-start.6 = (bf16[16,6,1,320]{3,2,1,0:T(2,128)(2,1)}, bf16[16,6,1,320]{3,2,1,0:T(2,128)(2,1)S(1)}, u32[]{:S(2)}, u32[]{:S(2)}) collective-permute-start(bf16[16,6,1,320]{3,2,1,0:T(2,128)(2,1)} %get-tuple-element.108), channel_id=1, source_target_pairs={{0,1},{1,2},{2,3},{3,4},{4,5},{5,6},{6,7},{7,8},{8,9},{9,10},{10,1... | collective-permute-start | bytes 184328 | tf_op jit(solution)/shard_map/ppermute | solution.py:16
  84.1 16.0 %collective-permute-start.7 = (bf16[16,6,1,320]{3,2,1,0:T(2,128)(2,1)}, bf16[16,6,1,320]{3,2,1,0:T(2,128)(2,1)}, u32[]{:S(2)}, u32[]{:S(2)}) collective-permute-start(bf16[16,6,1,320]{3,2,1,0:T(2,128)(2,1)} %get-tuple-element.109), channel_id=1, source_target_pairs={{1,0},{2,1},{3,2},{4,3},{5,4},{6,5},{7,6},{8,7},{9,8},{10,9},{11,1... | collective-permute-start | bytes 184328 | tf_op jit(solution)/shard_map/ppermute | solution.py:17
  98.5 0.7 copy-start.17
  105.3 6.6 %copy-start.8 = (bf16[256,320]{1,0:T(8,128)(2,1)S(1)}, bf16[256,320]{1,0:T(8,128)(2,1)}, u32[]{:S(2)}) copy-start(bf16[256,320]{1,0:T(8,128)(2,1)} %reshape.171) | copy-start | bytes 491524
  110.6 3.3 copy-start.4
  111.6 1.9 copy-start.10
  112.2 2.2 copy-start.9
  113.5 1.2 copy-start.6
  115.1 33.1 %copy-start.18 = (bf16[3,64,320]{2,1,0:T(8,128)(2,1)S(1)}, bf16[3,64,320]{2,1,0:T(8,128)(2,1)}, u32[]{:S(2)}) copy-start(bf16[3,64,320]{2,1,0:T(8,128)(2,1)} %param.11) | copy-start | bytes 368644
  115.1 35.0 %copy-start.20 = (bf16[2,64]{1,0:T(2,128)(2,1)S(1)}, bf16[2,64]{1,0:T(2,128)(2,1)}, u32[]{:S(2)}) copy-start(bf16[2,64]{1,0:T(2,128)(2,1)} %param.12) | copy-start | bytes 772
  115.1 38.9 %copy-start.19 = (bf16[64,320]{1,0:T(8,128)(2,1)S(1)}, bf16[64,320]{1,0:T(8,128)(2,1)}, u32[]{:S(2)}) copy-start(bf16[64,320]{1,0:T(8,128)(2,1)} %param.13) | copy-start | bytes 122884
  115.5 257.9 %copy-start.3 = (bf16[16,4,4,320]{3,2,1,0:T(4,128)(2,1)}, bf16[16,4,4,320]{3,2,1,0:T(4,128)(2,1)S(1)}, u32[]{:S(2)}) copy-start(bf16[16,4,4,320]{3,2,1,0:T(4,128)(2,1)S(1)} %fusion.36) | copy-start | bytes 491524
  148.1 13.0 %collective-permute-start.8 = (bf16[3,64,320]{2,1,0:T(8,128)(2,1)S(1)}, bf16[3,64,320]{2,1,0:T(8,128)(2,1)S(1)}, u32[]{:S(2)}, u32[]{:S(2)}) collective-permute-start(bf16[3,64,320]{2,1,0:T(8,128)(2,1)S(1)} %copy-done.18), channel_id=1, source_target_pairs={{0,1},{1,0},{2,3},{3,2},{4,5},{5,4},{6,7},{7,6},{8,9},{9,8},{10,11... | collective-permute-start | bytes 368648 | tf_op jit(solution)/shard_map/ppermute | solution.py:23
  150.1 6.0 %collective-permute-start.9 = (bf16[2,64]{1,0:T(2,128)(2,1)S(1)}, bf16[2,64]{1,0:T(2,128)(2,1)S(1)}, u32[]{:S(2)}, u32[]{:S(2)}) collective-permute-start(bf16[2,64]{1,0:T(2,128)(2,1)S(1)} %copy-done.20), channel_id=1, source_target_pairs={{0,1},{1,0},{2,3},{3,2},{4,5},{5,4},{6,7},{7,6},{8,9},{9,8},{10,11... | collective-permute-start | bytes 776 | tf_op jit(solution)/shard_map/ppermute | solution.py:23
  154.2 6.3 %collective-permute-start.10 = (bf16[64,320]{0,1:T(8,128)(2,1)S(1)}, bf16[64,320]{0,1:T(8,128)(2,1)S(1)}, u32[]{:S(2)}, u32[]{:S(2)}) collective-permute-start(bf16[64,320]{0,1:T(8,128)(2,1)S(1)} %copy.87), channel_id=1, source_target_pairs={{0,1},{1,0},{2,3},{3,2},{4,5},{5,4},{6,7},{7,6},{8,9},{9,8},{10,11... | collective-permute-start | bytes 122888 | tf_op jit(solution)/shard_map/ppermute | solution.py:23
  374.1 1.4 copy-start.1
  375.6 1.0 copy-start.16
  376.6 5.1 %copy-start.14 = (bf16[64,320]{0,1:T(8,128)(2,1)S(1)}, bf16[64,320]{0,1:T(8,128)(2,1)}, u32[]{:S(2)}) copy-start(bf16[64,320]{0,1:T(8,128)(2,1)} %get-tuple-element.122) | copy-start | bytes 122884
  376.6 5.1 %copy-start.15 = (bf16[64,320]{0,1:T(8,128)(2,1)S(1)}, bf16[64,320]{0,1:T(8,128)(2,1)}, u32[]{:S(2)}) copy-start(bf16[64,320]{0,1:T(8,128)(2,1)} %get-tuple-element.123) | copy-start | bytes 122884
  383.3 37.7 %all-to-all-start.1 = ((bf16[32,32,1,320]{3,0,2,1:T(8,128)(2,1)}), bf16[32,32,1,320]{3,0,2,1:T(8,128)(2,1)S(1)}, u32[]{:S(2)}, u32[]{:S(2)}) async-start(bf16[32,32,1,320]{3,0,2,1:T(8,128)(2,1)} %copy.89), calls=%async_computation.1 | async-start | bytes 1572864 | tf_op jit(solution)/shard_map/all_to_all | solution.py:113
Sparse Core Ops, SparseCore 0:
  148.3 223.1 all-gather.1
where the time goes:
time: 430 us; the launch traced here: 429 us
  waiting for transfers between devices  243 us (57%)
  starting transfers between devices  81.9 us (19%)
  local copies, waits for them, and re-layouts  31.6 us (7%)
  blocking collectives  31.2 us (7%)
  matrix products  16 us (4%)
  between operations  14.9 us (3%)
  other arithmetic  9.61 us (2%)
    all_gather x1, waiting for transfers between devices, shards(): image_tok = lax.all_gather(own_strip, 'col', axis=1, tiled=True)  210 us
    ppermute x4, starting transfers between devices, with_halo(): after = lax.ppermute(leading, axis, down)  47.3 us
    all_to_all x1, blocking collectives, shards(): lax.all_to_all(pooled, 'row', split_axis=0, concat_axis=1, tiled=True)[0]  31.2 us
    all_to_all x1, waiting for transfers between devices, shards(): lax.all_to_all(head_terms.astype(jnp.bfloat16), 'col', split_axis=1, conc...  26.2 us
    ppermute x4, starting transfers between devices, with_halo(): before = lax.ppermute(last, axis, up)  15.4 us
    reshape x18, local copies, waits for them, and re-layouts, conv_taps(): window.reshape(image_count * out_rows * out_cols, channels)  14.7 us
    all_to_all x1, starting transfers between devices, shards(): lax.all_to_all(head_terms.astype(jnp.bfloat16), 'col', split_axis=1, conc...  11.4 us
    dot_general x18, matrix products, conv_taps(): jnp.dot(window.reshape(image_count * out_rows * out_cols, channels), kern...  10.4 us
  transfers between devices with their start and end apart: 13, of which 7 were waited for; matrix products, arithmetic and copies ran while one was open for 2% of the time, Pallas kernels for 0%

commit v1 on v0

v1 whole, which is shorter than its diff:
```python
import jax
import jax.numpy as jnp
from jax import lax
from jax.sharding import Mesh
from jax.sharding import PartitionSpec as P

SIZES = {"y": 4, "h": 2, "c": 2, "x": 4, "l": 8}
ROW = ("y", "h", "c")
COL = ("x", "l")
DEPTH = ("h", "l")
PLANE = ("x", "y", "c")


def move(array, axes, target):
    sizes = [SIZES[axis] for axis in axes]
    pairs = []
    count = 1
    for size in sizes:
        count *= size
    for index in range(count):
        rest, place = index, []
        for size in reversed(sizes):
            place.insert(0, rest % size)
            rest //= size
        flat = 0
        for size, value in zip(sizes, target(*place)):
            flat = flat * size + value % size
        pairs.append((index, flat))
    return lax.ppermute(array, axes, pairs)


def exchange(array, axes):
    return lax.all_to_all(array, axes, split_axis=0, concat_axis=0, tiled=True)


def rms_silu(hidden, gain_row):
    factor = lax.rsqrt(jnp.mean(hidden * hidden, axis=-1, keepdims=True) + 1e-06)
    return jax.nn.silu(hidden * factor * gain_row).astype(jnp.bfloat16)


def conv_layer(hidden, gain_row, kernels):
    strips, rows, cols, channels = hidden.shape
    wide = hidden.astype(jnp.float32)
    act = rms_silu(wide, gain_row)
    total = jnp.zeros((strips * (rows - 2) * (cols - 2), channels), jnp.float32)
    for a in range(3):
        for b in range(3):
            window = act[:, a : a + rows - 2, b : b + cols - 2].reshape(-1, channels)
            total = total + jnp.dot(window, kernels[a, b], preferred_element_type=jnp.float32)
    total = total.reshape(strips, rows - 2, cols - 2, channels)
    return (wide[:, 1:-1, 1:-1] + total).astype(jnp.bfloat16)


def head_norm(projected, gain_row):
    factor = lax.rsqrt(jnp.mean(projected * projected, axis=-1, keepdims=True) + 1e-06)
    return (projected * factor * gain_row.astype(jnp.float32)).astype(jnp.bfloat16)


def project(source, matrix):
    return lax.dot_general(
        source, matrix, (((1,), (1,)), ((), ())), preferred_element_type=jnp.float32
    )


def source_plane(y, h, l, step):
    depth = 8 * h + l + 2 * y - 4 + step
    return l // 2, (depth // 8) % 2, depth % 8


def shards(latent, conv_weight, conv_gain, qkv_weight, qk_gain, out_weight):
    channels = latent.shape[-1]
    core = lax.axis_index("c")
    first = core == 0

    slots = latent.reshape(4, 2, 2, 4, 4, channels).transpose(1, 0, 2, 3, 4, 5)
    tiles = exchange(slots.reshape(16, 4, 4, channels), DEPTH)

    gains = jnp.pad(qk_gain.reshape(1, 128), ((0, 15), (0, channels - 128)))
    packed = jnp.concatenate([qkv_weight.reshape(192, channels), out_weight, gains], 0)
    packed, tiles = lax.optimization_barrier((packed, tiles))
    parts = [
        move(packed, ("y", "h", "l"), lambda y, h, l, s=step: source_plane(y, h, l, s))
        for step in range(2)
    ]

    own = tiles.reshape(2, 8, 4, 4, channels).transpose(0, 2, 1, 3, 4).reshape(8, 32, channels)
    far = lax.ppermute(jnp.where(first, own[2:8], own[0:6]), "c", [(0, 1), (1, 0)])
    edge = move(
        jnp.where(first, own[0:2], own[6:8]), ("y", "c"), lambda y, c: (y - 1 + 2 * c, 1 - c)
    )
    top_0 = jnp.where(first, edge, far[0:2])
    low_0 = jnp.where(first, far[0:2], far[2:4])
    top_1 = jnp.where(first, far[2:4], far[4:6])
    low_1 = jnp.where(first, far[4:6], edge)
    block = jnp.concatenate([top_0, own[0:4], low_0, top_1, own[4:8], low_1], 0)
    block = block.reshape(2, 8, 32, channels)
    before = move(block[:, :, 30:32], ("x",), lambda x: (x + 1,))
    after = move(block[:, :, 0:2], ("x",), lambda x: (x - 1,))
    block = jnp.concatenate([before, block, after], 2)

    hidden = conv_layer(block, conv_gain[0], conv_weight[0])
    hidden = conv_layer(hidden, conv_gain[1], conv_weight[1])
    pooled = (
        hidden.astype(jnp.float32)
        .reshape(2, 2, 2, 16, 2, channels)
        .mean(axis=(2, 4))
        .astype(jnp.bfloat16)
        .reshape(64, channels)
    )

    tokens = exchange(jnp.broadcast_to(pooled[None], (16, 64, channels)), ("x", "y"))
    tokens = tokens.reshape(1024, channels)

    back = hidden.reshape(2, 4, 8, 4, channels).transpose(0, 2, 1, 3, 4)
    back = exchange(back.reshape(16, 4, 4, channels), DEPTH)
    features = back.reshape(2, 4, 2, 4, 4, channels).transpose(1, 0, 2, 3, 4, 5)
    features = features.reshape(16, 4, 4, channels)

    even = lax.axis_index("l") % 2 == 0
    lower = jnp.where(even, parts[0], parts[1])
    upper = jnp.where(even, parts[1], parts[0])

    def joined(start, length=64):
        return jnp.concatenate([lower[start : start + length], upper[start : start + length]], 0)

    query_gain = jnp.concatenate([lower[256, 0:64], upper[256, 0:64]])
    key_gain = jnp.concatenate([lower[256, 64:128], upper[256, 64:128]])
    query_norm = head_norm(project(tokens, joined(0)), query_gain)
    key_norm = head_norm(project(tokens, joined(64)), key_gain)
    value_rows = project(tokens, joined(128)).astype(jnp.bfloat16)
    pair = jnp.concatenate([key_norm, value_rows], 1)
    pair = jnp.concatenate([pair, lax.ppermute(pair, "c", [(0, 1), (1, 0)])], 0)
    keys, values = pair[:, :128], pair[:, 128:]

    scores = project(query_norm, keys) * (128 ** (-0.5))
    shifted = jnp.exp(scores - jnp.max(scores, axis=1, keepdims=True))
    attended = jnp.dot(shifted.astype(jnp.bfloat16), values, preferred_element_type=jnp.float32)
    attended = (attended / jnp.sum(shifted, axis=1, keepdims=True)).astype(jnp.bfloat16)
    terms = jnp.dot(attended, joined(192), preferred_element_type=jnp.float32)
    terms = (terms + tokens.astype(jnp.float32) * 0.0625).astype(jnp.bfloat16)

    terms = terms.reshape(4, 16, 8, 2, channels).transpose(0, 2, 1, 3, 4)
    terms = exchange(terms.reshape(32, 32, channels), PLANE)
    summed = terms.reshape(16, 2, 4, 2, 2, 2, channels).astype(jnp.float32).sum(0)
    mixed = summed.transpose(1, 2, 0, 3, 4, 5).reshape(64, channels).astype(jnp.bfloat16)
    mixed = move(
        mixed,
        ("y", "h", "c", "x", "l"),
        lambda y, h, c, x, l: (l // 2, h, l % 2, x, 2 * y + c),
    )
    return (features, mixed.reshape(1, 32, 2, channels))


def solution(mesh):
    planes = Mesh(mesh.devices.reshape(tuple(SIZES.values())), tuple(SIZES))
    placed = (
        P(None, ROW, COL, None),
        P(),
        P(),
        P(None, COL, None),
        P(None, COL),
        P(COL, None),
    )
    return jax.shard_map(
        shards,
        mesh=planes,
        in_specs=placed,
        out_specs=(P(None, ROW, COL, None), P(ROW, None, COL, None)),
        check_vma=False,
    )
```

time: 430 us -> 176 us (0.41)
  waiting for transfers between devices: 243 us -> 42.7 us
  blocking collectives: 31.2 us -> 0 us
  starting transfers between devices: 81.9 us -> 67.8 us
  between operations: 14.9 us -> 1.31 us
    all_gather x1 -> x0, waiting for transfers between devices: 210 us -> none  [shards(): image_tok = lax.all_gather(own_strip, 'col', axis=1, tiled=True)]
    ppermute x11 -> x8, starting transfers between devices: 70.5 us -> 31.1 us  [the longest x6 25.9 us: move(): return lax.ppermute(array, axes, pairs)]
    all_to_all x1 -> x0, blocking collectives: 31.2 us -> none  [shards(): lax.all_to_all(pooled, 'row', split_axis=0, concat_axis=1, tiled=True)[0]]
    all_to_all x1 -> x4, starting transfers between devices: 11.4 us -> 36.7 us  [exchange(): return lax.all_to_all(array, axes, split_axis=0, concat_axis=0, tiled=True)]
    all_to_all x1 -> x4, waiting for transfers between devices: 26.2 us -> 38.1 us  [exchange(): return lax.all_to_all(array, axes, split_axis=0, concat_axis=0, tiled=True)]
    reshape x21 -> x22, local copies, waits for them, and re-layouts: 15.2 us -> 22.5 us  [the longest x9 14.6 us: conv_layer(): window = act[:, a:a + rows - 2, b:b + cols - 2].reshape(-1, channels)]
    dot_general x21 -> x19, matrix products: 12.7 us -> 14.5 us  [the longest x18 8.34 us: conv_layer(): jnp.dot(window, kernels[a, b], preferred_element_type=jnp.float32)]
  transfers between devices with their start and end apart: 13 -> 12, of which waited for: 7 -> 7; matrix products, arithmetic and copies ran while one was open for 2% -> 24% of each run, Pallas kernels for 0% -> 0%
where the time goes in v1:
time: 176 us; the launch traced here: 174 us
  starting transfers between devices  67.8 us (39%)
  waiting for transfers between devices  42.7 us (24%)
  local copies, waits for them, and re-layouts  35.3 us (20%)
  matrix products  17.1 us (10%)
  other arithmetic  9.87 us (6%)
    all_to_all x4, waiting for transfers between devices, exchange(): return lax.all_to_all(array, axes, split_axis=0, concat_axis=0, tiled=True)  38.1 us
    all_to_all x4, starting transfers between devices, exchange(): return lax.all_to_all(array, axes, split_axis=0, concat_axis=0, tiled=True)  36.7 us
    ppermute x6, starting transfers between devices, move(): return lax.ppermute(array, axes, pairs)  25.9 us
    reshape x9, local copies, waits for them, and re-layouts, conv_layer(): window = act[:, a:a + rows - 2, b:b + cols - 2].reshape(-1, channels)  14.6 us
    dot_general x18, matrix products, conv_layer(): jnp.dot(window, kernels[a, b], preferred_element_type=jnp.float32)  8.34 us
    dot_general x1, matrix products, shards(): terms = jnp.dot(attended, joined(192), preferred_element_type=jnp.float32)  6.13 us
    squeeze x1, local copies, waits for them, and re-layouts, shards(): hidden = conv_layer(hidden, conv_gain[1], conv_weight[1])  4.11 us
  transfers between devices with their start and end apart: 12, of which 7 were waited for; matrix products, arithmetic and copies ran while one was open for 24% of the time, Pallas kernels for 0%

profile of v1, /device:TPU:16, one launch (start us, length us, event | category | flops | bytes accessed | tf_op | source)
XLA Modules:
  0.0 174.1 jit_solution(10882376829660735551)
XLA Ops:
  0.6 1.7 copy.57
  2.3 15.2 %all-to-all-start = ((bf16[16,4,4,320]{3,2,1,0:T(4,128)(2,1)}), bf16[16,4,4,320]{3,2,1,0:T(4,128)(2,1)S(1)}, u32[]{:S(2)}, u32[]{:S(2)}) async-start(bf16[16,4,4,320]{3,2,1,0:T(4,128)(2,1)} %bitcast.3), calls=%async_computation | async-start | bytes 393216 | tf_op jit(solution)/shard_map/all_to_all | solution.py:33
  17.5 0.7 reshape.198
  18.2 1.7 fusion.26
  19.9 4.1 %slice_bitcast_fusion = (bf16[3,3,320,320]{3,2,1,0:T(8,128)(2,1)S(1)}, bf16[3,3,320,320]{3,2,1,0:T(8,128)(2,1)}) fusion(bf16[2,3,3,320,320]{4,3,2,1,0:T(8,128)(2,1)} %param.7), kind=kLoop, calls=%fused_computation.5 | loop fusion | bytes 7372800 | tf_op jit(solution)/shard_map/squeeze | solution.py:102
  24.0 9.9 %all-to-all-done = bf16[16,4,4,320]{3,2,1,0:T(4,128)(2,1)S(1)} async-done(((bf16[16,4,4,320]{3,2,1,0:T(4,128)(2,1)}), bf16[16,4,4,320]{3,2,1,0:T(4,128)(2,1)S(1)}, u32[]{:S(2)}, u32[]{:S(2)}) %all-to-all-start) | async-done | bytes 163872 | tf_op jit(solution)/shard_map/all_to_all | solution.py:33
  34.2 1.9 %collective-permute-start = (bf16[2,32,320]{2,1,0:T(8,128)(2,1)S(1)}, bf16[2,32,320]{2,1,0:T(8,128)(2,1)S(1)}, u32[]{:S(2)}, u32[]{:S(2)}) collective-permute-start(bf16[2,32,320]{2,1,0:T(8,128)(2,1)S(1)} %slice_select_fusion.1), channel_id=1, source_target_pairs={{0,416},{32,128},{128,32},{160,256},{256,160},{288,384},{384,288},... | collective-permute-start | bytes 122888 | tf_op jit(solution)/shard_map/ppermute | solution.py:29
  36.1 3.3 %collective-permute-start.1 = (bf16[6,32,320]{2,1,0:T(8,128)(2,1)S(1)}, bf16[6,32,320]{2,1,0:T(8,128)(2,1)S(1)}, u32[]{:S(2)}, u32[]{:S(2)}) collective-permute-start(bf16[6,32,320]{2,1,0:T(8,128)(2,1)S(1)} %slice_select_fusion), channel_id=1, source_target_pairs={{0,32},{32,0},{1,33},{33,1},{2,34},{34,2},{3,35},{35,3},{4,36},{36... | collective-permute-start | bytes 368648 | tf_op jit(solution)/shard_map/ppermute | solution.py:87
  39.6 0.8 collective-permute-done.1
  40.6 0.6 concatenate.50
  41.3 3.4 %collective-permute-start.2 = (bf16[2,8,2,320]{3,2,1,0:T(2,128)(2,1)S(1)}, bf16[2,8,2,320]{3,2,1,0:T(2,128)(2,1)S(1)}, u32[]{:S(2)}, u32[]{:S(2)}) collective-permute-start(bf16[2,8,2,320]{3,2,1,0:T(2,128)(2,1)S(1)} %get-tuple-element.23), channel_id=1, source_target_pairs={{0,8},{8,16},{16,24},{24,0},{1,9},{9,17},{17,25},{25,1},{2,10},{10... | collective-permute-start | bytes 61448 | tf_op jit(solution)/shard_map/ppermute | solution.py:29
  44.7 3.7 %collective-permute-start.3 = (bf16[2,8,2,320]{3,2,1,0:T(2,128)(2,1)S(1)}, bf16[2,8,2,320]{3,2,1,0:T(2,128)(2,1)S(1)}, u32[]{:S(2)}, u32[]{:S(2)}) collective-permute-start(bf16[2,8,2,320]{3,2,1,0:T(2,128)(2,1)S(1)} %get-tuple-element.24), channel_id=1, source_target_pairs={{0,24},{8,0},{16,8},{24,16},{1,25},{9,1},{17,9},{25,17},{2,26},{10... | collective-permute-start | bytes 61448 | tf_op jit(solution)/shard_map/ppermute | solution.py:29
  48.4 4.0 %collective-permute-start.5 = (bf16[272,320]{1,0:T(8,128)(2,1)}, bf16[272,320]{1,0:T(8,128)(2,1)}, u32[]{:S(2)}, u32[]{:S(2)}) collective-permute-start(bf16[272,320]{1,0:T(8,128)(2,1)} %fusion.26), channel_id=1, source_target_pairs={{0,69},{1,70},{2,199},{3,128},{4,257},{5,258},{6,387},{7,388},{64,... | collective-permute-start | bytes 522248 | tf_op jit(solution)/shard_map/ppermute | solution.py:29
  52.4 4.1 %collective-permute-start.4 = (bf16[272,320]{1,0:T(8,128)(2,1)}, bf16[272,320]{1,0:T(8,128)(2,1)}, u32[]{:S(2)}, u32[]{:S(2)}) collective-permute-start(bf16[272,320]{1,0:T(8,128)(2,1)} %fusion.26), channel_id=1, source_target_pairs={{0,68},{1,69},{2,198},{3,199},{4,256},{5,257},{6,386},{7,387},{64,... | collective-permute-start | bytes 522248 | tf_op jit(solution)/shard_map/ppermute | solution.py:29
  56.9 0.5 multiply_convert_fusion
  57.4 1.6 fusion.48
  58.9 1.8 %reshape.212 = bf16[408,320]{1,0:T(8,128)(2,1)} reshape(bf16[2,6,34,320]{3,2,1,0:T(8,128)(2,1)} %get-tuple-element.12) | data formatting | bytes 522240 | tf_op jit(solution)/shard_map/reshape | solution.py:48
  60.8 1.8 %reshape.211 = bf16[408,320]{1,0:T(8,128)(2,1)} reshape(bf16[2,6,34,320]{3,2,1,0:T(8,128)(2,1)} %get-tuple-element.13) | data formatting | bytes 522240 | tf_op jit(solution)/shard_map/reshape | solution.py:48
  62.6 1.8 %reshape.210 = bf16[408,320]{1,0:T(8,128)(2,1)} reshape(bf16[2,6,34,320]{3,2,1,0:T(8,128)(2,1)} %get-tuple-element.14) | data formatting | bytes 522240 | tf_op jit(solution)/shard_map/reshape | solution.py:48
  64.5 1.9 %reshape.209 = bf16[408,320]{1,0:T(8,128)(2,1)} reshape(bf16[2,6,34,320]{3,2,1,0:T(8,128)(2,1)} %get-tuple-element.15) | data formatting | bytes 522240 | tf_op jit(solution)/shard_map/reshape | solution.py:48
  66.3 1.8 %reshape.208 = bf16[408,320]{1,0:T(8,128)(2,1)} reshape(bf16[2,6,34,320]{3,2,1,0:T(8,128)(2,1)} %get-tuple-element.16) | data formatting | bytes 522240 | tf_op jit(solution)/shard_map/reshape | solution.py:48
  68.2 1.8 %reshape.207 = bf16[408,320]{1,0:T(8,128)(2,1)} reshape(bf16[2,6,34,320]{3,2,1,0:T(8,128)(2,1)} %get-tuple-element.17) | data formatting | bytes 522240 | tf_op jit(solution)/shard_map/reshape | solution.py:48
  70.0 1.9 %reshape.206 = bf16[408,320]{1,0:T(8,128)(2,1)} reshape(bf16[2,6,34,320]{3,2,1,0:T(8,128)(2,1)} %get-tuple-element.18) | data formatting | bytes 522240 | tf_op jit(solution)/shard_map/reshape | solution.py:48
  71.8 0.9 reshape.205
  72.7 0.9 reshape.204
  73.6 1.6 fusion.25
  75.1 1.4 convolution_add_fusion.8
  76.6 0.4 convolution_add_fusion.7
  77.0 0.4 convolution_add_fusion.6
  77.5 0.4 convolution_add_fusion.5
  78.0 0.4 convolution_add_fusion.4
  78.5 0.4 convolution_add_fusion.3
  79.0 0.4 convolution_add_fusion.2
  79.5 0.4 convolution_add_fusion.1
  79.9 0.9 reshape.213
  81.0 1.3 multiply_reduce_fusion.2
  86.4 1.0 broadcast_in_dim.2
  87.4 8.4 %all-to-all-start.2 = ((bf16[16,64,320]{2,1,0:T(8,128)(2,1)}), bf16[16,64,320]{2,1,0:T(8,128)(2,1)S(1)}, u32[]{:S(2)}, u32[]{:S(2)}) async-start(bf16[16,64,320]{2,1,0:T(8,128)(2,1)} %broadcast_in_dim.2), calls=%async_computation.2 | async-start | bytes 1572864 | tf_op jit(solution)/shard_map/all_to_all | solution.py:33
  95.8 1.1 broadcast_select_fusion.1
  97.1 10.1 %all-to-all-done.2 = bf16[16,64,320]{2,1,0:T(8,128)(2,1)S(1)} async-done(((bf16[16,64,320]{2,1,0:T(8,128)(2,1)}), bf16[16,64,320]{2,1,0:T(8,128)(2,1)S(1)}, u32[]{:S(2)}, u32[]{:S(2)}) %all-to-all-start.2) | async-done | bytes 655392 | tf_op jit(solution)/shard_map/all_to_all | solution.py:33
  107.2 0.4 multiply_reduce_fusion.3
  107.6 0.4 convolution_convert_fusion
  108.2 1.9 %collective-permute-start.6 = (bf16[1024,256]{0,1:T(8,128)(2,1)S(1)}, bf16[1024,256]{0,1:T(8,128)(2,1)}, u32[]{:S(2)}, u32[]{:S(2)}) collective-permute-start(bf16[1024,256]{0,1:T(8,128)(2,1)S(1)} %pad_maximum_fusion.1), channel_id=1, source_target_pairs={{0,32},{32,0},{1,33},{33,1},{2,34},{34,2},{3,35},{35,3},{4,36},{36... | collective-permute-start | bytes 1572872 | tf_op jit(solution)/shard_map/ppermute | solution.py:132
  110.2 1.2 copy.73
  111.3 0.4 multiply_reduce_fusion.4
  111.7 0.4 collective-permute-done.6
  112.1 1.1 pad_maximum_fusion
  113.2 1.4 multiply_reduce_fusion
  114.7 1.9 %fusion = f32[1024]{0:T(1024)S(1)} fusion(f32[1024,2048]{1,0:T(8,128)S(1)} %get-tuple-element.57, f32[1024]{0:T(1024)S(1)} %get-tuple-element.56), kind=kLoop, calls=%fused_computation.2 | loop fusion | flops 6290432 | bytes 8396800 | tf_op jit(solution)/shard_map/reduce_sum | solution.py:138
  116.6 1.3 copy-done
  117.9 6.1 %fusion.4 = bf16[1024,320]{0,1:T(8,128)(2,1)} fusion(bf16[1024,320]{0,1:T(8,128)(2,1)S(1)} %copy-done.9, f32[1024,2048]{1,0:T(8,128)} %copy-done, f32[1024]{0:T(1024)S(1)} %get-tuple-element.56, bf16[2048,256]{0,1:T(8,128)(2,1)S(1)} %pad_maximum_fusion, f32[1024]{0:T(1024)S(1)} %fusion, bf16[64,320]{1,0:T(8,128)(2,1)S(1)} %get-tuple-element.63, ...), kind=kOutput, calls=%fused_computation.8 | convolution fusion | flops 628785152 | bytes 10330112 | tf_op jit(solution)/shard_map/dot_general | solution.py:139
  124.0 1.4 copy.74
  125.4 0.3 reshape.231
  125.9 1.2 copy.76
  127.1 6.0 %all-to-all-start.3 = ((bf16[32,32,320]{2,1,0:T(8,128)(2,1)}), bf16[32,32,320]{2,1,0:T(8,128)(2,1)S(1)}, u32[]{:S(2)}, u32[]{:S(2)}) async-start(bf16[32,32,320]{2,1,0:T(8,128)(2,1)} %copy.76), calls=%async_computation.3 | async-start | bytes 1572864 | tf_op jit(solution)/shard_map/all_to_all | solution.py:33
  133.2 0.8 copy.71
  133.9 11.7 %all-to-all-done.3 = bf16[32,32,320]{2,1,0:T(8,128)(2,1)S(1)} async-done(((bf16[32,32,320]{2,1,0:T(8,128)(2,1)}), bf16[32,32,320]{2,1,0:T(8,128)(2,1)S(1)}, u32[]{:S(2)}, u32[]{:S(2)}) %all-to-all-start.3) | async-done | bytes 655392 | tf_op jit(solution)/shard_map/all_to_all | solution.py:33
  145.7 7.1 %all-to-all-start.1 = ((bf16[16,4,4,320]{3,2,1,0:T(4,128)(2,1)}), bf16[16,4,4,320]{3,2,1,0:T(4,128)(2,1)S(1)}, u32[]{:S(2)}, u32[]{:S(2)}) async-start(bf16[16,4,4,320]{3,2,1,0:T(4,128)(2,1)} %copy.71), calls=%async_computation.1 | async-start | bytes 393216 | tf_op jit(solution)/shard_map/all_to_all | solution.py:33
  153.1 0.8 reduce
  154.1 8.8 %collective-permute-start.7 = (bf16[64,320]{1,0:T(8,128)(2,1)S(1)}, bf16[64,320]{1,0:T(8,128)(2,1)S(1)}, u32[]{:S(2)}, u32[]{:S(2)}) collective-permute-start(bf16[64,320]{1,0:T(8,128)(2,1)S(1)} %convert_element_type.102), channel_id=1, source_target_pairs={{0,0},{1,32},{2,128},{3,160},{4,256},{5,288},{6,384},{7,416},{8,8}... | collective-permute-start | bytes 122888 | tf_op jit(solution)/shard_map/ppermute | solution.py:29
  162.9 6.4 %all-to-all-done.1 = bf16[16,4,4,320]{3,2,1,0:T(4,128)(2,1)S(1)} async-done(((bf16[16,4,4,320]{3,2,1,0:T(4,128)(2,1)}), bf16[16,4,4,320]{3,2,1,0:T(4,128)(2,1)S(1)}, u32[]{:S(2)}, u32[]{:S(2)}) %all-to-all-start.1) | async-done | bytes 163872 | tf_op jit(solution)/shard_map/all_to_all | solution.py:33
  169.3 0.7 copy.72
  170.1 3.4 %collective-permute-done.7 = bf16[64,320]{1,0:T(8,128)(2,1)S(1)} collective-permute-done((bf16[64,320]{1,0:T(8,128)(2,1)S(1)}, bf16[64,320]{1,0:T(8,128)(2,1)S(1)}, u32[]{:S(2)}, u32[]{:S(2)}) %collective-permute-start.7) | collective-permute-done | bytes 40992 | tf_op jit(solution)/shard_map/ppermute | solution.py:29
  173.5 0.6 reshape.233
  (76 shorter events, 6.8 us)
Async XLA Ops:
  2.3 31.6 %all-to-all-start = ((bf16[16,4,4,320]{3,2,1,0:T(4,128)(2,1)}), bf16[16,4,4,320]{3,2,1,0:T(4,128)(2,1)S(1)}, u32[]{:S(2)}, u32[]{:S(2)}) async-start(bf16[16,4,4,320]{3,2,1,0:T(4,128)(2,1)} %bitcast.3), calls=%async_computation | async-start | bytes 393216 | tf_op jit(solution)/shard_map/all_to_all | solution.py:33
  34.0 14.4 %copy-start.10 = (f32[2,320]{1,0:T(2,128)S(1)}, f32[2,320]{1,0:T(2,128)}, u32[]{:S(2)}) copy-start(f32[2,320]{1,0:T(2,128)} %param.8) | copy-start | bytes 7684
  34.2 5.4 %collective-permute-start = (bf16[2,32,320]{2,1,0:T(8,128)(2,1)S(1)}, bf16[2,32,320]{2,1,0:T(8,128)(2,1)S(1)}, u32[]{:S(2)}, u32[]{:S(2)}) collective-permute-start(bf16[2,32,320]{2,1,0:T(8,128)(2,1)S(1)} %slice_select_fusion.1), channel_id=1, source_target_pairs={{0,416},{32,128},{128,32},{160,256},{256,160},{288,384},{384,288},... | collective-permute-start | bytes 122888 | tf_op jit(solution)/shard_map/ppermute | solution.py:29
  36.1 4.3 %collective-permute-start.1 = (bf16[6,32,320]{2,1,0:T(8,128)(2,1)S(1)}, bf16[6,32,320]{2,1,0:T(8,128)(2,1)S(1)}, u32[]{:S(2)}, u32[]{:S(2)}) collective-permute-start(bf16[6,32,320]{2,1,0:T(8,128)(2,1)S(1)} %slice_select_fusion), channel_id=1, source_target_pairs={{0,32},{32,0},{1,33},{33,1},{2,34},{34,2},{3,35},{35,3},{4,36},{36... | collective-permute-start | bytes 368648 | tf_op jit(solution)/shard_map/ppermute | solution.py:87
  41.3 15.2 %collective-permute-start.2 = (bf16[2,8,2,320]{3,2,1,0:T(2,128)(2,1)S(1)}, bf16[2,8,2,320]{3,2,1,0:T(2,128)(2,1)S(1)}, u32[]{:S(2)}, u32[]{:S(2)}) collective-permute-start(bf16[2,8,2,320]{3,2,1,0:T(2,128)(2,1)S(1)} %get-tuple-element.23), channel_id=1, source_target_pairs={{0,8},{8,16},{16,24},{24,0},{1,9},{9,17},{17,25},{25,1},{2,10},{10... | collective-permute-start | bytes 61448 | tf_op jit(solution)/shard_map/ppermute | solution.py:29
  44.7 11.8 %collective-permute-start.3 = (bf16[2,8,2,320]{3,2,1,0:T(2,128)(2,1)S(1)}, bf16[2,8,2,320]{3,2,1,0:T(2,128)(2,1)S(1)}, u32[]{:S(2)}, u32[]{:S(2)}) collective-permute-start(bf16[2,8,2,320]{3,2,1,0:T(2,128)(2,1)S(1)} %get-tuple-element.24), channel_id=1, source_target_pairs={{0,24},{8,0},{16,8},{24,16},{1,25},{9,1},{17,9},{25,17},{2,26},{10... | collective-permute-start | bytes 61448 | tf_op jit(solution)/shard_map/ppermute | solution.py:29
  48.4 47.4 %collective-permute-start.5 = (bf16[272,320]{1,0:T(8,128)(2,1)}, bf16[272,320]{1,0:T(8,128)(2,1)}, u32[]{:S(2)}, u32[]{:S(2)}) collective-permute-start(bf16[272,320]{1,0:T(8,128)(2,1)} %fusion.26), channel_id=1, source_target_pairs={{0,69},{1,70},{2,199},{3,128},{4,257},{5,258},{6,387},{7,388},{64,... | collective-permute-start | bytes 522248 | tf_op jit(solution)/shard_map/ppermute | solution.py:29
  52.4 43.4 %collective-permute-start.4 = (bf16[272,320]{1,0:T(8,128)(2,1)}, bf16[272,320]{1,0:T(8,128)(2,1)}, u32[]{:S(2)}, u32[]{:S(2)}) collective-permute-start(bf16[272,320]{1,0:T(8,128)(2,1)} %fusion.26), channel_id=1, source_target_pairs={{0,68},{1,69},{2,198},{3,199},{4,256},{5,257},{6,386},{7,387},{64,... | collective-permute-start | bytes 522248 | tf_op jit(solution)/shard_map/ppermute | solution.py:29
  72.7 3.9 %copy-start.8 = (bf16[408,320]{1,0:T(8,128)(2,1)S(1)}, bf16[408,320]{1,0:T(8,128)(2,1)}, u32[]{:S(2)}) copy-start(bf16[408,320]{1,0:T(8,128)(2,1)} %reshape.206) | copy-start | bytes 783364
  73.6 3.0 %copy-start.1 = (bf16[3,3,320,320]{3,2,1,0:T(8,128)(2,1)S(1)}, bf16[3,3,320,320]{3,2,1,0:T(8,128)(2,1)}, u32[]{:S(2)}) copy-start(bf16[3,3,320,320]{3,2,1,0:T(8,128)(2,1)} %get-tuple-element.11) | copy-start | bytes 5529604
  73.6 3.4 %copy-start.7 = (bf16[408,320]{1,0:T(8,128)(2,1)S(1)}, bf16[408,320]{1,0:T(8,128)(2,1)}, u32[]{:S(2)}) copy-start(bf16[408,320]{1,0:T(8,128)(2,1)} %reshape.207) | copy-start | bytes 783364
  76.6 1.0 copy-start.6
  77.0 1.0 copy-start.5
  77.5 1.0 copy-start.4
  78.0 1.0 copy-start.3
  78.5 1.0 copy-start.2
  87.4 19.8 %all-to-all-start.2 = ((bf16[16,64,320]{2,1,0:T(8,128)(2,1)}), bf16[16,64,320]{2,1,0:T(8,128)(2,1)S(1)}, u32[]{:S(2)}, u32[]{:S(2)}) async-start(bf16[16,64,320]{2,1,0:T(8,128)(2,1)} %broadcast_in_dim.2), calls=%async_computation.2 | async-start | bytes 1572864 | tf_op jit(solution)/shard_map/all_to_all | solution.py:33
  108.2 3.9 %collective-permute-start.6 = (bf16[1024,256]{0,1:T(8,128)(2,1)S(1)}, bf16[1024,256]{0,1:T(8,128)(2,1)}, u32[]{:S(2)}, u32[]{:S(2)}) collective-permute-start(bf16[1024,256]{0,1:T(8,128)(2,1)S(1)} %pad_maximum_fusion.1), channel_id=1, source_target_pairs={{0,32},{32,0},{1,33},{33,1},{2,34},{34,2},{3,35},{35,3},{4,36},{36... | collective-permute-start | bytes 1572872 | tf_op jit(solution)/shard_map/ppermute | solution.py:132
  114.7 3.2 %copy-start = (f32[1024,2048]{1,0:T(8,128)}, f32[1024,2048]{1,0:T(8,128)S(1)}, u32[]{:S(2)}) copy-start(f32[1024,2048]{1,0:T(8,128)S(1)} %get-tuple-element.57) | copy-start | bytes 25165828
  114.7 3.2 %copy-start.9 = (bf16[1024,320]{0,1:T(8,128)(2,1)S(1)}, bf16[1024,320]{0,1:T(8,128)(2,1)}, u32[]{:S(2)}) copy-start(bf16[1024,320]{0,1:T(8,128)(2,1)} %copy.73) | copy-start | bytes 1966084
  127.1 18.6 %all-to-all-start.3 = ((bf16[32,32,320]{2,1,0:T(8,128)(2,1)}), bf16[32,32,320]{2,1,0:T(8,128)(2,1)S(1)}, u32[]{:S(2)}, u32[]{:S(2)}) async-start(bf16[32,32,320]{2,1,0:T(8,128)(2,1)} %copy.76), calls=%async_computation.3 | async-start | bytes 1572864 | tf_op jit(solution)/shard_map/all_to_all | solution.py:33
  145.7 23.7 %all-to-all-start.1 = ((bf16[16,4,4,320]{3,2,1,0:T(4,128)(2,1)}), bf16[16,4,4,320]{3,2,1,0:T(4,128)(2,1)S(1)}, u32[]{:S(2)}, u32[]{:S(2)}) async-start(bf16[16,4,4,320]{3,2,1,0:T(4,128)(2,1)} %copy.71), calls=%async_computation.1 | async-start | bytes 393216 | tf_op jit(solution)/shard_map/all_to_all | solution.py:33
  154.1 19.4 %collective-permute-start.7 = (bf16[64,320]{1,0:T(8,128)(2,1)S(1)}, bf16[64,320]{1,0:T(8,128)(2,1)S(1)}, u32[]{:S(2)}, u32[]{:S(2)}) collective-permute-start(bf16[64,320]{1,0:T(8,128)(2,1)S(1)} %convert_element_type.102), channel_id=1, source_target_pairs={{0,0},{1,32},{2,128},{3,160},{4,256},{5,288},{6,384},{7,416},{8,8}... | collective-permute-start | bytes 122888 | tf_op jit(solution)/shard_map/ppermute | solution.py:29

commit v2 on v1

v2 whole, which is shorter than its diff:
```python
import jax
import jax.numpy as jnp
from jax import lax
from jax.experimental import pallas as pl
from jax.experimental.pallas import tpu as pltpu
from jax.sharding import Mesh
from jax.sharding import PartitionSpec as P


SIZES = {"y": 4, "h": 2, "c": 2, "x": 4, "l": 8}
ROW = ("y", "h", "c")
COL = ("x", "l")
DEPTH = ("h", "l")
PLANE = ("x", "y", "c")
C = 320
BF = jnp.bfloat16
F32 = jnp.float32


def move(array, axes, target):
    sizes = [SIZES[axis] for axis in axes]
    pairs = []
    count = 1
    for size in sizes:
        count *= size
    for index in range(count):
        rest, place = index, []
        for size in reversed(sizes):
            place.insert(0, rest % size)
            rest //= size
        flat = 0
        for size, value in zip(sizes, target(*place)):
            flat = flat * size + value % size
        pairs.append((index, flat))
    return lax.ppermute(array, axes, pairs)


def exchange(array, axes):
    return lax.all_to_all(array, axes, split_axis=0, concat_axis=0, tiled=True)


def swap(array):
    return lax.ppermute(array, "c", [(0, 1), (1, 0)])


def dot(left, right):
    return jnp.dot(left, right, preferred_element_type=F32)


def dot_t(left, right):
    return lax.dot_general(left, right, (((1,), (1,)), ((), ())), preferred_element_type=F32)


def conv_kernel(block, before, after, kernels, gains, feat_out, pool_out, held, act, taps):
    held[0:32] = before[...].reshape(32, C).astype(F32)
    held[32:544] = block[...].reshape(512, C).astype(F32)
    held[544:576] = after[...].reshape(32, C).astype(F32)
    held[576:608] = jnp.zeros((32, C), F32)
    act[576:608] = jnp.zeros((32, C), F32)
    for layer in range(2):
        rows = 576 - 32 * layer
        wide = held[0:rows]
        factor = lax.rsqrt(jnp.mean(wide * wide, axis=-1, keepdims=True) + 1e-06)
        scaled = wide * factor * gains[layer : layer + 1]
        act[0:rows] = scaled * jax.nn.sigmoid(scaled)
        for a in range(3):
            taps[0:rows, a * C : (a + 1) * C] = act[a : a + rows].astype(BF)
        out = rows - 32
        total = dot(taps[0:out], kernels[layer, 0])
        total = total + dot(taps[16 : 16 + out], kernels[layer, 1])
        total = total + dot(taps[32 : 32 + out], kernels[layer, 2])
        fresh = (held[17 : 17 + out] + total).astype(BF)
        if layer == 0:
            held[0:out] = fresh.astype(F32)
    place = lax.broadcasted_iota(jnp.int32, (256, 512), 1)
    index = lax.broadcasted_iota(jnp.int32, (256, 512), 0)
    source = (((index >> 4) & 7) * 4 + (index & 3)) * 16 + (index >> 7) * 8 + ((index >> 2) & 3)
    feat_out[...] = dot((place == source).astype(F32).astype(BF), fresh).astype(BF)
    place, index = place[0:64], index[0:64]
    same = ((place >> 5) == (index >> 3) * 2 + (index & 1)) & (
        ((place >> 1) & 7) == ((index >> 2) & 1) * 4 + ((index >> 1) & 1)
    )
    pooled = dot(jnp.where(same, 0.25, 0.0).astype(BF), fresh).astype(BF)
    for copy in range(16):
        pool_out[copy] = pooled


def conv_stack(block, before, after, kernels, gains):
    return pl.pallas_call(
        conv_kernel,
        out_shape=(
            jax.ShapeDtypeStruct((256, C), BF),
            jax.ShapeDtypeStruct((16, 64, C), BF),
        ),
        scratch_shapes=[
            pltpu.VMEM((608, C), F32),
            pltpu.VMEM((608, C), F32),
            pltpu.VMEM((576, 3 * C), BF),
        ],
        cost_estimate=pl.CostEstimate(
            flops=2 * 1056 * 9 * C * C, bytes_accessed=5_000_000, transcendentals=360_000
        ),
        compiler_params=pltpu.CompilerParams(vmem_limit_bytes=24 << 20),
        name="conv_stack",
    )(block, before, after, kernels, gains)


def norm(projected, gain):
    factor = lax.rsqrt(jnp.mean(projected * projected, axis=-1, keepdims=True) + 1e-06)
    return (projected * factor * gain).astype(BF)


def heads_kernel(tokens, near, far, query_out, pair_out):
    def both(start):
        return jnp.concatenate([near[start : start + 64], far[start : start + 64]], 0)

    matrix = jnp.concatenate([both(0), both(64), both(128)], 0)
    projected = dot_t(tokens[...], matrix)
    query_gain = near[256:257, 0:128].astype(F32) + far[257:258, 0:128].astype(F32)
    key_gain = near[258:259, 0:128].astype(F32) + far[259:260, 0:128].astype(F32)
    query_out[...] = norm(projected[:, 0:128], query_gain)
    pair_out[:, 0:128] = norm(projected[:, 128:256], key_gain)
    pair_out[:, 128:256] = projected[:, 256:384].astype(BF)


def heads(tokens, near, far):
    return pl.pallas_call(
        heads_kernel,
        out_shape=(
            jax.ShapeDtypeStruct((1024, 128), BF),
            jax.ShapeDtypeStruct((1024, 256), BF),
        ),
        cost_estimate=pl.CostEstimate(
            flops=2 * 1024 * 384 * C, bytes_accessed=2_000_000, transcendentals=2048
        ),
        compiler_params=pltpu.CompilerParams(vmem_limit_bytes=16 << 20),
        name="heads",
    )(tokens, near, far)


def attend_kernel(query, pair, pair_far, tokens, near, far, terms_out):
    head_out = jnp.concatenate([near[192:256], far[192:256]], 0)
    scale = 128 ** (-0.5)

    def one_block(step, _):
        rows = pl.ds(pl.multiple_of(step * 256, 256), 256)
        asked = query[rows]
        scores_near = dot_t(asked, pair[:, 0:128])
        scores_far = dot_t(asked, pair_far[:, 0:128])
        top = jnp.maximum(
            jnp.max(scores_near, axis=1, keepdims=True), jnp.max(scores_far, axis=1, keepdims=True)
        )
        shifted_near = jnp.exp((scores_near - top) * scale)
        shifted_far = jnp.exp((scores_far - top) * scale)
        total = jnp.sum(shifted_near, axis=1, keepdims=True) + jnp.sum(
            shifted_far, axis=1, keepdims=True
        )
        attended = dot(shifted_near.astype(BF), pair[:, 128:256])
        attended = attended + dot(shifted_far.astype(BF), pair_far[:, 128:256])
        attended = (attended / total).astype(BF)
        terms = dot(attended, head_out) + tokens[rows].astype(F32) * 0.0625
        for column in range(8):
            parts = [
                terms[y * 64 + column * 8 : y * 64 + column * 8 + 8] for y in range(4)
            ]
            terms_out[step * 8 + column] = jnp.concatenate(parts, 0).astype(BF)
        return 0

    lax.fori_loop(0, 4, one_block, 0)


def attend(query, pair, pair_far, tokens, near, far):
    return pl.pallas_call(
        attend_kernel,
        out_shape=jax.ShapeDtypeStruct((32, 32, C), BF),
        cost_estimate=pl.CostEstimate(
            flops=2 * 1024 * 128 * (2 * 2048 + C),
            bytes_accessed=3_000_000,
            transcendentals=1024 * 2048,
        ),
        compiler_params=pltpu.CompilerParams(vmem_limit_bytes=24 << 20),
        name="attend",
    )(query, pair, pair_far, tokens, near, far)


def sum_kernel(terms, mixed_out):
    total = terms[0].astype(F32)
    for head in range(1, 16):
        total = total + terms[head].astype(F32)
    mixed_out[...] = total.astype(BF)


def sum_heads(terms):
    return pl.pallas_call(
        sum_kernel,
        out_shape=jax.ShapeDtypeStruct((64, C), BF),
        cost_estimate=pl.CostEstimate(
            flops=16 * 64 * C, bytes_accessed=700_000, transcendentals=0
        ),
        compiler_params=pltpu.CompilerParams(vmem_limit_bytes=8 << 20),
        name="sum_heads",
    )(terms)


def nearest_plane(y, h, c, l):
    depth = 8 * h + l + 2 * y - 4 + c
    return l // 2, depth // 8, c, depth % 8


def plan(latent, conv_weight, conv_gain, qkv_weight, qk_gain, out_weight):
    first = lax.axis_index("c") == 0
    kernels = conv_weight.transpose(0, 2, 1, 3, 4).reshape(2, 3, 3 * C, C)

    tiles = exchange(latent, DEPTH)

    gains = qk_gain.reshape(2, 1, 64)
    gains = jnp.concatenate([jnp.pad(gains, ((0, 0), (0, 0), (0, 64))), jnp.pad(gains, ((0, 0), (0, 0), (64, 0)))], 1)
    gains = jnp.pad(gains.reshape(4, 128), ((0, 12), (0, C - 128)))
    packed = jnp.concatenate([qkv_weight.reshape(192, C), out_weight, gains], 0)
    near = move(packed, ("y", "h", "c", "l"), nearest_plane)
    far = swap(near)
    near, far = jnp.where(first, near, far), jnp.where(first, far, near)

    own = tiles.reshape(2, 8, 4, 4, C).transpose(1, 3, 0, 2, 4).reshape(32, 8, C)
    sides = swap(jnp.where(first, own[:, 2:8], own[:, 0:6]))
    edge = move(
        jnp.where(first, own[:, 0:2], own[:, 6:8]), ("y", "c"), lambda y, c: (y - 1 + 2 * c, 1 - c)
    )
    block = jnp.where(
        first,
        jnp.concatenate([edge, own[:, 0:4], sides[:, 0:4], own[:, 4:8], sides[:, 4:6]], 1),
        jnp.concatenate([sides[:, 0:2], own[:, 0:4], sides[:, 2:6], own[:, 4:8], edge], 1),
    )
    before = move(block[30:32], ("x",), lambda x: (x + 1,))
    after = move(block[0:2], ("x",), lambda x: (x - 1,))

    feature_tiles, pooled = conv_stack(block, before, after, kernels, conv_gain)

    tokens = exchange(pooled, ("x", "y")).reshape(1024, C)
    features = exchange(feature_tiles.reshape(16, 4, 4, C), DEPTH)

    query, pair = heads(tokens, near, far)
    pair_far = swap(pair)
    terms = attend(query, pair, pair_far, tokens, near, far)
    terms = exchange(terms, PLANE)
    mixed = sum_heads(terms.reshape(16, 64, C))
    mixed = move(
        mixed,
        ("y", "h", "c", "x", "l"),
        lambda y, h, c, x, l: (2 * h + l // 4, (l // 2) % 2, l % 2, x, 2 * y + c),
    )
    mixed = mixed.reshape(2, 8, 2, 2, C).transpose(1, 0, 2, 3, 4)
    return (features, mixed.reshape(1, 32, 2, C))


def solution(mesh):
    planes = Mesh(mesh.devices.reshape(tuple(SIZES.values())), tuple(SIZES))
    placed = (
        P(None, ROW, COL, None),
        P(),
        P(),
        P(None, COL, None),
        P(None, COL),
        P(COL, None),
    )
    return jax.shard_map(
        plan,
        mesh=planes,
        in_specs=placed,
        out_specs=(P(None, ROW, COL, None), P(ROW, None, COL, None)),
        check_vma=False,
    )
```

time: 176 us -> 154 us (0.88)
  local copies, waits for them, and re-layouts: 35.3 us -> 7.61 us
  waiting for transfers between devices: 42.7 us -> 69.7 us
  matrix products: 17.1 us -> 0 us
  Pallas kernels: 0 us -> 12.7 us
  other arithmetic: 9.87 us -> 0.35 us
  starting transfers between devices: 67.8 us -> 62.3 us
    ppermute x6 -> x5, waiting for transfers between devices: 3.43 us -> 31.1 us  [move(): return lax.ppermute(array, axes, pairs)]
    reshape x22 -> x4, local copies, waits for them, and re-layouts: 22.5 us -> 0.94 us  [the longest x1 0.74 us: plan(): features = exchange(feature_tiles.reshape(16, 4, 4, C), DEPTH)]
    dot_general x23 -> x0, matrix products: 17.1 us -> none  [the longest x18 8.34 us: conv_layer(): jnp.dot(window, kernels[a, b], preferred_element_type=jnp.float32)]
    pallas_call x0 -> x4, Pallas kernels: none -> 12.7 us  [the longest x1 6.24 us: attend(): pl.pallas_call(attend_kernel, out_shape=jax.ShapeDtypeStruct((32, 32, C),...]
    ppermute x6 -> x5, starting transfers between devices: 25.9 us -> 20.4 us  [move(): return lax.ppermute(array, axes, pairs)]
    reduce_sum x5 -> x0, other arithmetic: 4.67 us -> none  [the longest x1 1.93 us: shards(): jnp.sum(shifted, axis=1, keepdims=True)]
    squeeze x1 -> x0, local copies, waits for them, and re-layouts: 4.11 us -> none  [shards(): hidden = conv_layer(hidden, conv_gain[1], conv_weight[1])]
    concatenate x3 -> x2, other arithmetic: 2.81 us -> 0.1 us  [the longest x1 0.07 us: plan(): jnp.concatenate([jnp.pad(gains, ((0, 0), (0, 0), (0, 64))), jnp.pad(gains...]
  transfers between devices with their start and end apart: 12 -> 12, of which waited for: 7 -> 8; matrix products, arithmetic and copies ran while one was open for 24% -> 2% of each run, Pallas kernels for 0% -> 0%
where the time goes in v2:
time: 154 us
  waiting for transfers between devices  69.7 us (45%)
  starting transfers between devices  62.3 us (40%)
  Pallas kernels  12.7 us (8%)
  local copies, waits for them, and re-layouts  7.61 us (5%)
    all_to_all x4, starting transfers between devices, exchange(): return lax.all_to_all(array, axes, split_axis=0, concat_axis=0, tiled=True)  36 us
    all_to_all x4, waiting for transfers between devices, exchange(): return lax.all_to_all(array, axes, split_axis=0, concat_axis=0, tiled=True)  35.4 us
    ppermute x5, waiting for transfers between devices, move(): return lax.ppermute(array, axes, pairs)  31.1 us
    ppermute x5, starting transfers between devices, move(): return lax.ppermute(array, axes, pairs)  20.4 us
    pallas_call x1, Pallas kernels, attend(): pl.pallas_call(attend_kernel, out_shape=jax.ShapeDtypeStruct((32, 32, C),...  6.24 us
    ppermute x3, starting transfers between devices, swap(): return lax.ppermute(array, 'c', [(0, 1), (1, 0)])  5.87 us
    pallas_call x1, Pallas kernels, conv_stack(): pl.pallas_call(conv_kernel, out_shape=(jax.ShapeDtypeStruct((256, C), BF)...  5.6 us
    ppermute x3, waiting for transfers between devices, swap(): return lax.ppermute(array, 'c', [(0, 1), (1, 0)])  3.18 us
  transfers between devices with their start and end apart: 12, of which 8 were waited for; matrix products, arithmetic and copies ran while one was open for 2% of the time, Pallas kernels for 0%

profile of v2, /device:TPU:16, one launch (start us, length us, event | category | flops | bytes accessed | tf_op | source)
XLA Modules:
  0.0 153.5 jit_solution(520182277041139469)
XLA Ops:
  0.6 0.0 copy-start.3
  0.6 15.2 %all-to-all-start = ((bf16[16,4,4,320]{3,2,1,0:T(4,128)(2,1)}), bf16[16,4,4,320]{3,2,1,0:T(4,128)(2,1)S(1)}, u32[]{:S(2)}, u32[]{:S(2)}) async-start(bf16[16,4,4,320]{3,2,1,0:T(4,128)(2,1)} %param.6), calls=%async_computation | async-start | bytes 393216 | tf_op jit(solution)/shard_map/all_to_all | solution.py:39
  15.9 16.4 %all-to-all-done = bf16[16,4,4,320]{3,2,1,0:T(4,128)(2,1)S(1)} async-done(((bf16[16,4,4,320]{3,2,1,0:T(4,128)(2,1)}), bf16[16,4,4,320]{3,2,1,0:T(4,128)(2,1)S(1)}, u32[]{:S(2)}, u32[]{:S(2)}) %all-to-all-start) | async-done | bytes 163872 | tf_op jit(solution)/shard_map/all_to_all | solution.py:39
  32.2 0.1 copy.17
  32.3 0.1 reshape.38
  32.4 0.1 slice_select_fusion
  32.5 0.1 broadcast_select_fusion.3
  32.6 1.9 %collective-permute-start.1 = (bf16[32,6,320]{2,1,0:T(8,128)(2,1)S(1)}, bf16[32,6,320]{2,1,0:T(8,128)(2,1)S(1)}, u32[]{:S(2)}, u32[]{:S(2)}) collective-permute-start(bf16[32,6,320]{2,1,0:T(8,128)(2,1)S(1)} %slice_select_fusion), channel_id=1, source_target_pairs={{0,32},{32,0},{1,33},{33,1},{2,34},{34,2},{3,35},{35,3},{4,36},{36... | collective-permute-start | bytes 368648 | tf_op jit(solution)/shard_map/ppermute | solution.py:43
  34.5 2.5 %collective-permute-start = (bf16[32,2,320]{2,1,0:T(2,128)(2,1)S(1)}, bf16[32,2,320]{2,1,0:T(2,128)(2,1)S(1)}, u32[]{:S(2)}, u32[]{:S(2)}) collective-permute-start(bf16[32,2,320]{2,1,0:T(2,128)(2,1)S(1)} %broadcast_select_fusion.3), channel_id=1, source_target_pairs={{0,416},{32,128},{128,32},{160,256},{256,160},{288,384},{384,288},... | collective-permute-start | bytes 122888 | tf_op jit(solution)/shard_map/ppermute | solution.py:35
  37.0 0.1 fusion.6
  37.0 0.0 collective-permute-done.1
  37.1 0.1 fusion.4
  37.1 0.1 fusion.5
  37.2 2.7 %collective-permute-done = bf16[32,2,320]{2,1,0:T(2,128)(2,1)S(1)} collective-permute-done((bf16[32,2,320]{2,1,0:T(2,128)(2,1)S(1)}, bf16[32,2,320]{2,1,0:T(2,128)(2,1)S(1)}, u32[]{:S(2)}, u32[]{:S(2)}) %collective-permute-start) | collective-permute-done | bytes 40992 | tf_op jit(solution)/shard_map/ppermute | solution.py:35
  39.9 1.2 concatenate.13
  41.1 1.2 concatenate.12
  42.3 0.1 broadcast_select_fusion.block
  42.4 3.4 %collective-permute-start.2 = (bf16[2,16,320]{2,1,0:T(8,128)(2,1)S(1)}, bf16[2,16,320]{2,1,0:T(8,128)(2,1)S(1)}, u32[]{:S(2)}, u32[]{:S(2)}) collective-permute-start(bf16[2,16,320]{2,1,0:T(8,128)(2,1)S(1)} %get-tuple-element.13), channel_id=1, source_target_pairs={{0,8},{8,16},{16,24},{24,0},{1,9},{9,17},{17,25},{25,1},{2,10},{10... | collective-permute-start | bytes 61448 | tf_op jit(solution)/shard_map/ppermute | solution.py:35
  45.8 3.7 %collective-permute-start.3 = (bf16[2,16,320]{2,1,0:T(8,128)(2,1)S(1)}, bf16[2,16,320]{2,1,0:T(8,128)(2,1)S(1)}, u32[]{:S(2)}, u32[]{:S(2)}) collective-permute-start(bf16[2,16,320]{2,1,0:T(8,128)(2,1)S(1)} %get-tuple-element.12), channel_id=1, source_target_pairs={{0,24},{8,0},{16,8},{24,16},{1,25},{9,1},{17,9},{25,17},{2,26},{10... | collective-permute-start | bytes 61448 | tf_op jit(solution)/shard_map/ppermute | solution.py:35
  49.5 0.0 copy-done.3
  49.5 0.1 fusion.2
  49.5 0.0 copy-start
  49.5 2.7 %copy.13 = bf16[2,3,3,320,320]{4,3,2,1,0:T(8,128)(2,1)S(1)} copy(bf16[2,3,3,320,320]{4,3,1,2,0:T(8,128)(2,1)} %bitcast.17) | data formatting | bytes 7372800 | tf_op jit(solution)/shard_map/transpose | solution.py:212
  52.3 0.0 copy-start.1
  52.3 0.0 copy-start.2
  52.3 0.0 collective-permute-done.2.before
  52.3 0.0 collective-permute-done.3.after
  52.3 0.0 copy-done
  52.3 5.6 %conv_stack.1 = (bf16[256,320]{1,0:T(8,128)(2,1)S(1)}, bf16[16,64,320]{2,1,0:T(8,128)(2,1)}) custom-call(bf16[32,16,320]{2,1,0:T(8,128)(2,1)S(1)} %broadcast_select_fusion.block, bf16[2,16,320]{2,1,0:T(8,128)(2,1)S(1)} %collective-permute-done.2.before, bf16[2,16,320]{2,1,0:T(8,128)(2,1)S(1)} %collective-permute-done.3.after, ...), custom_call_target="tpu_custom_call" | custom-call | flops 1946419200 | bytes 5000000 | tf_op jit(solution)/shard_map/conv_stack/pallas_call | solution.py:89
  57.9 6.4 %all-to-all-start.2 = ((bf16[16,64,320]{2,1,0:T(8,128)(2,1)}), bf16[16,64,320]{2,1,0:T(8,128)(2,1)S(1)}, u32[]{:S(2)}, u32[]{:S(2)}) async-start(bf16[16,64,320]{2,1,0:T(8,128)(2,1)} %get-tuple-element.7), calls=%async_computation.2 | async-start | bytes 1572864 | tf_op jit(solution)/shard_map/all_to_all | solution.py:39
  64.3 0.0 copy-done.1
  64.3 0.0 copy-done.2
  64.4 2.0 %collective-permute-start.4 = (bf16[272,320]{1,0:T(8,128)(2,1)S(1)}, bf16[272,320]{1,0:T(8,128)(2,1)S(1)}, u32[]{:S(2)}, u32[]{:S(2)}) collective-permute-start(bf16[272,320]{1,0:T(8,128)(2,1)S(1)} %fusion.1), channel_id=1, source_target_pairs={{0,68},{1,69},{2,198},{3,199},{4,256},{5,257},{6,386},{7,387},{32,... | collective-permute-start | bytes 522248 | tf_op jit(solution)/shard_map/ppermute | solution.py:35
  66.4 21.9 %collective-permute-done.4 = bf16[272,320]{1,0:T(8,128)(2,1)S(1)} collective-permute-done((bf16[272,320]{1,0:T(8,128)(2,1)S(1)}, bf16[272,320]{1,0:T(8,128)(2,1)S(1)}, u32[]{:S(2)}, u32[]{:S(2)}) %collective-permute-start.4) | collective-permute-done | bytes 174112 | tf_op jit(solution)/shard_map/ppermute | solution.py:35
  88.3 1.9 %collective-permute-start.5 = (bf16[272,320]{1,0:T(8,128)(2,1)S(1)}, bf16[272,320]{1,0:T(8,128)(2,1)S(1)}, u32[]{:S(2)}, u32[]{:S(2)}) collective-permute-start(bf16[272,320]{1,0:T(8,128)(2,1)S(1)} %collective-permute-done.4), channel_id=1, source_target_pairs={{0,32},{32,0},{1,33},{33,1},{2,34},{34,2},{3,35},{35,3},{4,36},{36... | collective-permute-start | bytes 522248 | tf_op jit(solution)/shard_map/ppermute | solution.py:43
  90.2 1.4 collective-permute-done.5
  91.7 0.0 all-to-all-done.2
  91.7 0.8 heads.1
  92.4 2.0 %collective-permute-start.6 = (bf16[1024,256]{1,0:T(8,128)(2,1)S(1)}, bf16[1024,256]{1,0:T(8,128)(2,1)S(1)}, u32[]{:S(2)}, u32[]{:S(2)}) collective-permute-start(bf16[1024,256]{1,0:T(8,128)(2,1)S(1)} %get-tuple-element.9.pair), channel_id=1, source_target_pairs={{0,32},{32,0},{1,33},{33,1},{2,34},{34,2},{3,35},{35,3},{4,36},{36... | collective-permute-start | bytes 1572872 | tf_op jit(solution)/shard_map/ppermute | solution.py:43
  94.5 1.8 %collective-permute-done.6.pair_far = bf16[1024,256]{1,0:T(8,128)(2,1)S(1)} collective-permute-done((bf16[1024,256]{1,0:T(8,128)(2,1)S(1)}, bf16[1024,256]{1,0:T(8,128)(2,1)S(1)}, u32[]{:S(2)}, u32[]{:S(2)}) %collective-permute-start.6) | collective-permute-done | bytes 524320 | tf_op jit(solution)/shard_map/ppermute | solution.py:43
  96.2 6.2 %attend.1 = bf16[32,32,320]{2,1,0:T(8,128)(2,1)} custom-call(bf16[1024,128]{1,0:T(8,128)(2,1)S(1)} %get-tuple-element.8.query, bf16[1024,256]{1,0:T(8,128)(2,1)S(1)} %get-tuple-element.9.pair, bf16[1024,256]{1,0:T(8,128)(2,1)S(1)} %collective-permute-done.6.pair_far, bf16[1024,320]{1,0:T(8,128)(2,1)S(1)} %bitcast.15, ...), custom_call_target="tpu_custom_call" | custom-call | flops 1157627904 | bytes 3000000 | tf_op jit(solution)/shard_map/attend/pallas_call | solution.py:173
  102.5 8.0 %all-to-all-start.3 = ((bf16[32,32,320]{2,1,0:T(8,128)(2,1)}), bf16[32,32,320]{2,1,0:T(8,128)(2,1)S(1)}, u32[]{:S(2)}, u32[]{:S(2)}) async-start(bf16[32,32,320]{2,1,0:T(8,128)(2,1)} %attend.1), calls=%async_computation.3 | async-start | bytes 1572864 | tf_op jit(solution)/shard_map/all_to_all | solution.py:39
  110.5 0.7 reshape.40
  111.2 11.7 %all-to-all-done.3 = bf16[32,32,320]{2,1,0:T(8,128)(2,1)S(1)} async-done(((bf16[32,32,320]{2,1,0:T(8,128)(2,1)}), bf16[32,32,320]{2,1,0:T(8,128)(2,1)S(1)}, u32[]{:S(2)}, u32[]{:S(2)}) %all-to-all-start.3) | async-done | bytes 655392 | tf_op jit(solution)/shard_map/all_to_all | solution.py:39
  123.0 6.4 %all-to-all-start.1 = ((bf16[16,4,4,320]{3,2,1,0:T(4,128)(2,1)}), bf16[16,4,4,320]{3,2,1,0:T(4,128)(2,1)S(1)}, u32[]{:S(2)}, u32[]{:S(2)}) async-start(bf16[16,4,4,320]{3,2,1,0:T(4,128)(2,1)} %reshape.40), calls=%async_computation.1 | async-start | bytes 393216 | tf_op jit(solution)/shard_map/all_to_all | solution.py:39
  129.4 0.1 sum_heads.1
  129.5 8.8 %collective-permute-start.7 = (bf16[64,320]{1,0:T(8,128)(2,1)S(1)}, bf16[64,320]{1,0:T(8,128)(2,1)S(1)}, u32[]{:S(2)}, u32[]{:S(2)}) collective-permute-start(bf16[64,320]{1,0:T(8,128)(2,1)S(1)} %sum_heads.1), channel_id=1, source_target_pairs={{0,0},{1,32},{2,64},{3,96},{4,128},{5,160},{6,192},{7,224},{8,8},{... | collective-permute-start | bytes 122888 | tf_op jit(solution)/shard_map/ppermute | solution.py:35
  138.3 7.3 %all-to-all-done.1 = bf16[16,4,4,320]{3,2,1,0:T(4,128)(2,1)S(1)} async-done(((bf16[16,4,4,320]{3,2,1,0:T(4,128)(2,1)}), bf16[16,4,4,320]{3,2,1,0:T(4,128)(2,1)S(1)}, u32[]{:S(2)}, u32[]{:S(2)}) %all-to-all-start.1) | async-done | bytes 163872 | tf_op jit(solution)/shard_map/all_to_all | solution.py:39
  145.7 6.5 %collective-permute-done.7 = bf16[64,320]{1,0:T(8,128)(2,1)S(1)} collective-permute-done((bf16[64,320]{1,0:T(8,128)(2,1)S(1)}, bf16[64,320]{1,0:T(8,128)(2,1)S(1)}, u32[]{:S(2)}, u32[]{:S(2)}) %collective-permute-start.7) | collective-permute-done | bytes 40992 | tf_op jit(solution)/shard_map/ppermute | solution.py:35
  152.2 0.7 copy.15
  152.8 0.7 copy.19
  (5 shorter events, 0.1 us)
Async XLA Ops:
  0.6 48.8 %copy-start.3 = (bf16[2,64]{1,0:T(2,128)(2,1)S(1)}, bf16[2,64]{1,0:T(2,128)(2,1)}, u32[]{:S(2)}) copy-start(bf16[2,64]{1,0:T(2,128)(2,1)} %param.10) | copy-start | bytes 772
  0.6 31.6 %all-to-all-start = ((bf16[16,4,4,320]{3,2,1,0:T(4,128)(2,1)}), bf16[16,4,4,320]{3,2,1,0:T(4,128)(2,1)S(1)}, u32[]{:S(2)}, u32[]{:S(2)}) async-start(bf16[16,4,4,320]{3,2,1,0:T(4,128)(2,1)} %param.6), calls=%async_computation | async-start | bytes 393216 | tf_op jit(solution)/shard_map/all_to_all | solution.py:39
  32.6 4.5 %collective-permute-start.1 = (bf16[32,6,320]{2,1,0:T(8,128)(2,1)S(1)}, bf16[32,6,320]{2,1,0:T(8,128)(2,1)S(1)}, u32[]{:S(2)}, u32[]{:S(2)}) collective-permute-start(bf16[32,6,320]{2,1,0:T(8,128)(2,1)S(1)} %slice_select_fusion), channel_id=1, source_target_pairs={{0,32},{32,0},{1,33},{33,1},{2,34},{34,2},{3,35},{35,3},{4,36},{36... | collective-permute-start | bytes 368648 | tf_op jit(solution)/shard_map/ppermute | solution.py:43
  34.5 5.4 %collective-permute-start = (bf16[32,2,320]{2,1,0:T(2,128)(2,1)S(1)}, bf16[32,2,320]{2,1,0:T(2,128)(2,1)S(1)}, u32[]{:S(2)}, u32[]{:S(2)}) collective-permute-start(bf16[32,2,320]{2,1,0:T(2,128)(2,1)S(1)} %broadcast_select_fusion.3), channel_id=1, source_target_pairs={{0,416},{32,128},{128,32},{160,256},{256,160},{288,384},{384,288},... | collective-permute-start | bytes 122888 | tf_op jit(solution)/shard_map/ppermute | solution.py:35
  42.4 9.9 %collective-permute-start.2 = (bf16[2,16,320]{2,1,0:T(8,128)(2,1)S(1)}, bf16[2,16,320]{2,1,0:T(8,128)(2,1)S(1)}, u32[]{:S(2)}, u32[]{:S(2)}) collective-permute-start(bf16[2,16,320]{2,1,0:T(8,128)(2,1)S(1)} %get-tuple-element.13), channel_id=1, source_target_pairs={{0,8},{8,16},{16,24},{24,0},{1,9},{9,17},{17,25},{25,1},{2,10},{10... | collective-permute-start | bytes 61448 | tf_op jit(solution)/shard_map/ppermute | solution.py:35
  45.8 6.5 %collective-permute-start.3 = (bf16[2,16,320]{2,1,0:T(8,128)(2,1)S(1)}, bf16[2,16,320]{2,1,0:T(8,128)(2,1)S(1)}, u32[]{:S(2)}, u32[]{:S(2)}) collective-permute-start(bf16[2,16,320]{2,1,0:T(8,128)(2,1)S(1)} %get-tuple-element.12), channel_id=1, source_target_pairs={{0,24},{8,0},{16,8},{24,16},{1,25},{9,1},{17,9},{25,17},{2,26},{10... | collective-permute-start | bytes 61448 | tf_op jit(solution)/shard_map/ppermute | solution.py:35
  49.5 2.8 %copy-start = (f32[2,320]{1,0:T(2,128)S(1)}, f32[2,320]{1,0:T(2,128)}, u32[]{:S(2)}) copy-start(f32[2,320]{1,0:T(2,128)} %gains.1) | copy-start | bytes 7684
  52.3 12.1 %copy-start.1 = (bf16[3,64,320]{2,1,0:T(8,128)(2,1)S(1)}, bf16[3,64,320]{2,1,0:T(8,128)(2,1)}, u32[]{:S(2)}) copy-start(bf16[3,64,320]{2,1,0:T(8,128)(2,1)} %param.9) | copy-start | bytes 368644
  52.3 12.1 %copy-start.2 = (bf16[64,320]{1,0:T(8,128)(2,1)S(1)}, bf16[64,320]{1,0:T(8,128)(2,1)}, u32[]{:S(2)}) copy-start(bf16[64,320]{1,0:T(8,128)(2,1)} %param.11) | copy-start | bytes 122884
  57.9 33.7 %all-to-all-start.2 = ((bf16[16,64,320]{2,1,0:T(8,128)(2,1)}), bf16[16,64,320]{2,1,0:T(8,128)(2,1)S(1)}, u32[]{:S(2)}, u32[]{:S(2)}) async-start(bf16[16,64,320]{2,1,0:T(8,128)(2,1)} %get-tuple-element.7), calls=%async_computation.2 | async-start | bytes 1572864 | tf_op jit(solution)/shard_map/all_to_all | solution.py:39
  64.4 23.9 %collective-permute-start.4 = (bf16[272,320]{1,0:T(8,128)(2,1)S(1)}, bf16[272,320]{1,0:T(8,128)(2,1)S(1)}, u32[]{:S(2)}, u32[]{:S(2)}) collective-permute-start(bf16[272,320]{1,0:T(8,128)(2,1)S(1)} %fusion.1), channel_id=1, source_target_pairs={{0,68},{1,69},{2,198},{3,199},{4,256},{5,257},{6,386},{7,387},{32,... | collective-permute-start | bytes 522248 | tf_op jit(solution)/shard_map/ppermute | solution.py:35
  88.3 3.3 %collective-permute-start.5 = (bf16[272,320]{1,0:T(8,128)(2,1)S(1)}, bf16[272,320]{1,0:T(8,128)(2,1)S(1)}, u32[]{:S(2)}, u32[]{:S(2)}) collective-permute-start(bf16[272,320]{1,0:T(8,128)(2,1)S(1)} %collective-permute-done.4), channel_id=1, source_target_pairs={{0,32},{32,0},{1,33},{33,1},{2,34},{34,2},{3,35},{35,3},{4,36},{36... | collective-permute-start | bytes 522248 | tf_op jit(solution)/shard_map/ppermute | solution.py:43
  92.4 3.8 %collective-permute-start.6 = (bf16[1024,256]{1,0:T(8,128)(2,1)S(1)}, bf16[1024,256]{1,0:T(8,128)(2,1)S(1)}, u32[]{:S(2)}, u32[]{:S(2)}) collective-permute-start(bf16[1024,256]{1,0:T(8,128)(2,1)S(1)} %get-tuple-element.9.pair), channel_id=1, source_target_pairs={{0,32},{32,0},{1,33},{33,1},{2,34},{34,2},{3,35},{35,3},{4,36},{36... | collective-permute-start | bytes 1572872 | tf_op jit(solution)/shard_map/ppermute | solution.py:43
  102.5 20.5 %all-to-all-start.3 = ((bf16[32,32,320]{2,1,0:T(8,128)(2,1)}), bf16[32,32,320]{2,1,0:T(8,128)(2,1)S(1)}, u32[]{:S(2)}, u32[]{:S(2)}) async-start(bf16[32,32,320]{2,1,0:T(8,128)(2,1)} %attend.1), calls=%async_computation.3 | async-start | bytes 1572864 | tf_op jit(solution)/shard_map/all_to_all | solution.py:39
  123.0 22.7 %all-to-all-start.1 = ((bf16[16,4,4,320]{3,2,1,0:T(4,128)(2,1)}), bf16[16,4,4,320]{3,2,1,0:T(4,128)(2,1)S(1)}, u32[]{:S(2)}, u32[]{:S(2)}) async-start(bf16[16,4,4,320]{3,2,1,0:T(4,128)(2,1)} %reshape.40), calls=%async_computation.1 | async-start | bytes 393216 | tf_op jit(solution)/shard_map/all_to_all | solution.py:39
  129.5 22.6 %collective-permute-start.7 = (bf16[64,320]{1,0:T(8,128)(2,1)S(1)}, bf16[64,320]{1,0:T(8,128)(2,1)S(1)}, u32[]{:S(2)}, u32[]{:S(2)}) collective-permute-start(bf16[64,320]{1,0:T(8,128)(2,1)S(1)} %sum_heads.1), channel_id=1, source_target_pairs={{0,0},{1,32},{2,64},{3,96},{4,128},{5,160},{6,192},{7,224},{8,8},{... | collective-permute-start | bytes 122888 | tf_op jit(solution)/shard_map/ppermute | solution.py:35

commit v3 on v2

--- a/solution.py
+++ b/solution.py
@@ -51,10 +51,49 @@
     return lax.dot_general(left, right, (((1,), (1,)), ((), ())), preferred_element_type=F32)
 
 
-def conv_kernel(block, before, after, kernels, gains, feat_out, pool_out, held, act, taps):
-    held[0:32] = before[...].reshape(32, C).astype(F32)
-    held[32:544] = block[...].reshape(512, C).astype(F32)
-    held[544:576] = after[...].reshape(32, C).astype(F32)
+def picked(core, first, count, own, other, edge):
+    place = lax.broadcasted_iota(jnp.int32, (count * 16, 1), 0)
+    column = first + (place >> 4)
+    row = ((place >> 3) & 1) * 8 + (place & 7) + core * 4 - 2
+    local = column * 8 + ((row >> 3) & 1) * 4 + (row & 3)
+    near = jnp.where(((row >> 2) & 1) == core, local, local + 256)
+    source = jnp.where((row < 0) | (row > 15), 512 + column * 2 + (row & 1), near)
+    at = lax.broadcasted_iota(jnp.int32, (count * 16, 576), 1)
+    choice = (at == source).astype(F32).astype(BF)
+    rows = dot(choice[:, 0:256], own[...].reshape(256, C))
+    rows = rows + dot(choice[:, 256:512], other[...].reshape(256, C))
+    return rows + dot(choice[:, 512:576], edge[...])
+
+
+def border_kernel(core, own, other, edge, left_out, right_out):
+    left_out[...] = picked(core[0], 0, 2, own, other, edge).astype(BF)
+    right_out[...] = picked(core[0], 30, 2, own, other, edge).astype(BF)
+
+
+def border(core, own, other, edge):
+    return pl.pallas_call(
+        border_kernel,
+        out_shape=(jax.ShapeDtypeStruct((32, C), BF),) * 2,
+        in_specs=[pl.BlockSpec(memory_space=pltpu.SMEM)] + [pl.BlockSpec(memory_space=pltpu.VMEM)] * 3,
+        compiler_params=pltpu.CompilerParams(vmem_limit_bytes=8 << 20),
+        cost_estimate=pl.CostEstimate(
+            flops=2 * 64 * 576 * C, bytes_accessed=400_000, transcendentals=0
+        ),
+        name="border",
+    )(core, own, other, edge)
+
+
+def conv_kernel(
+    core, own, other, edge, before, after, gains, stored, feat_out, pool_out, held, act, taps, kernels, arrived
+):
+    fetches = [
+        pltpu.make_async_copy(stored.at[layer], kernels.at[layer], arrived.at[layer]) for layer in range(2)
+    ]
+    for fetch in fetches:
+        fetch.start()
+    held[0:32] = before[...].astype(F32)
+    held[32:544] = picked(core[0], 0, 32, own, other, edge)
+    held[544:576] = after[...].astype(F32)
     held[576:608] = jnp.zeros((32, C), F32)
     act[576:608] = jnp.zeros((32, C), F32)
     for layer in range(2):
@@ -66,9 +105,10 @@
         for a in range(3):
             taps[0:rows, a * C : (a + 1) * C] = act[a : a + rows].astype(BF)
         out = rows - 32
-        total = dot(taps[0:out], kernels[layer, 0])
-        total = total + dot(taps[16 : 16 + out], kernels[layer, 1])
-        total = total + dot(taps[32 : 32 + out], kernels[layer, 2])
+        fetches[layer].wait()
+        total = dot(taps[0:out], kernels[layer, :, 0].reshape(3 * C, C))
+        total = total + dot(taps[16 : 16 + out], kernels[layer, :, 1].reshape(3 * C, C))
+        total = total + dot(taps[32 : 32 + out], kernels[layer, :, 2].reshape(3 * C, C))
         fresh = (held[17 : 17 + out] + total).astype(BF)
         if layer == 0:
             held[0:out] = fresh.astype(F32)
@@ -85,24 +125,29 @@
         pool_out[copy] = pooled
 
 
-def conv_stack(block, before, after, kernels, gains):
+def conv_stack(core, own, other, edge, before, after, kernels, gains):
     return pl.pallas_call(
         conv_kernel,
         out_shape=(
             jax.ShapeDtypeStruct((256, C), BF),
             jax.ShapeDtypeStruct((16, 64, C), BF),
         ),
+        in_specs=[pl.BlockSpec(memory_space=pltpu.SMEM)]
+        + [pl.BlockSpec(memory_space=pltpu.VMEM)] * 6
+        + [pl.BlockSpec(memory_space=pltpu.HBM)],
         scratch_shapes=[
             pltpu.VMEM((608, C), F32),
             pltpu.VMEM((608, C), F32),
             pltpu.VMEM((576, 3 * C), BF),
+            pltpu.VMEM((2, 3, 3, C, C), BF),
+            pltpu.SemaphoreType.DMA((2,)),
         ],
         cost_estimate=pl.CostEstimate(
             flops=2 * 1056 * 9 * C * C, bytes_accessed=5_000_000, transcendentals=360_000
         ),
-        compiler_params=pltpu.CompilerParams(vmem_limit_bytes=24 << 20),
+        compiler_params=pltpu.CompilerParams(vmem_limit_bytes=52 << 20),
         name="conv_stack",
-    )(block, before, after, kernels, gains)
+    )(core, own, other, edge, before, after, gains, kernels)
 
 
 def norm(projected, gain):
@@ -187,13 +232,17 @@
     total = terms[0].astype(F32)
     for head in range(1, 16):
         total = total + terms[head].astype(F32)
-    mixed_out[...] = total.astype(BF)
+    for half in range(2):
+        for strip in range(8):
+            part = total[half * 32 + strip * 4 : half * 32 + strip * 4 + 4].reshape(2, 2, C)
+            at = strip * 4 + half * 2
+            mixed_out[at : at + 2] = part.astype(BF)
 
 
 def sum_heads(terms):
     return pl.pallas_call(
         sum_kernel,
-        out_shape=jax.ShapeDtypeStruct((64, C), BF),
+        out_shape=jax.ShapeDtypeStruct((32, 2, C), BF),
         cost_estimate=pl.CostEstimate(
             flops=16 * 64 * C, bytes_accessed=700_000, transcendentals=0
         ),
@@ -202,15 +251,29 @@
     )(terms)
 
 
+def copy_kernel(source, target):
+    target[...] = source[...]
+
+
+def copied(array):
+    return pl.pallas_call(
+        copy_kernel,
+        out_shape=jax.ShapeDtypeStruct(array.shape, array.dtype),
+        compiler_params=pltpu.CompilerParams(vmem_limit_bytes=8 << 20),
+        cost_estimate=pl.CostEstimate(flops=0, bytes_accessed=400_000, transcendentals=0),
+        name="copied",
+    )(array)
+
+
 def nearest_plane(y, h, c, l):
     depth = 8 * h + l + 2 * y - 4 + c
     return l // 2, depth // 8, c, depth % 8
 
 
 def plan(latent, conv_weight, conv_gain, qkv_weight, qk_gain, out_weight):
-    first = lax.axis_index("c") == 0
-    kernels = conv_weight.transpose(0, 2, 1, 3, 4).reshape(2, 3, 3 * C, C)
-
+    core = lax.axis_index("c")
+    first = core == 0
+    core = core.astype(jnp.int32).reshape(1)
     tiles = exchange(latent, DEPTH)
 
     gains = qk_gain.reshape(2, 1, 64)
@@ -222,25 +285,23 @@
     near, far = jnp.where(first, near, far), jnp.where(first, far, near)
 
     own = tiles.reshape(2, 8, 4, 4, C).transpose(1, 3, 0, 2, 4).reshape(32, 8, C)
-    sides = swap(jnp.where(first, own[:, 2:8], own[:, 0:6]))
     edge = move(
         jnp.where(first, own[:, 0:2], own[:, 6:8]), ("y", "c"), lambda y, c: (y - 1 + 2 * c, 1 - c)
     )
-    block = jnp.where(
-        first,
-        jnp.concatenate([edge, own[:, 0:4], sides[:, 0:4], own[:, 4:8], sides[:, 4:6]], 1),
-        jnp.concatenate([sides[:, 0:2], own[:, 0:4], sides[:, 2:6], own[:, 4:8], edge], 1),
-    )
-    before = move(block[30:32], ("x",), lambda x: (x + 1,))
-    after = move(block[0:2], ("x",), lambda x: (x - 1,))
-
-    feature_tiles, pooled = conv_stack(block, before, after, kernels, conv_gain)
+    other = swap(own)
+    edge = edge.reshape(64, C)
+    left, right = border(core, own, other, edge)
+    before = move(right, ("x",), lambda x: (x + 1,))
+    after = move(left, ("x",), lambda x: (x - 1,))
+
+    feature_tiles, pooled = conv_stack(core, own, other, edge, before, after, conv_weight, conv_gain)
 
     tokens = exchange(pooled, ("x", "y")).reshape(1024, C)
     features = exchange(feature_tiles.reshape(16, 4, 4, C), DEPTH)
 
     query, pair = heads(tokens, near, far)
     pair_far = swap(pair)
+    features = copied(features)
     terms = attend(query, pair, pair_far, tokens, near, far)
     terms = exchange(terms, PLANE)
     mixed = sum_heads(terms.reshape(16, 64, C))
@@ -249,7 +310,6 @@
         ("y", "h", "c", "x", "l"),
         lambda y, h, c, x, l: (2 * h + l // 4, (l // 2) % 2, l % 2, x, 2 * y + c),
     )
-    mixed = mixed.reshape(2, 8, 2, 2, C).transpose(1, 0, 2, 3, 4)
     return (features, mixed.reshape(1, 32, 2, C))
 
 

time: 154 us -> 153 us (level)
  local copies, waits for them, and re-layouts: 7.61 us -> 2.27 us
  Pallas kernels: 12.7 us -> 15.5 us
    transpose x2 -> x0, local copies, waits for them, and re-layouts: 3.37 us -> none  [the longest x1 2.71 us: plan(): kernels = conv_weight.transpose(0, 2, 1, 3, 4).reshape(2, 3, 3 * C, C)]
    concatenate x2 -> x0, local copies, waits for them, and re-layouts: 2.38 us -> none  [the longest x1 1.2 us: plan(): jnp.concatenate([edge, own[:, 0:4], sides[:, 0:4], own[:, 4:8], sides[:,...]
    pallas_call x1, Pallas kernels: 5.6 us -> 7.42 us  [conv_stack(): pl.pallas_call(conv_kernel, out_shape=(jax.ShapeDtypeStruct((256, C), BF)...]
  transfers between devices with their start and end apart: 12 -> 12, of which waited for: 8 -> 9; matrix products, arithmetic and copies ran while one was open for 2% -> 1% of each run, Pallas kernels for 0% -> 1%
where the time goes in v3:
time: 153 us
  waiting for transfers between devices  69.6 us (45%)
  starting transfers between devices  63.3 us (41%)
  Pallas kernels  15.5 us (10%)
  local copies, waits for them, and re-layouts  2.27 us (1%)
    all_to_all x4, starting transfers between devices, exchange(): return lax.all_to_all(array, axes, split_axis=0, concat_axis=0, tiled=True)  37.1 us
    all_to_all x4, waiting for transfers between devices, exchange(): return lax.all_to_all(array, axes, split_axis=0, concat_axis=0, tiled=True)  35.4 us
    ppermute x5, waiting for transfers between devices, move(): return lax.ppermute(array, axes, pairs)  31.1 us
    ppermute x5, starting transfers between devices, move(): return lax.ppermute(array, axes, pairs)  20.4 us
    pallas_call x1, Pallas kernels, conv_stack(): pl.pallas_call(conv_kernel, out_shape=(jax.ShapeDtypeStruct((256, C), BF)...  7.42 us
    pallas_call x1, Pallas kernels, attend(): pl.pallas_call(attend_kernel, out_shape=jax.ShapeDtypeStruct((32, 32, C),...  6.24 us
    ppermute x3, starting transfers between devices, swap(): return lax.ppermute(array, 'c', [(0, 1), (1, 0)])  5.87 us
    ppermute x3, waiting for transfers between devices, swap(): return lax.ppermute(array, 'c', [(0, 1), (1, 0)])  3.18 us
  transfers between devices with their start and end apart: 12, of which 9 were waited for; matrix products, arithmetic and copies ran while one was open for 1% of the time, Pallas kernels for 1%

profile of v3, /device:TPU:16, one launch (start us, length us, event | category | flops | bytes accessed | tf_op | source)
XLA Modules:
  0.0 152.5 jit_solution(15266078445556681310)
XLA Ops:
  0.6 15.2 %all-to-all-start = ((bf16[16,4,4,320]{3,2,1,0:T(4,128)(2,1)}), bf16[16,4,4,320]{3,2,1,0:T(4,128)(2,1)S(1)}, u32[]{:S(2)}, u32[]{:S(2)}) async-start(bf16[16,4,4,320]{3,2,1,0:T(4,128)(2,1)} %param.6), calls=%async_computation | async-start | bytes 393216 | tf_op jit(solution)/shard_map/all_to_all | solution.py:39
  15.9 16.4 %all-to-all-done = bf16[16,4,4,320]{3,2,1,0:T(4,128)(2,1)S(1)} async-done(((bf16[16,4,4,320]{3,2,1,0:T(4,128)(2,1)}), bf16[16,4,4,320]{3,2,1,0:T(4,128)(2,1)S(1)}, u32[]{:S(2)}, u32[]{:S(2)}) %all-to-all-start) | async-done | bytes 163872 | tf_op jit(solution)/shard_map/all_to_all | solution.py:39
  32.2 0.1 copy.13
  32.3 0.1 reshape.39.own
  32.4 1.9 %collective-permute-start = (bf16[32,8,320]{2,1,0:T(8,128)(2,1)S(1)}, bf16[32,8,320]{2,1,0:T(8,128)(2,1)S(1)}, u32[]{:S(2)}, u32[]{:S(2)}) collective-permute-start(bf16[32,8,320]{2,1,0:T(8,128)(2,1)S(1)} %reshape.39.own), channel_id=1, source_target_pairs={{0,32},{32,0},{1,33},{33,1},{2,34},{34,2},{3,35},{35,3},{4,36},{36... | collective-permute-start | bytes 491528 | tf_op jit(solution)/shard_map/ppermute | solution.py:43
  34.3 0.1 broadcast_select_fusion.2
  34.4 2.5 %collective-permute-start.1 = (bf16[32,2,320]{2,1,0:T(2,128)(2,1)S(1)}, bf16[32,2,320]{2,1,0:T(2,128)(2,1)S(1)}, u32[]{:S(2)}, u32[]{:S(2)}) collective-permute-start(bf16[32,2,320]{2,1,0:T(2,128)(2,1)S(1)} %broadcast_select_fusion.2), channel_id=1, source_target_pairs={{0,416},{32,128},{128,32},{160,256},{256,160},{288,384},{384,288},... | collective-permute-start | bytes 122888 | tf_op jit(solution)/shard_map/ppermute | solution.py:35
  36.9 2.9 %collective-permute-done.1 = bf16[32,2,320]{2,1,0:T(2,128)(2,1)S(1)} collective-permute-done((bf16[32,2,320]{2,1,0:T(2,128)(2,1)S(1)}, bf16[32,2,320]{2,1,0:T(2,128)(2,1)S(1)}, u32[]{:S(2)}, u32[]{:S(2)}) %collective-permute-start.1) | collective-permute-done | bytes 40992 | tf_op jit(solution)/shard_map/ppermute | solution.py:35
  39.9 0.0 collective-permute-done.other
  39.9 0.0 copy-start.1
  39.9 0.0 copy-start.2
  39.9 0.2 border.1
  40.2 3.4 %collective-permute-start.2 = (bf16[32,320]{1,0:T(8,128)(2,1)S(1)}, bf16[32,320]{1,0:T(8,128)(2,1)S(1)}, u32[]{:S(2)}, u32[]{:S(2)}) collective-permute-start(bf16[32,320]{1,0:T(8,128)(2,1)S(1)} %get-tuple-element.8), channel_id=1, source_target_pairs={{0,8},{8,16},{16,24},{24,0},{1,9},{9,17},{17,25},{25,1},{2,10},{10... | collective-permute-start | bytes 61448 | tf_op jit(solution)/shard_map/ppermute | solution.py:35
  43.6 3.7 %collective-permute-start.3 = (bf16[32,320]{1,0:T(8,128)(2,1)S(1)}, bf16[32,320]{1,0:T(8,128)(2,1)S(1)}, u32[]{:S(2)}, u32[]{:S(2)}) collective-permute-start(bf16[32,320]{1,0:T(8,128)(2,1)S(1)} %get-tuple-element.9), channel_id=1, source_target_pairs={{0,24},{8,0},{16,8},{24,16},{1,25},{9,1},{17,9},{25,17},{2,26},{10... | collective-permute-start | bytes 61448 | tf_op jit(solution)/shard_map/ppermute | solution.py:35
  47.2 0.8 fusion.2
  48.0 0.0 collective-permute-done.2.before
  48.0 1.2 collective-permute-done.3.after
  49.3 0.0 copy-start
  49.3 0.7 copy-done
  50.0 7.4 %conv_stack.1 = (bf16[256,320]{1,0:T(8,128)(2,1)S(1)}, bf16[16,64,320]{2,1,0:T(8,128)(2,1)}) custom-call(s32[1]{0:T(128)} %bitcast.core, bf16[32,8,320]{2,1,0:T(8,128)(2,1)S(1)} %reshape.39.own, bf16[32,8,320]{2,1,0:T(8,128)(2,1)S(1)} %collective-permute-done.other, bf16[64,320]{1,0:T(8,128)(2,1)S(1)} %reshape.40.edge, ...), custom_call_target="tpu_custom_call" | custom-call | flops 1946419200 | bytes 5000000 | tf_op jit(solution)/shard_map/conv_stack/pallas_call | solution.py:129
  57.4 7.2 %all-to-all-start.2 = ((bf16[16,64,320]{2,1,0:T(8,128)(2,1)}), bf16[16,64,320]{2,1,0:T(8,128)(2,1)S(1)}, u32[]{:S(2)}, u32[]{:S(2)}) async-start(bf16[16,64,320]{2,1,0:T(8,128)(2,1)} %get-tuple-element.11), calls=%async_computation.2 | async-start | bytes 1572864 | tf_op jit(solution)/shard_map/all_to_all | solution.py:39
  64.6 0.0 copy-done.1
  64.6 0.0 copy-done.2
  64.7 2.0 %collective-permute-start.4 = (bf16[272,320]{1,0:T(8,128)(2,1)S(1)}, bf16[272,320]{1,0:T(8,128)(2,1)S(1)}, u32[]{:S(2)}, u32[]{:S(2)}) collective-permute-start(bf16[272,320]{1,0:T(8,128)(2,1)S(1)} %fusion.1), channel_id=1, source_target_pairs={{0,68},{1,69},{2,198},{3,199},{4,256},{5,257},{6,386},{7,387},{32,... | collective-permute-start | bytes 522248 | tf_op jit(solution)/shard_map/ppermute | solution.py:35
  66.7 21.1 %collective-permute-done.4 = bf16[272,320]{1,0:T(8,128)(2,1)S(1)} collective-permute-done((bf16[272,320]{1,0:T(8,128)(2,1)S(1)}, bf16[272,320]{1,0:T(8,128)(2,1)S(1)}, u32[]{:S(2)}, u32[]{:S(2)}) %collective-permute-start.4) | collective-permute-done | bytes 174112 | tf_op jit(solution)/shard_map/ppermute | solution.py:35
  87.8 1.9 %collective-permute-start.5 = (bf16[272,320]{1,0:T(8,128)(2,1)S(1)}, bf16[272,320]{1,0:T(8,128)(2,1)S(1)}, u32[]{:S(2)}, u32[]{:S(2)}) collective-permute-start(bf16[272,320]{1,0:T(8,128)(2,1)S(1)} %collective-permute-done.4), channel_id=1, source_target_pairs={{0,32},{32,0},{1,33},{33,1},{2,34},{34,2},{3,35},{35,3},{4,36},{36... | collective-permute-start | bytes 522248 | tf_op jit(solution)/shard_map/ppermute | solution.py:43
  89.7 1.4 collective-permute-done.5
  91.2 0.0 all-to-all-done.2
  91.2 0.8 heads.1
  91.9 2.0 %collective-permute-start.6 = (bf16[1024,256]{1,0:T(8,128)(2,1)S(1)}, bf16[1024,256]{1,0:T(8,128)(2,1)S(1)}, u32[]{:S(2)}, u32[]{:S(2)}) collective-permute-start(bf16[1024,256]{1,0:T(8,128)(2,1)S(1)} %get-tuple-element.13.pair), channel_id=1, source_target_pairs={{0,32},{32,0},{1,33},{33,1},{2,34},{34,2},{3,35},{35,3},{4,36},{36... | collective-permute-start | bytes 1572872 | tf_op jit(solution)/shard_map/ppermute | solution.py:43
  94.0 1.8 %collective-permute-done.6.pair_far = bf16[1024,256]{1,0:T(8,128)(2,1)S(1)} collective-permute-done((bf16[1024,256]{1,0:T(8,128)(2,1)S(1)}, bf16[1024,256]{1,0:T(8,128)(2,1)S(1)}, u32[]{:S(2)}, u32[]{:S(2)}) %collective-permute-start.6) | collective-permute-done | bytes 524320 | tf_op jit(solution)/shard_map/ppermute | solution.py:43
  95.7 6.2 %attend.1 = bf16[32,32,320]{2,1,0:T(8,128)(2,1)} custom-call(bf16[1024,128]{1,0:T(8,128)(2,1)S(1)} %get-tuple-element.12.query, bf16[1024,256]{1,0:T(8,128)(2,1)S(1)} %get-tuple-element.13.pair, bf16[1024,256]{1,0:T(8,128)(2,1)S(1)} %collective-permute-done.6.pair_far, bf16[1024,320]{1,0:T(8,128)(2,1)S(1)} %bitcast.12, ...), custom_call_target="tpu_custom_call" | custom-call | flops 1157627904 | bytes 3000000 | tf_op jit(solution)/shard_map/attend/pallas_call | solution.py:218
  102.0 7.9 %all-to-all-start.3 = ((bf16[32,32,320]{2,1,0:T(8,128)(2,1)}), bf16[32,32,320]{2,1,0:T(8,128)(2,1)S(1)}, u32[]{:S(2)}, u32[]{:S(2)}) async-start(bf16[32,32,320]{2,1,0:T(8,128)(2,1)} %attend.1), calls=%async_computation.3 | async-start | bytes 1572864 | tf_op jit(solution)/shard_map/all_to_all | solution.py:39
  109.9 0.7 reshape.41
  110.7 11.7 %all-to-all-done.3 = bf16[32,32,320]{2,1,0:T(8,128)(2,1)S(1)} async-done(((bf16[32,32,320]{2,1,0:T(8,128)(2,1)}), bf16[32,32,320]{2,1,0:T(8,128)(2,1)S(1)}, u32[]{:S(2)}, u32[]{:S(2)}) %all-to-all-start.3) | async-done | bytes 655392 | tf_op jit(solution)/shard_map/all_to_all | solution.py:39
  122.4 6.7 %all-to-all-start.1 = ((bf16[16,4,4,320]{3,2,1,0:T(4,128)(2,1)}), bf16[16,4,4,320]{3,2,1,0:T(4,128)(2,1)S(1)}, u32[]{:S(2)}, u32[]{:S(2)}) async-start(bf16[16,4,4,320]{3,2,1,0:T(4,128)(2,1)} %reshape.41), calls=%async_computation.1 | async-start | bytes 393216 | tf_op jit(solution)/shard_map/all_to_all | solution.py:39
  129.1 0.2 sum_heads.1
  129.3 8.8 %collective-permute-start.7 = (bf16[32,2,320]{2,1,0:T(2,128)(2,1)S(1)}, bf16[32,2,320]{2,1,0:T(2,128)(2,1)S(1)}, u32[]{:S(2)}, u32[]{:S(2)}) collective-permute-start(bf16[32,2,320]{2,1,0:T(2,128)(2,1)S(1)} %sum_heads.1), channel_id=1, source_target_pairs={{0,0},{1,32},{2,64},{3,96},{4,128},{5,160},{6,192},{7,224},{8,8},{... | collective-permute-start | bytes 122888 | tf_op jit(solution)/shard_map/ppermute | solution.py:35
  138.1 7.3 %all-to-all-done.1.source = bf16[16,4,4,320]{3,2,1,0:T(4,128)(2,1)S(1)} async-done(((bf16[16,4,4,320]{3,2,1,0:T(4,128)(2,1)}), bf16[16,4,4,320]{3,2,1,0:T(4,128)(2,1)S(1)}, u32[]{:S(2)}, u32[]{:S(2)}) %all-to-all-start.1) | async-done | bytes 163872 | tf_op jit(solution)/shard_map/all_to_all | solution.py:39
  145.4 0.7 copied.1
  146.1 5.8 %collective-permute-done.7 = bf16[32,2,320]{2,1,0:T(2,128)(2,1)S(1)} collective-permute-done((bf16[32,2,320]{2,1,0:T(2,128)(2,1)S(1)}, bf16[32,2,320]{2,1,0:T(2,128)(2,1)S(1)}, u32[]{:S(2)}, u32[]{:S(2)}) %collective-permute-start.7) | collective-permute-done | bytes 40992 | tf_op jit(solution)/shard_map/ppermute | solution.py:35
  151.9 0.6 copy.15
  (4 shorter events, 0.1 us)
Async XLA Ops:
  0.6 31.6 %all-to-all-start = ((bf16[16,4,4,320]{3,2,1,0:T(4,128)(2,1)}), bf16[16,4,4,320]{3,2,1,0:T(4,128)(2,1)S(1)}, u32[]{:S(2)}, u32[]{:S(2)}) async-start(bf16[16,4,4,320]{3,2,1,0:T(4,128)(2,1)} %param.6), calls=%async_computation | async-start | bytes 393216 | tf_op jit(solution)/shard_map/all_to_all | solution.py:39
  32.4 7.5 %collective-permute-start = (bf16[32,8,320]{2,1,0:T(8,128)(2,1)S(1)}, bf16[32,8,320]{2,1,0:T(8,128)(2,1)S(1)}, u32[]{:S(2)}, u32[]{:S(2)}) collective-permute-start(bf16[32,8,320]{2,1,0:T(8,128)(2,1)S(1)} %reshape.39.own), channel_id=1, source_target_pairs={{0,32},{32,0},{1,33},{33,1},{2,34},{34,2},{3,35},{35,3},{4,36},{36... | collective-permute-start | bytes 491528 | tf_op jit(solution)/shard_map/ppermute | solution.py:43
  34.4 5.4 %collective-permute-start.1 = (bf16[32,2,320]{2,1,0:T(2,128)(2,1)S(1)}, bf16[32,2,320]{2,1,0:T(2,128)(2,1)S(1)}, u32[]{:S(2)}, u32[]{:S(2)}) collective-permute-start(bf16[32,2,320]{2,1,0:T(2,128)(2,1)S(1)} %broadcast_select_fusion.2), channel_id=1, source_target_pairs={{0,416},{32,128},{128,32},{160,256},{256,160},{288,384},{384,288},... | collective-permute-start | bytes 122888 | tf_op jit(solution)/shard_map/ppermute | solution.py:35
  39.9 24.7 %copy-start.1 = (bf16[3,64,320]{2,1,0:T(8,128)(2,1)S(1)}, bf16[3,64,320]{2,1,0:T(8,128)(2,1)}, u32[]{:S(2)}) copy-start(bf16[3,64,320]{2,1,0:T(8,128)(2,1)} %param.9) | copy-start | bytes 368644
  39.9 24.7 %copy-start.2 = (bf16[64,320]{1,0:T(8,128)(2,1)S(1)}, bf16[64,320]{1,0:T(8,128)(2,1)}, u32[]{:S(2)}) copy-start(bf16[64,320]{1,0:T(8,128)(2,1)} %param.11) | copy-start | bytes 122884
  40.2 7.9 %collective-permute-start.2 = (bf16[32,320]{1,0:T(8,128)(2,1)S(1)}, bf16[32,320]{1,0:T(8,128)(2,1)S(1)}, u32[]{:S(2)}, u32[]{:S(2)}) collective-permute-start(bf16[32,320]{1,0:T(8,128)(2,1)S(1)} %get-tuple-element.8), channel_id=1, source_target_pairs={{0,8},{8,16},{16,24},{24,0},{1,9},{9,17},{17,25},{25,1},{2,10},{10... | collective-permute-start | bytes 61448 | tf_op jit(solution)/shard_map/ppermute | solution.py:35
  43.6 5.7 %collective-permute-start.3 = (bf16[32,320]{1,0:T(8,128)(2,1)S(1)}, bf16[32,320]{1,0:T(8,128)(2,1)S(1)}, u32[]{:S(2)}, u32[]{:S(2)}) collective-permute-start(bf16[32,320]{1,0:T(8,128)(2,1)S(1)} %get-tuple-element.9), channel_id=1, source_target_pairs={{0,24},{8,0},{16,8},{24,16},{1,25},{9,1},{17,9},{25,17},{2,26},{10... | collective-permute-start | bytes 61448 | tf_op jit(solution)/shard_map/ppermute | solution.py:35
  49.3 0.7 copy-start
  57.4 33.8 %all-to-all-start.2 = ((bf16[16,64,320]{2,1,0:T(8,128)(2,1)}), bf16[16,64,320]{2,1,0:T(8,128)(2,1)S(1)}, u32[]{:S(2)}, u32[]{:S(2)}) async-start(bf16[16,64,320]{2,1,0:T(8,128)(2,1)} %get-tuple-element.11), calls=%async_computation.2 | async-start | bytes 1572864 | tf_op jit(solution)/shard_map/all_to_all | solution.py:39
  64.7 23.1 %collective-permute-start.4 = (bf16[272,320]{1,0:T(8,128)(2,1)S(1)}, bf16[272,320]{1,0:T(8,128)(2,1)S(1)}, u32[]{:S(2)}, u32[]{:S(2)}) collective-permute-start(bf16[272,320]{1,0:T(8,128)(2,1)S(1)} %fusion.1), channel_id=1, source_target_pairs={{0,68},{1,69},{2,198},{3,199},{4,256},{5,257},{6,386},{7,387},{32,... | collective-permute-start | bytes 522248 | tf_op jit(solution)/shard_map/ppermute | solution.py:35
  87.8 3.3 %collective-permute-start.5 = (bf16[272,320]{1,0:T(8,128)(2,1)S(1)}, bf16[272,320]{1,0:T(8,128)(2,1)S(1)}, u32[]{:S(2)}, u32[]{:S(2)}) collective-permute-start(bf16[272,320]{1,0:T(8,128)(2,1)S(1)} %collective-permute-done.4), channel_id=1, source_target_pairs={{0,32},{32,0},{1,33},{33,1},{2,34},{34,2},{3,35},{35,3},{4,36},{36... | collective-permute-start | bytes 522248 | tf_op jit(solution)/shard_map/ppermute | solution.py:43
  91.9 3.8 %collective-permute-start.6 = (bf16[1024,256]{1,0:T(8,128)(2,1)S(1)}, bf16[1024,256]{1,0:T(8,128)(2,1)S(1)}, u32[]{:S(2)}, u32[]{:S(2)}) collective-permute-start(bf16[1024,256]{1,0:T(8,128)(2,1)S(1)} %get-tuple-element.13.pair), channel_id=1, source_target_pairs={{0,32},{32,0},{1,33},{33,1},{2,34},{34,2},{3,35},{35,3},{4,36},{36... | collective-permute-start | bytes 1572872 | tf_op jit(solution)/shard_map/ppermute | solution.py:43
  102.0 20.4 %all-to-all-start.3 = ((bf16[32,32,320]{2,1,0:T(8,128)(2,1)}), bf16[32,32,320]{2,1,0:T(8,128)(2,1)S(1)}, u32[]{:S(2)}, u32[]{:S(2)}) async-start(bf16[32,32,320]{2,1,0:T(8,128)(2,1)} %attend.1), calls=%async_computation.3 | async-start | bytes 1572864 | tf_op jit(solution)/shard_map/all_to_all | solution.py:39
  122.4 23.0 %all-to-all-start.1 = ((bf16[16,4,4,320]{3,2,1,0:T(4,128)(2,1)}), bf16[16,4,4,320]{3,2,1,0:T(4,128)(2,1)S(1)}, u32[]{:S(2)}, u32[]{:S(2)}) async-start(bf16[16,4,4,320]{3,2,1,0:T(4,128)(2,1)} %reshape.41), calls=%async_computation.1 | async-start | bytes 393216 | tf_op jit(solution)/shard_map/all_to_all | solution.py:39
  129.3 22.6 %collective-permute-start.7 = (bf16[32,2,320]{2,1,0:T(2,128)(2,1)S(1)}, bf16[32,2,320]{2,1,0:T(2,128)(2,1)S(1)}, u32[]{:S(2)}, u32[]{:S(2)}) collective-permute-start(bf16[32,2,320]{2,1,0:T(2,128)(2,1)S(1)} %sum_heads.1), channel_id=1, source_target_pairs={{0,0},{1,32},{2,64},{3,96},{4,128},{5,160},{6,192},{7,224},{8,8},{... | collective-permute-start | bytes 122888 | tf_op jit(solution)/shard_map/ppermute | solution.py:35

commit v4 on v3

--- a/solution.py
+++ b/solution.py
@@ -1,3 +1,5 @@
+import math
+
 import jax
 import jax.numpy as jnp
 from jax import lax
@@ -83,46 +85,90 @@
     )(core, own, other, edge)
 
 
+def packed_rows(array, shift):
+    pairs = array.reshape(array.shape[0] // 16, 2, 8, C)
+    sub = lax.broadcasted_iota(jnp.int32, pairs[:, 0].shape, 1)
+    upper = pltpu.roll(pairs[:, 0], (8 - shift) % 8, 1)
+    lower = pltpu.roll(pairs[:, 1], 4 - shift, 1)
+    return jnp.where(sub < 4, upper, lower).reshape(array.shape[0] // 2, C)
+
+
 def conv_kernel(
-    core, own, other, edge, before, after, gains, stored, feat_out, pool_out, held, act, taps, kernels, arrived
+    core,
+    own,
+    other,
+    edge,
+    before,
+    after,
+    stored_gains,
+    stored,
+    feat_out,
+    pool_out,
+    held,
+    act,
+    taps,
+    taps_odd,
+    gains,
+    kernels,
+    arrived,
+    pool,
+    sent,
 ):
-    fetches = [
-        pltpu.make_async_copy(stored.at[layer], kernels.at[layer], arrived.at[layer]) for layer in range(2)
-    ]
-    for fetch in fetches:
-        fetch.start()
+    gain_fetch = pltpu.make_async_copy(stored_gains, gains, arrived.at[6])
+    gain_fetch.start()
+    fetches = []
+    for layer in range(2):
+        for b in range(3):
+            fetch = pltpu.make_async_copy(
+                stored.at[layer, :, b], kernels.at[layer, b], arrived.at[3 * layer + b]
+            )
+            fetch.start()
+            fetches.append(fetch)
+
+    def activation(wide, layer):
+        factor = lax.rsqrt(jnp.mean(wide * wide, axis=-1, keepdims=True) + 1e-06)
+        scaled = wide * factor * gains[layer : layer + 1]
+        return scaled * jax.nn.sigmoid(scaled)
+
+    def tap(rows, layer, b):
+        fetches[3 * layer + b].wait()
+        return dot(rows, kernels[layer, b].reshape(3 * C, C))
+
     held[0:32] = before[...].astype(F32)
     held[32:544] = picked(core[0], 0, 32, own, other, edge)
     held[544:576] = after[...].astype(F32)
-    held[576:608] = jnp.zeros((32, C), F32)
-    act[576:608] = jnp.zeros((32, C), F32)
-    for layer in range(2):
-        rows = 576 - 32 * layer
-        wide = held[0:rows]
-        factor = lax.rsqrt(jnp.mean(wide * wide, axis=-1, keepdims=True) + 1e-06)
-        scaled = wide * factor * gains[layer : layer + 1]
-        act[0:rows] = scaled * jax.nn.sigmoid(scaled)
-        for a in range(3):
-            taps[0:rows, a * C : (a + 1) * C] = act[a : a + rows].astype(BF)
-        out = rows - 32
-        fetches[layer].wait()
-        total = dot(taps[0:out], kernels[layer, :, 0].reshape(3 * C, C))
-        total = total + dot(taps[16 : 16 + out], kernels[layer, :, 1].reshape(3 * C, C))
-        total = total + dot(taps[32 : 32 + out], kernels[layer, :, 2].reshape(3 * C, C))
-        fresh = (held[17 : 17 + out] + total).astype(BF)
-        if layer == 0:
-            held[0:out] = fresh.astype(F32)
-    place = lax.broadcasted_iota(jnp.int32, (256, 512), 1)
-    index = lax.broadcasted_iota(jnp.int32, (256, 512), 0)
-    source = (((index >> 4) & 7) * 4 + (index & 3)) * 16 + (index >> 7) * 8 + ((index >> 2) & 3)
+    gain_fetch.wait()
+    act[0:576] = activation(held[0:576], 0)
+    act[576:592] = jnp.zeros((16, C), F32)
+    for a in range(3):
+        taps[:, a * C : (a + 1) * C] = act[a : a + 576].astype(BF)
+    total = tap(taps[0:544], 0, 0) + tap(taps[16:560], 0, 1) + tap(taps[32:576], 0, 2)
+    held[576:592] = jnp.zeros((16, C), F32)
+    middle = (held[17:561] + total).astype(BF).astype(F32)
+    center = packed_rows(middle, 1)[8:264]
+    wide = activation(middle, 1)
+    for a in range(3):
+        rows = packed_rows(wide, a)
+        taps[0:272, a * C : (a + 1) * C] = rows.astype(BF)
+        taps_odd[:, a * C : (a + 1) * C] = rows[8:264].astype(BF)
+    total = tap(taps[0:256], 1, 0) + tap(taps_odd[...], 1, 1) + tap(taps[16:272], 1, 2)
+    fresh = (center + total).astype(BF)
+    place = lax.broadcasted_iota(jnp.int32, (64, 256), 1)
+    index = lax.broadcasted_iota(jnp.int32, (64, 256), 0)
+    same = ((place >> 4) == (index >> 3) * 2 + (index & 1)) & (
+        ((place >> 1) & 3) == ((index >> 2) & 1) * 2 + ((index >> 1) & 1)
+    )
+    pooled = dot(jnp.where(same, 0.25, 0.0).astype(BF), fresh).astype(BF)
+    pool[...] = pooled
+    copies = [pltpu.make_async_copy(pool, pool_out.at[slot], sent.at[slot]) for slot in range(16)]
+    for copy in copies:
+        copy.start()
+    place = lax.broadcasted_iota(jnp.int32, (256, 256), 1)
+    index = lax.broadcasted_iota(jnp.int32, (256, 256), 0)
+    source = (((index >> 4) & 7) * 4 + (index & 3)) * 8 + (index >> 7) * 4 + ((index >> 2) & 3)
     feat_out[...] = dot((place == source).astype(F32).astype(BF), fresh).astype(BF)
-    place, index = place[0:64], index[0:64]
-    same = ((place >> 5) == (index >> 3) * 2 + (index & 1)) & (
-        ((place >> 1) & 7) == ((index >> 2) & 1) * 4 + ((index >> 1) & 1)
-    )
-    pooled = dot(jnp.where(same, 0.25, 0.0).astype(BF), fresh).astype(BF)
-    for copy in range(16):
-        pool_out[copy] = pooled
+    for copy in copies:
+        copy.wait()
 
 
 def conv_stack(core, own, other, edge, before, after, kernels, gains):
@@ -132,15 +178,20 @@
             jax.ShapeDtypeStruct((256, C), BF),
             jax.ShapeDtypeStruct((16, 64, C), BF),
         ),
+        out_specs=(pl.BlockSpec(memory_space=pltpu.VMEM), pl.BlockSpec(memory_space=pltpu.HBM)),
         in_specs=[pl.BlockSpec(memory_space=pltpu.SMEM)]
-        + [pl.BlockSpec(memory_space=pltpu.VMEM)] * 6
-        + [pl.BlockSpec(memory_space=pltpu.HBM)],
+        + [pl.BlockSpec(memory_space=pltpu.VMEM)] * 5
+        + [pl.BlockSpec(memory_space=pltpu.HBM)] * 2,
         scratch_shapes=[
             pltpu.VMEM((608, C), F32),
             pltpu.VMEM((608, C), F32),
             pltpu.VMEM((576, 3 * C), BF),
+            pltpu.VMEM((256, 3 * C), BF),
+            pltpu.VMEM((2, C), F32),
             pltpu.VMEM((2, 3, 3, C, C), BF),
-            pltpu.SemaphoreType.DMA((2,)),
+            pltpu.SemaphoreType.DMA((7,)),
+            pltpu.VMEM((64, C), BF),
+            pltpu.SemaphoreType.DMA((16,)),
         ],
         cost_estimate=pl.CostEstimate(
             flops=2 * 1056 * 9 * C * C, bytes_accessed=5_000_000, transcendentals=360_000
@@ -163,7 +214,7 @@
     projected = dot_t(tokens[...], matrix)
     query_gain = near[256:257, 0:128].astype(F32) + far[257:258, 0:128].astype(F32)
     key_gain = near[258:259, 0:128].astype(F32) + far[259:260, 0:128].astype(F32)
-    query_out[...] = norm(projected[:, 0:128], query_gain)
+    query_out[...] = norm(projected[:, 0:128], query_gain * (128 ** (-0.5) * math.log2(math.e)))
     pair_out[:, 0:128] = norm(projected[:, 128:256], key_gain)
     pair_out[:, 128:256] = projected[:, 256:384].astype(BF)
 
@@ -183,24 +234,25 @@
     )(tokens, near, far)
 
 
-def attend_kernel(query, pair, pair_far, tokens, near, far, terms_out):
+def attend_kernel(query, pair, pair_far, tokens, near, far, terms_out, ready, sent):
     head_out = jnp.concatenate([near[192:256], far[192:256]], 0)
-    scale = 128 ** (-0.5)
+
+    def send(step):
+        part = pl.ds(pl.multiple_of(step * 8, 8), 8)
+        return pltpu.make_async_copy(ready.at[part], terms_out.at[part], sent.at[step])
 
     def one_block(step, _):
         rows = pl.ds(pl.multiple_of(step * 256, 256), 256)
         asked = query[rows]
-        scores_near = dot_t(asked, pair[:, 0:128])
+        scores = dot_t(asked, pair[:, 0:128])
         scores_far = dot_t(asked, pair_far[:, 0:128])
         top = jnp.maximum(
-            jnp.max(scores_near, axis=1, keepdims=True), jnp.max(scores_far, axis=1, keepdims=True)
+            jnp.max(scores, axis=1, keepdims=True), jnp.max(scores_far, axis=1, keepdims=True)
         )
-        shifted_near = jnp.exp((scores_near - top) * scale)
-        shifted_far = jnp.exp((scores_far - top) * scale)
-        total = jnp.sum(shifted_near, axis=1, keepdims=True) + jnp.sum(
-            shifted_far, axis=1, keepdims=True
-        )
-        attended = dot(shifted_near.astype(BF), pair[:, 128:256])
+        shifted = jnp.exp2(scores - top)
+        shifted_far = jnp.exp2(scores_far - top)
+        total = jnp.sum(shifted, axis=1, keepdims=True) + jnp.sum(shifted_far, axis=1, keepdims=True)
+        attended = dot(shifted.astype(BF), pair[:, 128:256])
         attended = attended + dot(shifted_far.astype(BF), pair_far[:, 128:256])
         attended = (attended / total).astype(BF)
         terms = dot(attended, head_out) + tokens[rows].astype(F32) * 0.0625
@@ -208,16 +260,21 @@
             parts = [
                 terms[y * 64 + column * 8 : y * 64 + column * 8 + 8] for y in range(4)
             ]
-            terms_out[step * 8 + column] = jnp.concatenate(parts, 0).astype(BF)
+            ready[step * 8 + column] = jnp.concatenate(parts, 0).astype(BF)
+        send(step).start()
         return 0
 
-    lax.fori_loop(0, 4, one_block, 0)
+    lax.fori_loop(0, 4, one_block, 0, unroll=True)
+    for step in range(4):
+        send(step).wait()
 
 
 def attend(query, pair, pair_far, tokens, near, far):
     return pl.pallas_call(
         attend_kernel,
         out_shape=jax.ShapeDtypeStruct((32, 32, C), BF),
+        out_specs=pl.BlockSpec(memory_space=pltpu.HBM),
+        scratch_shapes=[pltpu.VMEM((32, 32, C), BF), pltpu.SemaphoreType.DMA((4,))],
         cost_estimate=pl.CostEstimate(
             flops=2 * 1024 * 128 * (2 * 2048 + C),
             bytes_accessed=3_000_000,

time: 153 us -> 152 us (level)
  no operation moved by 1% of the time
where the time goes in v4:
time: 152 us; the launch traced here: 151 us
  waiting for transfers between devices  69.7 us (46%)
  starting transfers between devices  63.3 us (42%)
  Pallas kernels  14 us (9%)
  local copies, waits for them, and re-layouts  2.27 us (1%)
    all_to_all x4, starting transfers between devices, exchange(): return lax.all_to_all(array, axes, split_axis=0, concat_axis=0, tiled=True)  37 us
    all_to_all x4, waiting for transfers between devices, exchange(): return lax.all_to_all(array, axes, split_axis=0, concat_axis=0, tiled=True)  35.4 us
    ppermute x5, waiting for transfers between devices, move(): return lax.ppermute(array, axes, pairs)  31.1 us
    ppermute x5, starting transfers between devices, move(): return lax.ppermute(array, axes, pairs)  20.4 us
    pallas_call x1, Pallas kernels, conv_stack(): pl.pallas_call(conv_kernel, out_shape=(jax.ShapeDtypeStruct((256, C), BF)...  7.07 us
    ppermute x3, starting transfers between devices, swap(): return lax.ppermute(array, 'c', [(0, 1), (1, 0)])  5.88 us
    pallas_call x1, Pallas kernels, attend(): pl.pallas_call(attend_kernel, out_shape=jax.ShapeDtypeStruct((32, 32, C),...  5.04 us
    ppermute x3, waiting for transfers between devices, swap(): return lax.ppermute(array, 'c', [(0, 1), (1, 0)])  3.18 us
  transfers between devices with their start and end apart: 12, of which 9 were waited for; matrix products, arithmetic and copies ran while one was open for 1% of the time, Pallas kernels for 1%

profile of v4, /device:TPU:16, one launch (start us, length us, event | category | flops | bytes accessed | tf_op | source)
XLA Modules:
  0.0 151.0 jit_solution(7563807167304817896)
XLA Ops:
  0.6 15.2 %all-to-all-start = ((bf16[16,4,4,320]{3,2,1,0:T(4,128)(2,1)}), bf16[16,4,4,320]{3,2,1,0:T(4,128)(2,1)S(1)}, u32[]{:S(2)}, u32[]{:S(2)}) async-start(bf16[16,4,4,320]{3,2,1,0:T(4,128)(2,1)} %param.6), calls=%async_computation | async-start | bytes 393216 | tf_op jit(solution)/shard_map/all_to_all | solution.py:41
  15.9 16.4 %all-to-all-done = bf16[16,4,4,320]{3,2,1,0:T(4,128)(2,1)S(1)} async-done(((bf16[16,4,4,320]{3,2,1,0:T(4,128)(2,1)}), bf16[16,4,4,320]{3,2,1,0:T(4,128)(2,1)S(1)}, u32[]{:S(2)}, u32[]{:S(2)}) %all-to-all-start) | async-done | bytes 163872 | tf_op jit(solution)/shard_map/all_to_all | solution.py:41
  32.2 0.1 copy.13
  32.3 0.1 reshape.39.own
  32.4 1.9 %collective-permute-start = (bf16[32,8,320]{2,1,0:T(8,128)(2,1)S(1)}, bf16[32,8,320]{2,1,0:T(8,128)(2,1)S(1)}, u32[]{:S(2)}, u32[]{:S(2)}) collective-permute-start(bf16[32,8,320]{2,1,0:T(8,128)(2,1)S(1)} %reshape.39.own), channel_id=1, source_target_pairs={{0,32},{32,0},{1,33},{33,1},{2,34},{34,2},{3,35},{35,3},{4,36},{36... | collective-permute-start | bytes 491528 | tf_op jit(solution)/shard_map/ppermute | solution.py:45
  34.3 0.1 broadcast_select_fusion.2
  34.4 2.5 %collective-permute-start.1 = (bf16[32,2,320]{2,1,0:T(2,128)(2,1)S(1)}, bf16[32,2,320]{2,1,0:T(2,128)(2,1)S(1)}, u32[]{:S(2)}, u32[]{:S(2)}) collective-permute-start(bf16[32,2,320]{2,1,0:T(2,128)(2,1)S(1)} %broadcast_select_fusion.2), channel_id=1, source_target_pairs={{0,416},{32,128},{128,32},{160,256},{256,160},{288,384},{384,288},... | collective-permute-start | bytes 122888 | tf_op jit(solution)/shard_map/ppermute | solution.py:37
  36.9 2.9 %collective-permute-done.1 = bf16[32,2,320]{2,1,0:T(2,128)(2,1)S(1)} collective-permute-done((bf16[32,2,320]{2,1,0:T(2,128)(2,1)S(1)}, bf16[32,2,320]{2,1,0:T(2,128)(2,1)S(1)}, u32[]{:S(2)}, u32[]{:S(2)}) %collective-permute-start.1) | collective-permute-done | bytes 40992 | tf_op jit(solution)/shard_map/ppermute | solution.py:37
  39.9 0.0 collective-permute-done.other
  39.9 0.0 copy-start.1
  39.9 0.0 copy-start.2
  39.9 0.2 border.1
  40.2 3.4 %collective-permute-start.2 = (bf16[32,320]{1,0:T(8,128)(2,1)S(1)}, bf16[32,320]{1,0:T(8,128)(2,1)S(1)}, u32[]{:S(2)}, u32[]{:S(2)}) collective-permute-start(bf16[32,320]{1,0:T(8,128)(2,1)S(1)} %get-tuple-element.8), channel_id=1, source_target_pairs={{0,8},{8,16},{16,24},{24,0},{1,9},{9,17},{17,25},{25,1},{2,10},{10... | collective-permute-start | bytes 61448 | tf_op jit(solution)/shard_map/ppermute | solution.py:37
  43.6 3.7 %collective-permute-start.3 = (bf16[32,320]{1,0:T(8,128)(2,1)S(1)}, bf16[32,320]{1,0:T(8,128)(2,1)S(1)}, u32[]{:S(2)}, u32[]{:S(2)}) collective-permute-start(bf16[32,320]{1,0:T(8,128)(2,1)S(1)} %get-tuple-element.9), channel_id=1, source_target_pairs={{0,24},{8,0},{16,8},{24,16},{1,25},{9,1},{17,9},{25,17},{2,26},{10... | collective-permute-start | bytes 61448 | tf_op jit(solution)/shard_map/ppermute | solution.py:37
  47.2 0.8 fusion.2
  48.0 0.0 collective-permute-done.2.before
  48.0 1.2 collective-permute-done.3.after
  49.3 0.0 copy-start
  49.3 0.7 copy-done
  50.0 7.1 %conv_stack.1 = (bf16[256,320]{1,0:T(8,128)(2,1)S(1)}, bf16[16,64,320]{2,1,0:T(8,128)(2,1)}) custom-call(s32[1]{0:T(128)} %bitcast.core, bf16[32,8,320]{2,1,0:T(8,128)(2,1)S(1)} %reshape.39.own, bf16[32,8,320]{2,1,0:T(8,128)(2,1)S(1)} %collective-permute-done.other, bf16[64,320]{1,0:T(8,128)(2,1)S(1)} %reshape.40.edge, ...), custom_call_target="tpu_custom_call" | custom-call | flops 1946419200 | bytes 5000000 | tf_op jit(solution)/shard_map/conv_stack/pallas_call | solution.py:175
  57.1 7.2 %all-to-all-start.2 = ((bf16[16,64,320]{2,1,0:T(8,128)(2,1)}), bf16[16,64,320]{2,1,0:T(8,128)(2,1)S(1)}, u32[]{:S(2)}, u32[]{:S(2)}) async-start(bf16[16,64,320]{2,1,0:T(8,128)(2,1)} %get-tuple-element.11), calls=%async_computation.2 | async-start | bytes 1572864 | tf_op jit(solution)/shard_map/all_to_all | solution.py:41
  64.3 0.0 copy-done.1
  64.3 0.0 copy-done.2
  64.3 2.0 %collective-permute-start.4 = (bf16[272,320]{1,0:T(8,128)(2,1)S(1)}, bf16[272,320]{1,0:T(8,128)(2,1)S(1)}, u32[]{:S(2)}, u32[]{:S(2)}) collective-permute-start(bf16[272,320]{1,0:T(8,128)(2,1)S(1)} %fusion.1), channel_id=1, source_target_pairs={{0,68},{1,69},{2,198},{3,199},{4,256},{5,257},{6,386},{7,387},{32,... | collective-permute-start | bytes 522248 | tf_op jit(solution)/shard_map/ppermute | solution.py:37
  66.4 21.1 %collective-permute-done.4 = bf16[272,320]{1,0:T(8,128)(2,1)S(1)} collective-permute-done((bf16[272,320]{1,0:T(8,128)(2,1)S(1)}, bf16[272,320]{1,0:T(8,128)(2,1)S(1)}, u32[]{:S(2)}, u32[]{:S(2)}) %collective-permute-start.4) | collective-permute-done | bytes 174112 | tf_op jit(solution)/shard_map/ppermute | solution.py:37
  87.5 1.9 %collective-permute-start.5 = (bf16[272,320]{1,0:T(8,128)(2,1)S(1)}, bf16[272,320]{1,0:T(8,128)(2,1)S(1)}, u32[]{:S(2)}, u32[]{:S(2)}) collective-permute-start(bf16[272,320]{1,0:T(8,128)(2,1)S(1)} %collective-permute-done.4), channel_id=1, source_target_pairs={{0,32},{32,0},{1,33},{33,1},{2,34},{34,2},{3,35},{35,3},{4,36},{36... | collective-permute-start | bytes 522248 | tf_op jit(solution)/shard_map/ppermute | solution.py:45
  89.4 1.4 collective-permute-done.5
  90.9 0.0 all-to-all-done.2
  90.9 0.8 heads.1
  91.6 2.0 %collective-permute-start.6 = (bf16[1024,256]{1,0:T(8,128)(2,1)S(1)}, bf16[1024,256]{1,0:T(8,128)(2,1)S(1)}, u32[]{:S(2)}, u32[]{:S(2)}) collective-permute-start(bf16[1024,256]{1,0:T(8,128)(2,1)S(1)} %get-tuple-element.13.pair), channel_id=1, source_target_pairs={{0,32},{32,0},{1,33},{33,1},{2,34},{34,2},{3,35},{35,3},{4,36},{36... | collective-permute-start | bytes 1572872 | tf_op jit(solution)/shard_map/ppermute | solution.py:45
  93.7 1.7 %collective-permute-done.6.pair_far = bf16[1024,256]{1,0:T(8,128)(2,1)S(1)} collective-permute-done((bf16[1024,256]{1,0:T(8,128)(2,1)S(1)}, bf16[1024,256]{1,0:T(8,128)(2,1)S(1)}, u32[]{:S(2)}, u32[]{:S(2)}) %collective-permute-start.6) | collective-permute-done | bytes 524320 | tf_op jit(solution)/shard_map/ppermute | solution.py:45
  95.5 5.0 %attend.1 = bf16[32,32,320]{2,1,0:T(8,128)(2,1)} custom-call(bf16[1024,128]{1,0:T(8,128)(2,1)S(1)} %get-tuple-element.12.query, bf16[1024,256]{1,0:T(8,128)(2,1)S(1)} %get-tuple-element.13.pair, bf16[1024,256]{1,0:T(8,128)(2,1)S(1)} %collective-permute-done.6.pair_far, bf16[1024,320]{1,0:T(8,128)(2,1)S(1)} %bitcast.12, ...), custom_call_target="tpu_custom_call" | custom-call | flops 1157627904 | bytes 3000000 | tf_op jit(solution)/shard_map/attend/pallas_call | solution.py:273
  100.5 7.9 %all-to-all-start.3 = ((bf16[32,32,320]{2,1,0:T(8,128)(2,1)}), bf16[32,32,320]{2,1,0:T(8,128)(2,1)S(1)}, u32[]{:S(2)}, u32[]{:S(2)}) async-start(bf16[32,32,320]{2,1,0:T(8,128)(2,1)} %attend.1), calls=%async_computation.3 | async-start | bytes 1572864 | tf_op jit(solution)/shard_map/all_to_all | solution.py:41
  108.4 0.7 reshape.41
  109.2 11.7 %all-to-all-done.3 = bf16[32,32,320]{2,1,0:T(8,128)(2,1)S(1)} async-done(((bf16[32,32,320]{2,1,0:T(8,128)(2,1)}), bf16[32,32,320]{2,1,0:T(8,128)(2,1)S(1)}, u32[]{:S(2)}, u32[]{:S(2)}) %all-to-all-start.3) | async-done | bytes 655392 | tf_op jit(solution)/shard_map/all_to_all | solution.py:41
  120.9 6.6 %all-to-all-start.1 = ((bf16[16,4,4,320]{3,2,1,0:T(4,128)(2,1)}), bf16[16,4,4,320]{3,2,1,0:T(4,128)(2,1)S(1)}, u32[]{:S(2)}, u32[]{:S(2)}) async-start(bf16[16,4,4,320]{3,2,1,0:T(4,128)(2,1)} %reshape.41), calls=%async_computation.1 | async-start | bytes 393216 | tf_op jit(solution)/shard_map/all_to_all | solution.py:41
  127.6 0.2 sum_heads.1
  127.7 8.8 %collective-permute-start.7 = (bf16[32,2,320]{2,1,0:T(2,128)(2,1)S(1)}, bf16[32,2,320]{2,1,0:T(2,128)(2,1)S(1)}, u32[]{:S(2)}, u32[]{:S(2)}) collective-permute-start(bf16[32,2,320]{2,1,0:T(2,128)(2,1)S(1)} %sum_heads.1), channel_id=1, source_target_pairs={{0,0},{1,32},{2,64},{3,96},{4,128},{5,160},{6,192},{7,224},{8,8},{... | collective-permute-start | bytes 122888 | tf_op jit(solution)/shard_map/ppermute | solution.py:37
  136.6 7.3 %all-to-all-done.1.source = bf16[16,4,4,320]{3,2,1,0:T(4,128)(2,1)S(1)} async-done(((bf16[16,4,4,320]{3,2,1,0:T(4,128)(2,1)}), bf16[16,4,4,320]{3,2,1,0:T(4,128)(2,1)S(1)}, u32[]{:S(2)}, u32[]{:S(2)}) %all-to-all-start.1) | async-done | bytes 163872 | tf_op jit(solution)/shard_map/all_to_all | solution.py:41
  143.8 0.7 copied.1
  144.5 5.8 %collective-permute-done.7 = bf16[32,2,320]{2,1,0:T(2,128)(2,1)S(1)} collective-permute-done((bf16[32,2,320]{2,1,0:T(2,128)(2,1)S(1)}, bf16[32,2,320]{2,1,0:T(2,128)(2,1)S(1)}, u32[]{:S(2)}, u32[]{:S(2)}) %collective-permute-start.7) | collective-permute-done | bytes 40992 | tf_op jit(solution)/shard_map/ppermute | solution.py:37
  150.4 0.6 copy.15
  (4 shorter events, 0.1 us)
Async XLA Ops:
  0.6 31.6 %all-to-all-start = ((bf16[16,4,4,320]{3,2,1,0:T(4,128)(2,1)}), bf16[16,4,4,320]{3,2,1,0:T(4,128)(2,1)S(1)}, u32[]{:S(2)}, u32[]{:S(2)}) async-start(bf16[16,4,4,320]{3,2,1,0:T(4,128)(2,1)} %param.6), calls=%async_computation | async-start | bytes 393216 | tf_op jit(solution)/shard_map/all_to_all | solution.py:41
  32.4 7.5 %collective-permute-start = (bf16[32,8,320]{2,1,0:T(8,128)(2,1)S(1)}, bf16[32,8,320]{2,1,0:T(8,128)(2,1)S(1)}, u32[]{:S(2)}, u32[]{:S(2)}) collective-permute-start(bf16[32,8,320]{2,1,0:T(8,128)(2,1)S(1)} %reshape.39.own), channel_id=1, source_target_pairs={{0,32},{32,0},{1,33},{33,1},{2,34},{34,2},{3,35},{35,3},{4,36},{36... | collective-permute-start | bytes 491528 | tf_op jit(solution)/shard_map/ppermute | solution.py:45
  34.4 5.4 %collective-permute-start.1 = (bf16[32,2,320]{2,1,0:T(2,128)(2,1)S(1)}, bf16[32,2,320]{2,1,0:T(2,128)(2,1)S(1)}, u32[]{:S(2)}, u32[]{:S(2)}) collective-permute-start(bf16[32,2,320]{2,1,0:T(2,128)(2,1)S(1)} %broadcast_select_fusion.2), channel_id=1, source_target_pairs={{0,416},{32,128},{128,32},{160,256},{256,160},{288,384},{384,288},... | collective-permute-start | bytes 122888 | tf_op jit(solution)/shard_map/ppermute | solution.py:37
  39.9 24.4 %copy-start.1 = (bf16[3,64,320]{2,1,0:T(8,128)(2,1)S(1)}, bf16[3,64,320]{2,1,0:T(8,128)(2,1)}, u32[]{:S(2)}) copy-start(bf16[3,64,320]{2,1,0:T(8,128)(2,1)} %param.9) | copy-start | bytes 368644
  39.9 24.4 %copy-start.2 = (bf16[64,320]{1,0:T(8,128)(2,1)S(1)}, bf16[64,320]{1,0:T(8,128)(2,1)}, u32[]{:S(2)}) copy-start(bf16[64,320]{1,0:T(8,128)(2,1)} %param.11) | copy-start | bytes 122884
  40.2 7.9 %collective-permute-start.2 = (bf16[32,320]{1,0:T(8,128)(2,1)S(1)}, bf16[32,320]{1,0:T(8,128)(2,1)S(1)}, u32[]{:S(2)}, u32[]{:S(2)}) collective-permute-start(bf16[32,320]{1,0:T(8,128)(2,1)S(1)} %get-tuple-element.8), channel_id=1, source_target_pairs={{0,8},{8,16},{16,24},{24,0},{1,9},{9,17},{17,25},{25,1},{2,10},{10... | collective-permute-start | bytes 61448 | tf_op jit(solution)/shard_map/ppermute | solution.py:37
  43.6 5.7 %collective-permute-start.3 = (bf16[32,320]{1,0:T(8,128)(2,1)S(1)}, bf16[32,320]{1,0:T(8,128)(2,1)S(1)}, u32[]{:S(2)}, u32[]{:S(2)}) collective-permute-start(bf16[32,320]{1,0:T(8,128)(2,1)S(1)} %get-tuple-element.9), channel_id=1, source_target_pairs={{0,24},{8,0},{16,8},{24,16},{1,25},{9,1},{17,9},{25,17},{2,26},{10... | collective-permute-start | bytes 61448 | tf_op jit(solution)/shard_map/ppermute | solution.py:37
  49.3 0.7 copy-start
  57.1 33.8 %all-to-all-start.2 = ((bf16[16,64,320]{2,1,0:T(8,128)(2,1)}), bf16[16,64,320]{2,1,0:T(8,128)(2,1)S(1)}, u32[]{:S(2)}, u32[]{:S(2)}) async-start(bf16[16,64,320]{2,1,0:T(8,128)(2,1)} %get-tuple-element.11), calls=%async_computation.2 | async-start | bytes 1572864 | tf_op jit(solution)/shard_map/all_to_all | solution.py:41
  64.3 23.2 %collective-permute-start.4 = (bf16[272,320]{1,0:T(8,128)(2,1)S(1)}, bf16[272,320]{1,0:T(8,128)(2,1)S(1)}, u32[]{:S(2)}, u32[]{:S(2)}) collective-permute-start(bf16[272,320]{1,0:T(8,128)(2,1)S(1)} %fusion.1), channel_id=1, source_target_pairs={{0,68},{1,69},{2,198},{3,199},{4,256},{5,257},{6,386},{7,387},{32,... | collective-permute-start | bytes 522248 | tf_op jit(solution)/shard_map/ppermute | solution.py:37
  87.5 3.3 %collective-permute-start.5 = (bf16[272,320]{1,0:T(8,128)(2,1)S(1)}, bf16[272,320]{1,0:T(8,128)(2,1)S(1)}, u32[]{:S(2)}, u32[]{:S(2)}) collective-permute-start(bf16[272,320]{1,0:T(8,128)(2,1)S(1)} %collective-permute-done.4), channel_id=1, source_target_pairs={{0,32},{32,0},{1,33},{33,1},{2,34},{34,2},{3,35},{35,3},{4,36},{36... | collective-permute-start | bytes 522248 | tf_op jit(solution)/shard_map/ppermute | solution.py:45
  91.6 3.8 %collective-permute-start.6 = (bf16[1024,256]{1,0:T(8,128)(2,1)S(1)}, bf16[1024,256]{1,0:T(8,128)(2,1)S(1)}, u32[]{:S(2)}, u32[]{:S(2)}) collective-permute-start(bf16[1024,256]{1,0:T(8,128)(2,1)S(1)} %get-tuple-element.13.pair), channel_id=1, source_target_pairs={{0,32},{32,0},{1,33},{33,1},{2,34},{34,2},{3,35},{35,3},{4,36},{36... | collective-permute-start | bytes 1572872 | tf_op jit(solution)/shard_map/ppermute | solution.py:45
  100.5 20.4 %all-to-all-start.3 = ((bf16[32,32,320]{2,1,0:T(8,128)(2,1)}), bf16[32,32,320]{2,1,0:T(8,128)(2,1)S(1)}, u32[]{:S(2)}, u32[]{:S(2)}) async-start(bf16[32,32,320]{2,1,0:T(8,128)(2,1)} %attend.1), calls=%async_computation.3 | async-start | bytes 1572864 | tf_op jit(solution)/shard_map/all_to_all | solution.py:41
  120.9 22.9 %all-to-all-start.1 = ((bf16[16,4,4,320]{3,2,1,0:T(4,128)(2,1)}), bf16[16,4,4,320]{3,2,1,0:T(4,128)(2,1)S(1)}, u32[]{:S(2)}, u32[]{:S(2)}) async-start(bf16[16,4,4,320]{3,2,1,0:T(4,128)(2,1)} %reshape.41), calls=%async_computation.1 | async-start | bytes 393216 | tf_op jit(solution)/shard_map/all_to_all | solution.py:41
  127.7 22.6 %collective-permute-start.7 = (bf16[32,2,320]{2,1,0:T(2,128)(2,1)S(1)}, bf16[32,2,320]{2,1,0:T(2,128)(2,1)S(1)}, u32[]{:S(2)}, u32[]{:S(2)}) collective-permute-start(bf16[32,2,320]{2,1,0:T(2,128)(2,1)S(1)} %sum_heads.1), channel_id=1, source_target_pairs={{0,0},{1,32},{2,64},{3,96},{4,128},{5,160},{6,192},{7,224},{8,8},{... | collective-permute-start | bytes 122888 | tf_op jit(solution)/shard_map/ppermute | solution.py:37

commit v5 on v4

--- a/solution.py
+++ b/solution.py
@@ -100,7 +100,7 @@
     edge,
     before,
     after,
-    stored_gains,
+    gains,
     stored,
     feat_out,
     pool_out,
@@ -108,14 +108,11 @@
     act,
     taps,
     taps_odd,
-    gains,
     kernels,
     arrived,
     pool,
     sent,
 ):
-    gain_fetch = pltpu.make_async_copy(stored_gains, gains, arrived.at[6])
-    gain_fetch.start()
     fetches = []
     for layer in range(2):
         for b in range(3):
@@ -137,7 +134,6 @@
     held[0:32] = before[...].astype(F32)
     held[32:544] = picked(core[0], 0, 32, own, other, edge)
     held[544:576] = after[...].astype(F32)
-    gain_fetch.wait()
     act[0:576] = activation(held[0:576], 0)
     act[576:592] = jnp.zeros((16, C), F32)
     for a in range(3):
@@ -180,16 +176,15 @@
         ),
         out_specs=(pl.BlockSpec(memory_space=pltpu.VMEM), pl.BlockSpec(memory_space=pltpu.HBM)),
         in_specs=[pl.BlockSpec(memory_space=pltpu.SMEM)]
-        + [pl.BlockSpec(memory_space=pltpu.VMEM)] * 5
-        + [pl.BlockSpec(memory_space=pltpu.HBM)] * 2,
+        + [pl.BlockSpec(memory_space=pltpu.VMEM)] * 6
+        + [pl.BlockSpec(memory_space=pltpu.HBM)],
         scratch_shapes=[
             pltpu.VMEM((608, C), F32),
             pltpu.VMEM((608, C), F32),
             pltpu.VMEM((576, 3 * C), BF),
             pltpu.VMEM((256, 3 * C), BF),
-            pltpu.VMEM((2, C), F32),
             pltpu.VMEM((2, 3, 3, C, C), BF),
-            pltpu.SemaphoreType.DMA((7,)),
+            pltpu.SemaphoreType.DMA((6,)),
             pltpu.VMEM((64, C), BF),
             pltpu.SemaphoreType.DMA((16,)),
         ],
@@ -331,13 +326,20 @@
     core = lax.axis_index("c")
     first = core == 0
     core = core.astype(jnp.int32).reshape(1)
+    near = move(qkv_weight.reshape(192, C), ("y", "h", "c", "l"), nearest_plane)
+
     tiles = exchange(latent, DEPTH)
 
     gains = qk_gain.reshape(2, 1, 64)
-    gains = jnp.concatenate([jnp.pad(gains, ((0, 0), (0, 0), (0, 64))), jnp.pad(gains, ((0, 0), (0, 0), (64, 0)))], 1)
+    gains = jnp.concatenate(
+        [jnp.pad(gains, ((0, 0), (0, 0), (0, 64))), jnp.pad(gains, ((0, 0), (0, 0), (64, 0)))], 1
+    )
     gains = jnp.pad(gains.reshape(4, 128), ((0, 12), (0, C - 128)))
-    packed = jnp.concatenate([qkv_weight.reshape(192, C), out_weight, gains], 0)
-    near = move(packed, ("y", "h", "c", "l"), nearest_plane)
+    rest = move(
+        jnp.concatenate([out_weight, gains], 0), ("y", "h", "c", "l"), nearest_plane
+    )
+    near = jnp.concatenate([near, rest], 0)
+    conv_gain = jnp.pad(conv_gain, ((0, 6), (0, 0)))
     far = swap(near)
     near, far = jnp.where(first, near, far), jnp.where(first, far, near)
 

time: 152 us -> 143 us (0.941)
  waiting for transfers between devices: 69.7 us -> 54.6 us
  starting transfers between devices: 63.3 us -> 69.2 us
    ppermute x5 -> x6, waiting for transfers between devices: 31.1 us -> 10.6 us  [move(): return lax.ppermute(array, axes, pairs)]
    ppermute x5 -> x6, starting transfers between devices: 20.4 us -> 26.7 us  [move(): return lax.ppermute(array, axes, pairs)]
    all_to_all x4, waiting for transfers between devices: 35.4 us -> 40.6 us  [exchange(): return lax.all_to_all(array, axes, split_axis=0, concat_axis=0, tiled=True)]
  transfers between devices with their start and end apart: 12 -> 13, of which waited for: 9 -> 9; matrix products, arithmetic and copies ran while one was open for 1% -> 2% of each run, Pallas kernels for 1% -> 6%
where the time goes in v5:
time: 143 us
  starting transfers between devices  69.2 us (48%)
  waiting for transfers between devices  54.6 us (38%)
  Pallas kernels  13.9 us (10%)
  local copies, waits for them, and re-layouts  2.3 us (2%)
  other arithmetic  1.75 us (1%)
    all_to_all x4, waiting for transfers between devices, exchange(): return lax.all_to_all(array, axes, split_axis=0, concat_axis=0, tiled=True)  40.6 us
    all_to_all x4, starting transfers between devices, exchange(): return lax.all_to_all(array, axes, split_axis=0, concat_axis=0, tiled=True)  36.7 us
    ppermute x6, starting transfers between devices, move(): return lax.ppermute(array, axes, pairs)  26.7 us
    ppermute x6, waiting for transfers between devices, move(): return lax.ppermute(array, axes, pairs)  10.6 us
    pallas_call x1, Pallas kernels, conv_stack(): pl.pallas_call(conv_kernel, out_shape=(jax.ShapeDtypeStruct((256, C), BF)...  7.04 us
    ppermute x3, starting transfers between devices, swap(): return lax.ppermute(array, 'c', [(0, 1), (1, 0)])  5.76 us
    pallas_call x1, Pallas kernels, attend(): pl.pallas_call(attend_kernel, out_shape=jax.ShapeDtypeStruct((32, 32, C),...  5.04 us
    ppermute x3, waiting for transfers between devices, swap(): return lax.ppermute(array, 'c', [(0, 1), (1, 0)])  3.3 us
  transfers between devices with their start and end apart: 13, of which 9 were waited for; matrix products, arithmetic and copies ran while one was open for 2% of the time, Pallas kernels for 6%

profile of v5, /device:TPU:16, one launch (start us, length us, event | category | flops | bytes accessed | tf_op | source)
XLA Modules:
  0.0 142.6 jit_solution(10926433221038297958)
XLA Ops:
  0.6 15.2 %all-to-all-start = ((bf16[16,4,4,320]{3,2,1,0:T(4,128)(2,1)}), bf16[16,4,4,320]{3,2,1,0:T(4,128)(2,1)S(1)}, u32[]{:S(2)}, u32[]{:S(2)}) async-start(bf16[16,4,4,320]{3,2,1,0:T(4,128)(2,1)} %param.6), calls=%async_computation | async-start | bytes 393216 | tf_op jit(solution)/shard_map/all_to_all | solution.py:41
  15.9 16.4 %all-to-all-done = bf16[16,4,4,320]{3,2,1,0:T(4,128)(2,1)S(1)} async-done(((bf16[16,4,4,320]{3,2,1,0:T(4,128)(2,1)}), bf16[16,4,4,320]{3,2,1,0:T(4,128)(2,1)S(1)}, u32[]{:S(2)}, u32[]{:S(2)}) %all-to-all-start) | async-done | bytes 163872 | tf_op jit(solution)/shard_map/all_to_all | solution.py:41
  32.2 0.1 copy.13
  32.3 0.1 reshape.39.own
  32.4 1.9 %collective-permute-start = (bf16[32,8,320]{2,1,0:T(8,128)(2,1)S(1)}, bf16[32,8,320]{2,1,0:T(8,128)(2,1)S(1)}, u32[]{:S(2)}, u32[]{:S(2)}) collective-permute-start(bf16[32,8,320]{2,1,0:T(8,128)(2,1)S(1)} %reshape.39.own), channel_id=1, source_target_pairs={{0,32},{32,0},{1,33},{33,1},{2,34},{34,2},{3,35},{35,3},{4,36},{36... | collective-permute-start | bytes 491528 | tf_op jit(solution)/shard_map/ppermute | solution.py:45
  34.3 0.1 broadcast_select_fusion.2
  34.4 2.5 %collective-permute-start.1 = (bf16[32,2,320]{2,1,0:T(2,128)(2,1)S(1)}, bf16[32,2,320]{2,1,0:T(2,128)(2,1)S(1)}, u32[]{:S(2)}, u32[]{:S(2)}) collective-permute-start(bf16[32,2,320]{2,1,0:T(2,128)(2,1)S(1)} %broadcast_select_fusion.2), channel_id=1, source_target_pairs={{0,416},{32,128},{128,32},{160,256},{256,160},{288,384},{384,288},... | collective-permute-start | bytes 122888 | tf_op jit(solution)/shard_map/ppermute | solution.py:37
  36.9 0.8 fusion.2
  37.7 2.1 %collective-permute-done.1 = bf16[32,2,320]{2,1,0:T(2,128)(2,1)S(1)} collective-permute-done((bf16[32,2,320]{2,1,0:T(2,128)(2,1)S(1)}, bf16[32,2,320]{2,1,0:T(2,128)(2,1)S(1)}, u32[]{:S(2)}, u32[]{:S(2)}) %collective-permute-start.1) | collective-permute-done | bytes 40992 | tf_op jit(solution)/shard_map/ppermute | solution.py:37
  39.9 0.0 collective-permute-done.other
  39.9 0.2 border.1
  40.1 3.4 %collective-permute-start.2 = (bf16[32,320]{1,0:T(8,128)(2,1)S(1)}, bf16[32,320]{1,0:T(8,128)(2,1)S(1)}, u32[]{:S(2)}, u32[]{:S(2)}) collective-permute-start(bf16[32,320]{1,0:T(8,128)(2,1)S(1)} %get-tuple-element.8), channel_id=1, source_target_pairs={{0,8},{8,16},{16,24},{24,0},{1,9},{9,17},{17,25},{25,1},{2,10},{10... | collective-permute-start | bytes 61448 | tf_op jit(solution)/shard_map/ppermute | solution.py:37
  43.5 3.7 %collective-permute-start.3 = (bf16[32,320]{1,0:T(8,128)(2,1)S(1)}, bf16[32,320]{1,0:T(8,128)(2,1)S(1)}, u32[]{:S(2)}, u32[]{:S(2)}) collective-permute-start(bf16[32,320]{1,0:T(8,128)(2,1)S(1)} %get-tuple-element.9), channel_id=1, source_target_pairs={{0,24},{8,0},{16,8},{24,16},{1,25},{9,1},{17,9},{25,17},{2,26},{10... | collective-permute-start | bytes 61448 | tf_op jit(solution)/shard_map/ppermute | solution.py:37
  47.2 0.8 fusion.1
  48.0 3.6 %collective-permute-start.5 = (bf16[80,320]{1,0:T(8,128)(2,1)S(1)}, bf16[80,320]{1,0:T(8,128)(2,1)S(1)}, u32[]{:S(2)}, u32[]{:S(2)}) collective-permute-start(bf16[80,320]{1,0:T(8,128)(2,1)S(1)} %fusion.1), channel_id=1, source_target_pairs={{0,68},{1,69},{2,198},{3,199},{4,256},{5,257},{6,386},{7,387},{32,... | collective-permute-start | bytes 153608 | tf_op jit(solution)/shard_map/ppermute | solution.py:37
  51.6 4.8 %collective-permute-start.4 = (bf16[192,320]{1,0:T(8,128)(2,1)}, bf16[192,320]{1,0:T(8,128)(2,1)S(1)}, u32[]{:S(2)}, u32[]{:S(2)}) collective-permute-start(bf16[192,320]{1,0:T(8,128)(2,1)} %bitcast.18), channel_id=1, source_target_pairs={{0,68},{1,69},{2,198},{3,199},{4,256},{5,257},{6,386},{7,387},{32,... | collective-permute-start | bytes 368648 | tf_op jit(solution)/shard_map/ppermute | solution.py:37
  56.4 0.7 pad.16.gains
  57.1 0.0 collective-permute-done.2.before
  57.1 0.0 collective-permute-done.3.after
  57.1 7.0 %conv_stack.1 = (bf16[256,320]{1,0:T(8,128)(2,1)S(1)}, bf16[16,64,320]{2,1,0:T(8,128)(2,1)}) custom-call(s32[1]{0:T(128)} %bitcast.core, bf16[32,8,320]{2,1,0:T(8,128)(2,1)S(1)} %reshape.39.own, bf16[32,8,320]{2,1,0:T(8,128)(2,1)S(1)} %collective-permute-done.other, bf16[64,320]{1,0:T(8,128)(2,1)S(1)} %reshape.40.edge, ...), custom_call_target="tpu_custom_call" | custom-call | flops 1946419200 | bytes 5000000 | tf_op jit(solution)/shard_map/conv_stack/pallas_call | solution.py:171
  64.2 7.0 %all-to-all-start.2 = ((bf16[16,64,320]{2,1,0:T(8,128)(2,1)}), bf16[16,64,320]{2,1,0:T(8,128)(2,1)S(1)}, u32[]{:S(2)}, u32[]{:S(2)}) async-start(bf16[16,64,320]{2,1,0:T(8,128)(2,1)} %get-tuple-element.11), calls=%async_computation.2 | async-start | bytes 1572864 | tf_op jit(solution)/shard_map/all_to_all | solution.py:41
  71.2 2.7 %collective-permute-done.4 = bf16[192,320]{1,0:T(8,128)(2,1)S(1)} collective-permute-done((bf16[192,320]{1,0:T(8,128)(2,1)}, bf16[192,320]{1,0:T(8,128)(2,1)S(1)}, u32[]{:S(2)}, u32[]{:S(2)}) %collective-permute-start.4) | collective-permute-done | bytes 122912 | tf_op jit(solution)/shard_map/ppermute | solution.py:37
  73.9 0.0 collective-permute-done.5
  74.0 1.9 %collective-permute-start.6 = (bf16[272,320]{1,0:T(8,128)(2,1)S(1)}, bf16[272,320]{1,0:T(8,128)(2,1)S(1)}, u32[]{:S(2)}, u32[]{:S(2)}) collective-permute-start(bf16[272,320]{1,0:T(8,128)(2,1)S(1)} %constant_dynamic-update-slice_fusion), channel_id=1, source_target_pairs={{0,32},{32,0},{1,33},{33,1},{2,34},{34,2},{3,35},{35,3},{4,36},{36... | collective-permute-start | bytes 522248 | tf_op jit(solution)/shard_map/ppermute | solution.py:45
  75.9 1.4 collective-permute-done.6
  77.4 5.2 %all-to-all-done.2 = bf16[16,64,320]{2,1,0:T(8,128)(2,1)S(1)} async-done(((bf16[16,64,320]{2,1,0:T(8,128)(2,1)}), bf16[16,64,320]{2,1,0:T(8,128)(2,1)S(1)}, u32[]{:S(2)}, u32[]{:S(2)}) %all-to-all-start.2) | async-done | bytes 655392 | tf_op jit(solution)/shard_map/all_to_all | solution.py:41
  82.6 0.8 heads.1
  83.3 1.9 %collective-permute-start.7 = (bf16[1024,256]{1,0:T(8,128)(2,1)S(1)}, bf16[1024,256]{1,0:T(8,128)(2,1)S(1)}, u32[]{:S(2)}, u32[]{:S(2)}) collective-permute-start(bf16[1024,256]{1,0:T(8,128)(2,1)S(1)} %get-tuple-element.13.pair), channel_id=1, source_target_pairs={{0,32},{32,0},{1,33},{33,1},{2,34},{34,2},{3,35},{35,3},{4,36},{36... | collective-permute-start | bytes 1572872 | tf_op jit(solution)/shard_map/ppermute | solution.py:45
  85.3 1.9 %collective-permute-done.7.pair_far = bf16[1024,256]{1,0:T(8,128)(2,1)S(1)} collective-permute-done((bf16[1024,256]{1,0:T(8,128)(2,1)S(1)}, bf16[1024,256]{1,0:T(8,128)(2,1)S(1)}, u32[]{:S(2)}, u32[]{:S(2)}) %collective-permute-start.7) | collective-permute-done | bytes 524320 | tf_op jit(solution)/shard_map/ppermute | solution.py:45
  87.1 5.0 %attend.1 = bf16[32,32,320]{2,1,0:T(8,128)(2,1)} custom-call(bf16[1024,128]{1,0:T(8,128)(2,1)S(1)} %get-tuple-element.12.query, bf16[1024,256]{1,0:T(8,128)(2,1)S(1)} %get-tuple-element.13.pair, bf16[1024,256]{1,0:T(8,128)(2,1)S(1)} %collective-permute-done.7.pair_far, bf16[1024,320]{1,0:T(8,128)(2,1)S(1)} %bitcast.12, ...), custom_call_target="tpu_custom_call" | custom-call | flops 1157627904 | bytes 3000000 | tf_op jit(solution)/shard_map/attend/pallas_call | solution.py:268
  92.2 6.0 %all-to-all-start.3 = ((bf16[32,32,320]{2,1,0:T(8,128)(2,1)}), bf16[32,32,320]{2,1,0:T(8,128)(2,1)S(1)}, u32[]{:S(2)}, u32[]{:S(2)}) async-start(bf16[32,32,320]{2,1,0:T(8,128)(2,1)} %attend.1), calls=%async_computation.3 | async-start | bytes 1572864 | tf_op jit(solution)/shard_map/all_to_all | solution.py:41
  98.2 0.7 reshape.41
  99.0 11.8 %all-to-all-done.3 = bf16[32,32,320]{2,1,0:T(8,128)(2,1)S(1)} async-done(((bf16[32,32,320]{2,1,0:T(8,128)(2,1)}), bf16[32,32,320]{2,1,0:T(8,128)(2,1)S(1)}, u32[]{:S(2)}, u32[]{:S(2)}) %all-to-all-start.3) | async-done | bytes 655392 | tf_op jit(solution)/shard_map/all_to_all | solution.py:41
  110.8 8.4 %all-to-all-start.1 = ((bf16[16,4,4,320]{3,2,1,0:T(4,128)(2,1)}), bf16[16,4,4,320]{3,2,1,0:T(4,128)(2,1)S(1)}, u32[]{:S(2)}, u32[]{:S(2)}) async-start(bf16[16,4,4,320]{3,2,1,0:T(4,128)(2,1)} %reshape.41), calls=%async_computation.1 | async-start | bytes 393216 | tf_op jit(solution)/shard_map/all_to_all | solution.py:41
  119.1 0.2 sum_heads.1
  119.3 8.8 %collective-permute-start.8 = (bf16[32,2,320]{2,1,0:T(2,128)(2,1)S(1)}, bf16[32,2,320]{2,1,0:T(2,128)(2,1)S(1)}, u32[]{:S(2)}, u32[]{:S(2)}) collective-permute-start(bf16[32,2,320]{2,1,0:T(2,128)(2,1)S(1)} %sum_heads.1), channel_id=1, source_target_pairs={{0,0},{1,32},{2,64},{3,96},{4,128},{5,160},{6,192},{7,224},{8,8},{... | collective-permute-start | bytes 122888 | tf_op jit(solution)/shard_map/ppermute | solution.py:37
  128.1 7.3 %all-to-all-done.1.source = bf16[16,4,4,320]{3,2,1,0:T(4,128)(2,1)S(1)} async-done(((bf16[16,4,4,320]{3,2,1,0:T(4,128)(2,1)}), bf16[16,4,4,320]{3,2,1,0:T(4,128)(2,1)S(1)}, u32[]{:S(2)}, u32[]{:S(2)}) %all-to-all-start.1) | async-done | bytes 163872 | tf_op jit(solution)/shard_map/all_to_all | solution.py:41
  135.4 0.7 copied.1
  136.1 5.8 %collective-permute-done.8 = bf16[32,2,320]{2,1,0:T(2,128)(2,1)S(1)} collective-permute-done((bf16[32,2,320]{2,1,0:T(2,128)(2,1)S(1)}, bf16[32,2,320]{2,1,0:T(2,128)(2,1)S(1)}, u32[]{:S(2)}, u32[]{:S(2)}) %collective-permute-start.8) | collective-permute-done | bytes 40992 | tf_op jit(solution)/shard_map/ppermute | solution.py:37
  141.9 0.6 copy.16
  (5 shorter events, 0.1 us)
Async XLA Ops:
  0.6 31.6 %all-to-all-start = ((bf16[16,4,4,320]{3,2,1,0:T(4,128)(2,1)}), bf16[16,4,4,320]{3,2,1,0:T(4,128)(2,1)S(1)}, u32[]{:S(2)}, u32[]{:S(2)}) async-start(bf16[16,4,4,320]{3,2,1,0:T(4,128)(2,1)} %param.6), calls=%async_computation | async-start | bytes 393216 | tf_op jit(solution)/shard_map/all_to_all | solution.py:41
  32.4 7.5 %collective-permute-start = (bf16[32,8,320]{2,1,0:T(8,128)(2,1)S(1)}, bf16[32,8,320]{2,1,0:T(8,128)(2,1)S(1)}, u32[]{:S(2)}, u32[]{:S(2)}) collective-permute-start(bf16[32,8,320]{2,1,0:T(8,128)(2,1)S(1)} %reshape.39.own), channel_id=1, source_target_pairs={{0,32},{32,0},{1,33},{33,1},{2,34},{34,2},{3,35},{35,3},{4,36},{36... | collective-permute-start | bytes 491528 | tf_op jit(solution)/shard_map/ppermute | solution.py:45
  34.4 5.4 %collective-permute-start.1 = (bf16[32,2,320]{2,1,0:T(2,128)(2,1)S(1)}, bf16[32,2,320]{2,1,0:T(2,128)(2,1)S(1)}, u32[]{:S(2)}, u32[]{:S(2)}) collective-permute-start(bf16[32,2,320]{2,1,0:T(2,128)(2,1)S(1)} %broadcast_select_fusion.2), channel_id=1, source_target_pairs={{0,416},{32,128},{128,32},{160,256},{256,160},{288,384},{384,288},... | collective-permute-start | bytes 122888 | tf_op jit(solution)/shard_map/ppermute | solution.py:37
  40.1 17.0 %collective-permute-start.2 = (bf16[32,320]{1,0:T(8,128)(2,1)S(1)}, bf16[32,320]{1,0:T(8,128)(2,1)S(1)}, u32[]{:S(2)}, u32[]{:S(2)}) collective-permute-start(bf16[32,320]{1,0:T(8,128)(2,1)S(1)} %get-tuple-element.8), channel_id=1, source_target_pairs={{0,8},{8,16},{16,24},{24,0},{1,9},{9,17},{17,25},{25,1},{2,10},{10... | collective-permute-start | bytes 61448 | tf_op jit(solution)/shard_map/ppermute | solution.py:37
  43.5 13.6 %collective-permute-start.3 = (bf16[32,320]{1,0:T(8,128)(2,1)S(1)}, bf16[32,320]{1,0:T(8,128)(2,1)S(1)}, u32[]{:S(2)}, u32[]{:S(2)}) collective-permute-start(bf16[32,320]{1,0:T(8,128)(2,1)S(1)} %get-tuple-element.9), channel_id=1, source_target_pairs={{0,24},{8,0},{16,8},{24,16},{1,25},{9,1},{17,9},{25,17},{2,26},{10... | collective-permute-start | bytes 61448 | tf_op jit(solution)/shard_map/ppermute | solution.py:37
  48.0 25.9 %collective-permute-start.5 = (bf16[80,320]{1,0:T(8,128)(2,1)S(1)}, bf16[80,320]{1,0:T(8,128)(2,1)S(1)}, u32[]{:S(2)}, u32[]{:S(2)}) collective-permute-start(bf16[80,320]{1,0:T(8,128)(2,1)S(1)} %fusion.1), channel_id=1, source_target_pairs={{0,68},{1,69},{2,198},{3,199},{4,256},{5,257},{6,386},{7,387},{32,... | collective-permute-start | bytes 153608 | tf_op jit(solution)/shard_map/ppermute | solution.py:37
  51.6 22.3 %collective-permute-start.4 = (bf16[192,320]{1,0:T(8,128)(2,1)}, bf16[192,320]{1,0:T(8,128)(2,1)S(1)}, u32[]{:S(2)}, u32[]{:S(2)}) collective-permute-start(bf16[192,320]{1,0:T(8,128)(2,1)} %bitcast.18), channel_id=1, source_target_pairs={{0,68},{1,69},{2,198},{3,199},{4,256},{5,257},{6,386},{7,387},{32,... | collective-permute-start | bytes 368648 | tf_op jit(solution)/shard_map/ppermute | solution.py:37
  64.2 18.4 %all-to-all-start.2 = ((bf16[16,64,320]{2,1,0:T(8,128)(2,1)}), bf16[16,64,320]{2,1,0:T(8,128)(2,1)S(1)}, u32[]{:S(2)}, u32[]{:S(2)}) async-start(bf16[16,64,320]{2,1,0:T(8,128)(2,1)} %get-tuple-element.11), calls=%async_computation.2 | async-start | bytes 1572864 | tf_op jit(solution)/shard_map/all_to_all | solution.py:41
  74.0 3.4 %collective-permute-start.6 = (bf16[272,320]{1,0:T(8,128)(2,1)S(1)}, bf16[272,320]{1,0:T(8,128)(2,1)S(1)}, u32[]{:S(2)}, u32[]{:S(2)}) collective-permute-start(bf16[272,320]{1,0:T(8,128)(2,1)S(1)} %constant_dynamic-update-slice_fusion), channel_id=1, source_target_pairs={{0,32},{32,0},{1,33},{33,1},{2,34},{34,2},{3,35},{35,3},{4,36},{36... | collective-permute-start | bytes 522248 | tf_op jit(solution)/shard_map/ppermute | solution.py:45
  83.3 3.8 %collective-permute-start.7 = (bf16[1024,256]{1,0:T(8,128)(2,1)S(1)}, bf16[1024,256]{1,0:T(8,128)(2,1)S(1)}, u32[]{:S(2)}, u32[]{:S(2)}) collective-permute-start(bf16[1024,256]{1,0:T(8,128)(2,1)S(1)} %get-tuple-element.13.pair), channel_id=1, source_target_pairs={{0,32},{32,0},{1,33},{33,1},{2,34},{34,2},{3,35},{35,3},{4,36},{36... | collective-permute-start | bytes 1572872 | tf_op jit(solution)/shard_map/ppermute | solution.py:45
  92.2 18.6 %all-to-all-start.3 = ((bf16[32,32,320]{2,1,0:T(8,128)(2,1)}), bf16[32,32,320]{2,1,0:T(8,128)(2,1)S(1)}, u32[]{:S(2)}, u32[]{:S(2)}) async-start(bf16[32,32,320]{2,1,0:T(8,128)(2,1)} %attend.1), calls=%async_computation.3 | async-start | bytes 1572864 | tf_op jit(solution)/shard_map/all_to_all | solution.py:41
  110.8 24.7 %all-to-all-start.1 = ((bf16[16,4,4,320]{3,2,1,0:T(4,128)(2,1)}), bf16[16,4,4,320]{3,2,1,0:T(4,128)(2,1)S(1)}, u32[]{:S(2)}, u32[]{:S(2)}) async-start(bf16[16,4,4,320]{3,2,1,0:T(4,128)(2,1)} %reshape.41), calls=%async_computation.1 | async-start | bytes 393216 | tf_op jit(solution)/shard_map/all_to_all | solution.py:41
  119.3 22.6 %collective-permute-start.8 = (bf16[32,2,320]{2,1,0:T(2,128)(2,1)S(1)}, bf16[32,2,320]{2,1,0:T(2,128)(2,1)S(1)}, u32[]{:S(2)}, u32[]{:S(2)}) collective-permute-start(bf16[32,2,320]{2,1,0:T(2,128)(2,1)S(1)} %sum_heads.1), channel_id=1, source_target_pairs={{0,0},{1,32},{2,64},{3,96},{4,128},{5,160},{6,192},{7,224},{8,8},{... | collective-permute-start | bytes 122888 | tf_op jit(solution)/shard_map/ppermute | solution.py:37

commit v6 on v5

--- a/solution.py
+++ b/solution.py
@@ -51,6 +51,20 @@
 
 def dot_t(left, right):
     return lax.dot_general(left, right, (((1,), (1,)), ((), ())), preferred_element_type=F32)
+
+
+def dense(array):
+    half = array.shape[-2] // 2
+    tail = array[..., 256:C]
+    tail = jnp.concatenate([tail[..., 0:half, :], tail[..., half:, :]], -1)
+    return jnp.concatenate([array[..., 0:128], array[..., 128:256], tail], -2)
+
+
+def undense(array):
+    rows = array.shape[-2] * 2 // 5
+    tail = array[..., 2 * rows :, :]
+    tail = jnp.concatenate([tail[..., 0:64], tail[..., 64:128]], -2)
+    return jnp.concatenate([array[..., 0:rows, :], array[..., rows : 2 * rows, :], tail], -1)
 
 
 def picked(core, first, count, own, other, edge):
@@ -162,7 +176,8 @@
     place = lax.broadcasted_iota(jnp.int32, (256, 256), 1)
     index = lax.broadcasted_iota(jnp.int32, (256, 256), 0)
     source = (((index >> 4) & 7) * 4 + (index & 3)) * 8 + (index >> 7) * 4 + ((index >> 2) & 3)
-    feat_out[...] = dot((place == source).astype(F32).astype(BF), fresh).astype(BF)
+    tiles = dot((place == source).astype(F32).astype(BF), fresh).reshape(16, 16, C)
+    feat_out[...] = dense(tiles).astype(BF)
     for copy in copies:
         copy.wait()
 
@@ -171,7 +186,7 @@
     return pl.pallas_call(
         conv_kernel,
         out_shape=(
-            jax.ShapeDtypeStruct((256, C), BF),
+            jax.ShapeDtypeStruct((16, 40, 128), BF),
             jax.ShapeDtypeStruct((16, 64, C), BF),
         ),
         out_specs=(pl.BlockSpec(memory_space=pltpu.VMEM), pl.BlockSpec(memory_space=pltpu.HBM)),
@@ -255,7 +270,7 @@
             parts = [
                 terms[y * 64 + column * 8 : y * 64 + column * 8 + 8] for y in range(4)
             ]
-            ready[step * 8 + column] = jnp.concatenate(parts, 0).astype(BF)
+            ready[step * 8 + column] = dense(jnp.concatenate(parts, 0)).astype(BF)
         send(step).start()
         return 0
 
@@ -267,9 +282,9 @@
 def attend(query, pair, pair_far, tokens, near, far):
     return pl.pallas_call(
         attend_kernel,
-        out_shape=jax.ShapeDtypeStruct((32, 32, C), BF),
+        out_shape=jax.ShapeDtypeStruct((32, 80, 128), BF),
         out_specs=pl.BlockSpec(memory_space=pltpu.HBM),
-        scratch_shapes=[pltpu.VMEM((32, 32, C), BF), pltpu.SemaphoreType.DMA((4,))],
+        scratch_shapes=[pltpu.VMEM((32, 80, 128), BF), pltpu.SemaphoreType.DMA((4,))],
         cost_estimate=pl.CostEstimate(
             flops=2 * 1024 * 128 * (2 * 2048 + C),
             bytes_accessed=3_000_000,
@@ -281,9 +296,10 @@
 
 
 def sum_kernel(terms, mixed_out):
-    total = terms[0].astype(F32)
+    total = terms[0:2].astype(F32)
     for head in range(1, 16):
-        total = total + terms[head].astype(F32)
+        total = total + terms[2 * head : 2 * head + 2].astype(F32)
+    total = undense(total).reshape(64, C)
     for half in range(2):
         for strip in range(8):
             part = total[half * 32 + strip * 4 : half * 32 + strip * 4 + 4].reshape(2, 2, C)
@@ -304,13 +320,15 @@
 
 
 def copy_kernel(source, target):
-    target[...] = source[...]
+    tiles = undense(source[...].astype(F32))
+    for row in range(4):
+        target[:, row] = tiles[:, row * 4 : row * 4 + 4].astype(BF)
 
 
 def copied(array):
     return pl.pallas_call(
         copy_kernel,
-        out_shape=jax.ShapeDtypeStruct(array.shape, array.dtype),
+        out_shape=jax.ShapeDtypeStruct((16, 4, 4, C), BF),
         compiler_params=pltpu.CompilerParams(vmem_limit_bytes=8 << 20),
         cost_estimate=pl.CostEstimate(flops=0, bytes_accessed=400_000, transcendentals=0),
         name="copied",
@@ -326,22 +344,17 @@
     core = lax.axis_index("c")
     first = core == 0
     core = core.astype(jnp.int32).reshape(1)
-    near = move(qkv_weight.reshape(192, C), ("y", "h", "c", "l"), nearest_plane)
-
     tiles = exchange(latent, DEPTH)
 
     gains = qk_gain.reshape(2, 1, 64)
-    gains = jnp.concatenate(
-        [jnp.pad(gains, ((0, 0), (0, 0), (0, 64))), jnp.pad(gains, ((0, 0), (0, 0), (64, 0)))], 1
-    )
+    gains = jnp.concatenate([jnp.pad(gains, ((0, 0), (0, 0), (0, 64))), jnp.pad(gains, ((0, 0), (0, 0), (64, 0)))], 1)
     gains = jnp.pad(gains.reshape(4, 128), ((0, 12), (0, C - 128)))
-    rest = move(
-        jnp.concatenate([out_weight, gains], 0), ("y", "h", "c", "l"), nearest_plane
-    )
-    near = jnp.concatenate([near, rest], 0)
-    conv_gain = jnp.pad(conv_gain, ((0, 6), (0, 0)))
+    packed = jnp.concatenate([qkv_weight.reshape(192, C), out_weight, gains], 0)
+    near = move(packed, ("y", "h", "c", "l"), nearest_plane)
     far = swap(near)
     near, far = jnp.where(first, near, far), jnp.where(first, far, near)
+
+    conv_gain = jnp.pad(conv_gain, ((0, 6), (0, 0)))
 
     own = tiles.reshape(2, 8, 4, 4, C).transpose(1, 3, 0, 2, 4).reshape(32, 8, C)
     edge = move(
@@ -356,14 +369,14 @@
     feature_tiles, pooled = conv_stack(core, own, other, edge, before, after, conv_weight, conv_gain)
 
     tokens = exchange(pooled, ("x", "y")).reshape(1024, C)
-    features = exchange(feature_tiles.reshape(16, 4, 4, C), DEPTH)
+    features = exchange(feature_tiles, DEPTH)
 
     query, pair = heads(tokens, near, far)
     pair_far = swap(pair)
     features = copied(features)
     terms = attend(query, pair, pair_far, tokens, near, far)
     terms = exchange(terms, PLANE)
-    mixed = sum_heads(terms.reshape(16, 64, C))
+    mixed = sum_heads(terms)
     mixed = move(
         mixed,
         ("y", "h", "c", "x", "l"),

time: 143 us -> 149 us (1.042)
  blocking collectives: 0 us -> 18.8 us
  starting transfers between devices: 69.2 us -> 55.6 us
  Pallas kernels: 13.9 us -> 15.6 us
    ppermute x6 -> x5, waiting for transfers between devices: 10.6 us -> 29.7 us  [move(): return lax.ppermute(array, axes, pairs)]
    all_to_all x0 -> x1, blocking collectives: none -> 18.8 us  [exchange(): return lax.all_to_all(array, axes, split_axis=0, concat_axis=0, tiled=True)]
    all_to_all x4 -> x3, waiting for transfers between devices: 40.6 us -> 22.6 us  [exchange(): return lax.all_to_all(array, axes, split_axis=0, concat_axis=0, tiled=True)]
    all_to_all x4 -> x3, starting transfers between devices: 36.7 us -> 29.2 us  [exchange(): return lax.all_to_all(array, axes, split_axis=0, concat_axis=0, tiled=True)]
    ppermute x6 -> x5, starting transfers between devices: 26.7 us -> 20.5 us  [move(): return lax.ppermute(array, axes, pairs)]
    pallas_call x3, Pallas kernels: 12.8 us -> 14.5 us  [the longest x1 7.73 us: conv_stack(): pl.pallas_call(conv_kernel, out_shape=(jax.ShapeDtypeStruct((16, 40, 128)...]
  transfers between devices with their start and end apart: 13 -> 11, of which waited for: 9 -> 8; matrix products, arithmetic and copies ran while one was open for 2% -> 1% of each run, Pallas kernels for 6% -> 1%
where the time goes in v6:
time: 149 us
  starting transfers between devices  55.6 us (37%)
  waiting for transfers between devices  55.5 us (37%)
  blocking collectives  18.8 us (13%)
  Pallas kernels  15.6 us (10%)
  local copies, waits for them, and re-layouts  1.54 us (1%)
    ppermute x5, waiting for transfers between devices, move(): return lax.ppermute(array, axes, pairs)  29.7 us
    all_to_all x3, starting transfers between devices, exchange(): return lax.all_to_all(array, axes, split_axis=0, concat_axis=0, tiled=True)  29.2 us
    all_to_all x3, waiting for transfers between devices, exchange(): return lax.all_to_all(array, axes, split_axis=0, concat_axis=0, tiled=True)  22.6 us
    ppermute x5, starting transfers between devices, move(): return lax.ppermute(array, axes, pairs)  20.5 us
    all_to_all x1, blocking collectives, exchange(): return lax.all_to_all(array, axes, split_axis=0, concat_axis=0, tiled=True)  18.8 us
    pallas_call x1, Pallas kernels, conv_stack(): pl.pallas_call(conv_kernel, out_shape=(jax.ShapeDtypeStruct((16, 40, 128)...  7.73 us
    pallas_call x1, Pallas kernels, attend(): pl.pallas_call(attend_kernel, out_shape=jax.ShapeDtypeStruct((32, 80, 128...  5.97 us
    ppermute x3, starting transfers between devices, swap(): return lax.ppermute(array, 'c', [(0, 1), (1, 0)])  5.87 us
  transfers between devices with their start and end apart: 11, of which 8 were waited for; matrix products, arithmetic and copies ran while one was open for 1% of the time, Pallas kernels for 1%

profile of v6, /device:TPU:16, one launch (start us, length us, event | category | flops | bytes accessed | tf_op | source)
XLA Modules:
  0.0 148.8 jit_solution(11331498714376928682)
XLA Ops:
  0.6 15.2 %all-to-all-start = ((bf16[16,4,4,320]{3,2,1,0:T(4,128)(2,1)}), bf16[16,4,4,320]{3,2,1,0:T(4,128)(2,1)S(1)}, u32[]{:S(2)}, u32[]{:S(2)}) async-start(bf16[16,4,4,320]{3,2,1,0:T(4,128)(2,1)} %param.6), calls=%async_computation | async-start | bytes 393216 | tf_op jit(solution)/shard_map/all_to_all | solution.py:41
  15.9 16.4 %all-to-all-done = bf16[16,4,4,320]{3,2,1,0:T(4,128)(2,1)S(1)} async-done(((bf16[16,4,4,320]{3,2,1,0:T(4,128)(2,1)}), bf16[16,4,4,320]{3,2,1,0:T(4,128)(2,1)S(1)}, u32[]{:S(2)}, u32[]{:S(2)}) %all-to-all-start) | async-done | bytes 163872 | tf_op jit(solution)/shard_map/all_to_all | solution.py:41
  32.2 0.1 copy.11
  32.3 0.1 reshape.33.own
  32.4 1.9 %collective-permute-start = (bf16[32,8,320]{2,1,0:T(8,128)(2,1)S(1)}, bf16[32,8,320]{2,1,0:T(8,128)(2,1)S(1)}, u32[]{:S(2)}, u32[]{:S(2)}) collective-permute-start(bf16[32,8,320]{2,1,0:T(8,128)(2,1)S(1)} %reshape.33.own), channel_id=1, source_target_pairs={{0,32},{32,0},{1,33},{33,1},{2,34},{34,2},{3,35},{35,3},{4,36},{36... | collective-permute-start | bytes 491528 | tf_op jit(solution)/shard_map/ppermute | solution.py:45
  34.3 0.1 broadcast_select_fusion.2
  34.4 2.5 %collective-permute-start.1 = (bf16[32,2,320]{2,1,0:T(2,128)(2,1)S(1)}, bf16[32,2,320]{2,1,0:T(2,128)(2,1)S(1)}, u32[]{:S(2)}, u32[]{:S(2)}) collective-permute-start(bf16[32,2,320]{2,1,0:T(2,128)(2,1)S(1)} %broadcast_select_fusion.2), channel_id=1, source_target_pairs={{0,416},{32,128},{128,32},{160,256},{256,160},{288,384},{384,288},... | collective-permute-start | bytes 122888 | tf_op jit(solution)/shard_map/ppermute | solution.py:37
  36.9 2.9 %collective-permute-done.1 = bf16[32,2,320]{2,1,0:T(2,128)(2,1)S(1)} collective-permute-done((bf16[32,2,320]{2,1,0:T(2,128)(2,1)S(1)}, bf16[32,2,320]{2,1,0:T(2,128)(2,1)S(1)}, u32[]{:S(2)}, u32[]{:S(2)}) %collective-permute-start.1) | collective-permute-done | bytes 40992 | tf_op jit(solution)/shard_map/ppermute | solution.py:37
  39.9 0.0 collective-permute-done.other
  39.9 0.2 border.1
  40.1 0.0 copy-start
  40.2 0.0 copy-start.1
  40.2 3.5 %collective-permute-start.2 = (bf16[32,320]{1,0:T(8,128)(2,1)S(1)}, bf16[32,320]{1,0:T(8,128)(2,1)S(1)}, u32[]{:S(2)}, u32[]{:S(2)}) collective-permute-start(bf16[32,320]{1,0:T(8,128)(2,1)S(1)} %get-tuple-element.8), channel_id=1, source_target_pairs={{0,8},{8,16},{16,24},{24,0},{1,9},{9,17},{17,25},{25,1},{2,10},{10... | collective-permute-start | bytes 61448 | tf_op jit(solution)/shard_map/ppermute | solution.py:37
  43.7 3.7 %collective-permute-start.3 = (bf16[32,320]{1,0:T(8,128)(2,1)S(1)}, bf16[32,320]{1,0:T(8,128)(2,1)S(1)}, u32[]{:S(2)}, u32[]{:S(2)}) collective-permute-start(bf16[32,320]{1,0:T(8,128)(2,1)S(1)} %get-tuple-element.9), channel_id=1, source_target_pairs={{0,24},{8,0},{16,8},{24,16},{1,25},{9,1},{17,9},{25,17},{2,26},{10... | collective-permute-start | bytes 61448 | tf_op jit(solution)/shard_map/ppermute | solution.py:37
  47.4 0.8 fusion.2
  48.2 0.7 pad.16.gains
  48.9 0.0 collective-permute-done.2.before
  48.9 0.6 collective-permute-done.3.after
  49.4 7.7 %conv_stack.1 = (bf16[16,40,128]{2,1,0:T(8,128)(2,1)}, bf16[16,64,320]{2,1,0:T(8,128)(2,1)}) custom-call(s32[1]{0:T(128)} %bitcast.core, bf16[32,8,320]{2,1,0:T(8,128)(2,1)S(1)} %reshape.33.own, bf16[32,8,320]{2,1,0:T(8,128)(2,1)S(1)} %collective-permute-done.other, bf16[64,320]{1,0:T(8,128)(2,1)S(1)} %reshape.34.edge, ...), custom_call_target="tpu_custom_call" | custom-call | flops 1946419200 | bytes 5000000 | tf_op jit(solution)/shard_map/conv_stack/pallas_call | solution.py:186
  57.2 7.2 %all-to-all-start.2 = ((bf16[16,64,320]{2,1,0:T(8,128)(2,1)}), bf16[16,64,320]{2,1,0:T(8,128)(2,1)S(1)}, u32[]{:S(2)}, u32[]{:S(2)}) async-start(bf16[16,64,320]{2,1,0:T(8,128)(2,1)} %get-tuple-element.11), calls=%async_computation.2 | async-start | bytes 1572864 | tf_op jit(solution)/shard_map/all_to_all | solution.py:41
  64.4 0.0 copy-done
  64.4 0.0 copy-done.1
  64.4 2.0 %collective-permute-start.4 = (bf16[272,320]{1,0:T(8,128)(2,1)S(1)}, bf16[272,320]{1,0:T(8,128)(2,1)S(1)}, u32[]{:S(2)}, u32[]{:S(2)}) collective-permute-start(bf16[272,320]{1,0:T(8,128)(2,1)S(1)} %fusion.1), channel_id=1, source_target_pairs={{0,68},{1,69},{2,198},{3,199},{4,256},{5,257},{6,386},{7,387},{32,... | collective-permute-start | bytes 522248 | tf_op jit(solution)/shard_map/ppermute | solution.py:37
  66.5 21.1 %collective-permute-done.4 = bf16[272,320]{1,0:T(8,128)(2,1)S(1)} collective-permute-done((bf16[272,320]{1,0:T(8,128)(2,1)S(1)}, bf16[272,320]{1,0:T(8,128)(2,1)S(1)}, u32[]{:S(2)}, u32[]{:S(2)}) %collective-permute-start.4) | collective-permute-done | bytes 174112 | tf_op jit(solution)/shard_map/ppermute | solution.py:37
  87.5 1.9 %collective-permute-start.5 = (bf16[272,320]{1,0:T(8,128)(2,1)S(1)}, bf16[272,320]{1,0:T(8,128)(2,1)S(1)}, u32[]{:S(2)}, u32[]{:S(2)}) collective-permute-start(bf16[272,320]{1,0:T(8,128)(2,1)S(1)} %collective-permute-done.4), channel_id=1, source_target_pairs={{0,32},{32,0},{1,33},{33,1},{2,34},{34,2},{3,35},{35,3},{4,36},{36... | collective-permute-start | bytes 522248 | tf_op jit(solution)/shard_map/ppermute | solution.py:45
  89.4 1.4 collective-permute-done.5
  90.9 0.0 all-to-all-done.2
  90.9 0.8 heads.1
  91.7 2.0 %collective-permute-start.6 = (bf16[1024,256]{1,0:T(8,128)(2,1)S(1)}, bf16[1024,256]{1,0:T(8,128)(2,1)S(1)}, u32[]{:S(2)}, u32[]{:S(2)}) collective-permute-start(bf16[1024,256]{1,0:T(8,128)(2,1)S(1)} %get-tuple-element.13.pair), channel_id=1, source_target_pairs={{0,32},{32,0},{1,33},{33,1},{2,34},{34,2},{3,35},{35,3},{4,36},{36... | collective-permute-start | bytes 1572872 | tf_op jit(solution)/shard_map/ppermute | solution.py:45
  93.7 1.8 %collective-permute-done.6.pair_far = bf16[1024,256]{1,0:T(8,128)(2,1)S(1)} collective-permute-done((bf16[1024,256]{1,0:T(8,128)(2,1)S(1)}, bf16[1024,256]{1,0:T(8,128)(2,1)S(1)}, u32[]{:S(2)}, u32[]{:S(2)}) %collective-permute-start.6) | collective-permute-done | bytes 524320 | tf_op jit(solution)/shard_map/ppermute | solution.py:45
  95.5 6.0 %attend.1 = bf16[32,80,128]{2,1,0:T(8,128)(2,1)S(1)} custom-call(bf16[1024,128]{1,0:T(8,128)(2,1)S(1)} %get-tuple-element.12.query, bf16[1024,256]{1,0:T(8,128)(2,1)S(1)} %get-tuple-element.13.pair, bf16[1024,256]{1,0:T(8,128)(2,1)S(1)} %collective-permute-done.6.pair_far, bf16[1024,320]{1,0:T(8,128)(2,1)S(1)} %bitcast.11, ...), custom_call_target="tpu_custom_call" | custom-call | flops 1157627904 | bytes 3000000 | tf_op jit(solution)/shard_map/attend/pallas_call | solution.py:283
  101.5 18.8 %all_to_all.20.terms = bf16[32,80,128]{2,1,0:T(8,128)(2,1)S(1)} all-to-all(bf16[32,80,128]{2,1,0:T(8,128)(2,1)S(1)} %attend.1), channel_id=1, replica_groups=mesh['y'=4,'h'=2,'c'=2,'x'=4,'l'=8] {'x','y','c'}, dimensions={0} | all-to-all | bytes 1310720 | tf_op jit(solution)/shard_map/all_to_all | solution.py:41
  120.3 6.7 %all-to-all-start.1 = ((bf16[16,40,128]{2,1,0:T(8,128)(2,1)}), bf16[16,40,128]{2,1,0:T(8,128)(2,1)S(1)}, u32[]{:S(2)}, u32[]{:S(2)}) async-start(bf16[16,40,128]{2,1,0:T(8,128)(2,1)} %get-tuple-element.10), calls=%async_computation.1 | async-start | bytes 327680 | tf_op jit(solution)/shard_map/all_to_all | solution.py:41
  127.0 0.1 sum_heads.1
  127.2 8.9 %collective-permute-start.7 = (bf16[32,2,320]{2,1,0:T(2,128)(2,1)S(1)}, bf16[32,2,320]{2,1,0:T(2,128)(2,1)S(1)}, u32[]{:S(2)}, u32[]{:S(2)}) collective-permute-start(bf16[32,2,320]{2,1,0:T(2,128)(2,1)S(1)} %sum_heads.1), channel_id=1, source_target_pairs={{0,0},{1,32},{2,64},{3,96},{4,128},{5,160},{6,192},{7,224},{8,8},{... | collective-permute-start | bytes 122888 | tf_op jit(solution)/shard_map/ppermute | solution.py:37
  136.0 6.2 %all-to-all-done.1.source = bf16[16,40,128]{2,1,0:T(8,128)(2,1)S(1)} async-done(((bf16[16,40,128]{2,1,0:T(8,128)(2,1)}), bf16[16,40,128]{2,1,0:T(8,128)(2,1)S(1)}, u32[]{:S(2)}, u32[]{:S(2)}) %all-to-all-start.1) | async-done | bytes 163872 | tf_op jit(solution)/shard_map/all_to_all | solution.py:41
  142.3 0.8 copied.1
  143.1 5.1 %collective-permute-done.7 = bf16[32,2,320]{2,1,0:T(2,128)(2,1)S(1)} collective-permute-done((bf16[32,2,320]{2,1,0:T(2,128)(2,1)S(1)}, bf16[32,2,320]{2,1,0:T(2,128)(2,1)S(1)}, u32[]{:S(2)}, u32[]{:S(2)}) %collective-permute-start.7) | collective-permute-done | bytes 40992 | tf_op jit(solution)/shard_map/ppermute | solution.py:37
  148.2 0.6 copy.13
  (4 shorter events, 0.1 us)
Async XLA Ops:
  0.6 31.6 %all-to-all-start = ((bf16[16,4,4,320]{3,2,1,0:T(4,128)(2,1)}), bf16[16,4,4,320]{3,2,1,0:T(4,128)(2,1)S(1)}, u32[]{:S(2)}, u32[]{:S(2)}) async-start(bf16[16,4,4,320]{3,2,1,0:T(4,128)(2,1)} %param.6), calls=%async_computation | async-start | bytes 393216 | tf_op jit(solution)/shard_map/all_to_all | solution.py:41
  32.4 7.5 %collective-permute-start = (bf16[32,8,320]{2,1,0:T(8,128)(2,1)S(1)}, bf16[32,8,320]{2,1,0:T(8,128)(2,1)S(1)}, u32[]{:S(2)}, u32[]{:S(2)}) collective-permute-start(bf16[32,8,320]{2,1,0:T(8,128)(2,1)S(1)} %reshape.33.own), channel_id=1, source_target_pairs={{0,32},{32,0},{1,33},{33,1},{2,34},{34,2},{3,35},{35,3},{4,36},{36... | collective-permute-start | bytes 491528 | tf_op jit(solution)/shard_map/ppermute | solution.py:45
  34.4 5.4 %collective-permute-start.1 = (bf16[32,2,320]{2,1,0:T(2,128)(2,1)S(1)}, bf16[32,2,320]{2,1,0:T(2,128)(2,1)S(1)}, u32[]{:S(2)}, u32[]{:S(2)}) collective-permute-start(bf16[32,2,320]{2,1,0:T(2,128)(2,1)S(1)} %broadcast_select_fusion.2), channel_id=1, source_target_pairs={{0,416},{32,128},{128,32},{160,256},{256,160},{288,384},{384,288},... | collective-permute-start | bytes 122888 | tf_op jit(solution)/shard_map/ppermute | solution.py:37
  40.1 24.2 %copy-start = (bf16[3,64,320]{2,1,0:T(8,128)(2,1)S(1)}, bf16[3,64,320]{2,1,0:T(8,128)(2,1)}, u32[]{:S(2)}) copy-start(bf16[3,64,320]{2,1,0:T(8,128)(2,1)} %param.9) | copy-start | bytes 368644
  40.2 24.2 %copy-start.1 = (bf16[64,320]{1,0:T(8,128)(2,1)S(1)}, bf16[64,320]{1,0:T(8,128)(2,1)}, u32[]{:S(2)}) copy-start(bf16[64,320]{1,0:T(8,128)(2,1)} %param.11) | copy-start | bytes 122884
  40.2 8.7 %collective-permute-start.2 = (bf16[32,320]{1,0:T(8,128)(2,1)S(1)}, bf16[32,320]{1,0:T(8,128)(2,1)S(1)}, u32[]{:S(2)}, u32[]{:S(2)}) collective-permute-start(bf16[32,320]{1,0:T(8,128)(2,1)S(1)} %get-tuple-element.8), channel_id=1, source_target_pairs={{0,8},{8,16},{16,24},{24,0},{1,9},{9,17},{17,25},{25,1},{2,10},{10... | collective-permute-start | bytes 61448 | tf_op jit(solution)/shard_map/ppermute | solution.py:37
  43.7 5.7 %collective-permute-start.3 = (bf16[32,320]{1,0:T(8,128)(2,1)S(1)}, bf16[32,320]{1,0:T(8,128)(2,1)S(1)}, u32[]{:S(2)}, u32[]{:S(2)}) collective-permute-start(bf16[32,320]{1,0:T(8,128)(2,1)S(1)} %get-tuple-element.9), channel_id=1, source_target_pairs={{0,24},{8,0},{16,8},{24,16},{1,25},{9,1},{17,9},{25,17},{2,26},{10... | collective-permute-start | bytes 61448 | tf_op jit(solution)/shard_map/ppermute | solution.py:37
  57.2 33.8 %all-to-all-start.2 = ((bf16[16,64,320]{2,1,0:T(8,128)(2,1)}), bf16[16,64,320]{2,1,0:T(8,128)(2,1)S(1)}, u32[]{:S(2)}, u32[]{:S(2)}) async-start(bf16[16,64,320]{2,1,0:T(8,128)(2,1)} %get-tuple-element.11), calls=%async_computation.2 | async-start | bytes 1572864 | tf_op jit(solution)/shard_map/all_to_all | solution.py:41
  64.4 23.1 %collective-permute-start.4 = (bf16[272,320]{1,0:T(8,128)(2,1)S(1)}, bf16[272,320]{1,0:T(8,128)(2,1)S(1)}, u32[]{:S(2)}, u32[]{:S(2)}) collective-permute-start(bf16[272,320]{1,0:T(8,128)(2,1)S(1)} %fusion.1), channel_id=1, source_target_pairs={{0,68},{1,69},{2,198},{3,199},{4,256},{5,257},{6,386},{7,387},{32,... | collective-permute-start | bytes 522248 | tf_op jit(solution)/shard_map/ppermute | solution.py:37
  87.5 3.3 %collective-permute-start.5 = (bf16[272,320]{1,0:T(8,128)(2,1)S(1)}, bf16[272,320]{1,0:T(8,128)(2,1)S(1)}, u32[]{:S(2)}, u32[]{:S(2)}) collective-permute-start(bf16[272,320]{1,0:T(8,128)(2,1)S(1)} %collective-permute-done.4), channel_id=1, source_target_pairs={{0,32},{32,0},{1,33},{33,1},{2,34},{34,2},{3,35},{35,3},{4,36},{36... | collective-permute-start | bytes 522248 | tf_op jit(solution)/shard_map/ppermute | solution.py:45
  91.7 3.8 %collective-permute-start.6 = (bf16[1024,256]{1,0:T(8,128)(2,1)S(1)}, bf16[1024,256]{1,0:T(8,128)(2,1)S(1)}, u32[]{:S(2)}, u32[]{:S(2)}) collective-permute-start(bf16[1024,256]{1,0:T(8,128)(2,1)S(1)} %get-tuple-element.13.pair), channel_id=1, source_target_pairs={{0,32},{32,0},{1,33},{33,1},{2,34},{34,2},{3,35},{35,3},{4,36},{36... | collective-permute-start | bytes 1572872 | tf_op jit(solution)/shard_map/ppermute | solution.py:45
  120.3 22.0 %all-to-all-start.1 = ((bf16[16,40,128]{2,1,0:T(8,128)(2,1)}), bf16[16,40,128]{2,1,0:T(8,128)(2,1)S(1)}, u32[]{:S(2)}, u32[]{:S(2)}) async-start(bf16[16,40,128]{2,1,0:T(8,128)(2,1)} %get-tuple-element.10), calls=%async_computation.1 | async-start | bytes 327680 | tf_op jit(solution)/shard_map/all_to_all | solution.py:41
  127.2 21.0 %collective-permute-start.7 = (bf16[32,2,320]{2,1,0:T(2,128)(2,1)S(1)}, bf16[32,2,320]{2,1,0:T(2,128)(2,1)S(1)}, u32[]{:S(2)}, u32[]{:S(2)}) collective-permute-start(bf16[32,2,320]{2,1,0:T(2,128)(2,1)S(1)} %sum_heads.1), channel_id=1, source_target_pairs={{0,0},{1,32},{2,64},{3,96},{4,128},{5,160},{6,192},{7,224},{8,8},{... | collective-permute-start | bytes 122888 | tf_op jit(solution)/shard_map/ppermute | solution.py:37

commit v7 on v6

--- a/solution.py
+++ b/solution.py
@@ -173,11 +173,7 @@
     copies = [pltpu.make_async_copy(pool, pool_out.at[slot], sent.at[slot]) for slot in range(16)]
     for copy in copies:
         copy.start()
-    place = lax.broadcasted_iota(jnp.int32, (256, 256), 1)
-    index = lax.broadcasted_iota(jnp.int32, (256, 256), 0)
-    source = (((index >> 4) & 7) * 4 + (index & 3)) * 8 + (index >> 7) * 4 + ((index >> 2) & 3)
-    tiles = dot((place == source).astype(F32).astype(BF), fresh).reshape(16, 16, C)
-    feat_out[...] = dense(tiles).astype(BF)
+    feat_out[...] = fresh
     for copy in copies:
         copy.wait()
 
@@ -186,7 +182,7 @@
     return pl.pallas_call(
         conv_kernel,
         out_shape=(
-            jax.ShapeDtypeStruct((16, 40, 128), BF),
+            jax.ShapeDtypeStruct((256, C), BF),
             jax.ShapeDtypeStruct((16, 64, C), BF),
         ),
         out_specs=(pl.BlockSpec(memory_space=pltpu.VMEM), pl.BlockSpec(memory_space=pltpu.HBM)),
@@ -209,6 +205,26 @@
         compiler_params=pltpu.CompilerParams(vmem_limit_bytes=52 << 20),
         name="conv_stack",
     )(core, own, other, edge, before, after, gains, kernels)
+
+
+def tiled_kernel(fresh, feat_out):
+    place = lax.broadcasted_iota(jnp.int32, (256, 256), 1)
+    index = lax.broadcasted_iota(jnp.int32, (256, 256), 0)
+    source = (((index >> 4) & 7) * 4 + (index & 3)) * 8 + (index >> 7) * 4 + ((index >> 2) & 3)
+    tiles = dot((place == source).astype(F32).astype(BF), fresh[...]).reshape(16, 16, C)
+    feat_out[...] = dense(tiles).astype(BF)
+
+
+def tiled(fresh):
+    return pl.pallas_call(
+        tiled_kernel,
+        out_shape=jax.ShapeDtypeStruct((16, 40, 128), BF),
+        compiler_params=pltpu.CompilerParams(vmem_limit_bytes=8 << 20),
+        cost_estimate=pl.CostEstimate(
+            flops=2 * 256 * 256 * C, bytes_accessed=400_000, transcendentals=0
+        ),
+        name="tiled",
+    )(fresh)
 
 
 def norm(projected, gain):
@@ -366,9 +382,10 @@
     before = move(right, ("x",), lambda x: (x + 1,))
     after = move(left, ("x",), lambda x: (x - 1,))
 
-    feature_tiles, pooled = conv_stack(core, own, other, edge, before, after, conv_weight, conv_gain)
+    fresh, pooled = conv_stack(core, own, other, edge, before, after, conv_weight, conv_gain)
 
     tokens = exchange(pooled, ("x", "y")).reshape(1024, C)
+    feature_tiles = tiled(fresh)
     features = exchange(feature_tiles, DEPTH)
 
     query, pair = heads(tokens, near, far)

time: 149 us -> 148 us (level)
  blocking collectives: 18.8 us -> 0 us
  waiting for transfers between devices: 55.5 us -> 65.6 us
  starting transfers between devices: 55.6 us -> 63.5 us
    all_to_all x1 -> x0, blocking collectives: 18.8 us -> none  [exchange(): return lax.all_to_all(array, axes, split_axis=0, concat_axis=0, tiled=True)]
    all_to_all x3 -> x4, waiting for transfers between devices: 22.6 us -> 32.7 us  [exchange(): return lax.all_to_all(array, axes, split_axis=0, concat_axis=0, tiled=True)]
    all_to_all x3 -> x4, starting transfers between devices: 29.2 us -> 37.1 us  [exchange(): return lax.all_to_all(array, axes, split_axis=0, concat_axis=0, tiled=True)]
    pallas_call x1 -> x2, Pallas kernels: 7.73 us -> 7.8 us  [the longest x1 6.86 us: conv_stack(): pl.pallas_call(conv_kernel, out_shape=(jax.ShapeDtypeStruct((256, C), BF)...]
  transfers between devices with their start and end apart: 11 -> 12, of which waited for: 8 -> 9; matrix products, arithmetic and copies ran while one was open for 1% -> 1% of each run, Pallas kernels for 1% -> 1%
where the time goes in v7:
time: 148 us; the launch traced here: 147 us
  waiting for transfers between devices  65.6 us (44%)
  starting transfers between devices  63.5 us (43%)
  Pallas kernels  14.8 us (10%)
  local copies, waits for them, and re-layouts  1.54 us (1%)
    all_to_all x4, starting transfers between devices, exchange(): return lax.all_to_all(array, axes, split_axis=0, concat_axis=0, tiled=True)  37.1 us
    all_to_all x4, waiting for transfers between devices, exchange(): return lax.all_to_all(array, axes, split_axis=0, concat_axis=0, tiled=True)  32.7 us
    ppermute x5, waiting for transfers between devices, move(): return lax.ppermute(array, axes, pairs)  29.7 us
    ppermute x5, starting transfers between devices, move(): return lax.ppermute(array, axes, pairs)  20.5 us
    pallas_call x1, Pallas kernels, conv_stack(): pl.pallas_call(conv_kernel, out_shape=(jax.ShapeDtypeStruct((256, C), BF)...  6.86 us
    ppermute x3, starting transfers between devices, swap(): return lax.ppermute(array, 'c', [(0, 1), (1, 0)])  5.88 us
    pallas_call x1, Pallas kernels, attend(): pl.pallas_call(attend_kernel, out_shape=jax.ShapeDtypeStruct((32, 80, 128...  5.11 us
    ppermute x3, waiting for transfers between devices, swap(): return lax.ppermute(array, 'c', [(0, 1), (1, 0)])  3.18 us
  transfers between devices with their start and end apart: 12, of which 9 were waited for; matrix products, arithmetic and copies ran while one was open for 1% of the time, Pallas kernels for 1%

profile of v7, /device:TPU:16, one launch (start us, length us, event | category | flops | bytes accessed | tf_op | source)
XLA Modules:
  0.0 147.3 jit_solution(762897396696883304)
XLA Ops:
  0.6 15.2 %all-to-all-start = ((bf16[16,4,4,320]{3,2,1,0:T(4,128)(2,1)}), bf16[16,4,4,320]{3,2,1,0:T(4,128)(2,1)S(1)}, u32[]{:S(2)}, u32[]{:S(2)}) async-start(bf16[16,4,4,320]{3,2,1,0:T(4,128)(2,1)} %param.6), calls=%async_computation | async-start | bytes 393216 | tf_op jit(solution)/shard_map/all_to_all | solution.py:41
  15.9 16.4 %all-to-all-done = bf16[16,4,4,320]{3,2,1,0:T(4,128)(2,1)S(1)} async-done(((bf16[16,4,4,320]{3,2,1,0:T(4,128)(2,1)}), bf16[16,4,4,320]{3,2,1,0:T(4,128)(2,1)S(1)}, u32[]{:S(2)}, u32[]{:S(2)}) %all-to-all-start) | async-done | bytes 163872 | tf_op jit(solution)/shard_map/all_to_all | solution.py:41
  32.2 0.1 copy.11
  32.3 0.1 reshape.33.own
  32.4 1.9 %collective-permute-start = (bf16[32,8,320]{2,1,0:T(8,128)(2,1)S(1)}, bf16[32,8,320]{2,1,0:T(8,128)(2,1)S(1)}, u32[]{:S(2)}, u32[]{:S(2)}) collective-permute-start(bf16[32,8,320]{2,1,0:T(8,128)(2,1)S(1)} %reshape.33.own), channel_id=1, source_target_pairs={{0,32},{32,0},{1,33},{33,1},{2,34},{34,2},{3,35},{35,3},{4,36},{36... | collective-permute-start | bytes 491528 | tf_op jit(solution)/shard_map/ppermute | solution.py:45
  34.3 0.1 broadcast_select_fusion.2
  34.4 2.5 %collective-permute-start.1 = (bf16[32,2,320]{2,1,0:T(2,128)(2,1)S(1)}, bf16[32,2,320]{2,1,0:T(2,128)(2,1)S(1)}, u32[]{:S(2)}, u32[]{:S(2)}) collective-permute-start(bf16[32,2,320]{2,1,0:T(2,128)(2,1)S(1)} %broadcast_select_fusion.2), channel_id=1, source_target_pairs={{0,416},{32,128},{128,32},{160,256},{256,160},{288,384},{384,288},... | collective-permute-start | bytes 122888 | tf_op jit(solution)/shard_map/ppermute | solution.py:37
  36.9 2.9 %collective-permute-done.1 = bf16[32,2,320]{2,1,0:T(2,128)(2,1)S(1)} collective-permute-done((bf16[32,2,320]{2,1,0:T(2,128)(2,1)S(1)}, bf16[32,2,320]{2,1,0:T(2,128)(2,1)S(1)}, u32[]{:S(2)}, u32[]{:S(2)}) %collective-permute-start.1) | collective-permute-done | bytes 40992 | tf_op jit(solution)/shard_map/ppermute | solution.py:37
  39.9 0.0 collective-permute-done.other
  39.9 0.2 border.1
  40.1 0.0 copy-start
  40.2 0.0 copy-start.1
  40.2 3.5 %collective-permute-start.2 = (bf16[32,320]{1,0:T(8,128)(2,1)S(1)}, bf16[32,320]{1,0:T(8,128)(2,1)S(1)}, u32[]{:S(2)}, u32[]{:S(2)}) collective-permute-start(bf16[32,320]{1,0:T(8,128)(2,1)S(1)} %get-tuple-element.8), channel_id=1, source_target_pairs={{0,8},{8,16},{16,24},{24,0},{1,9},{9,17},{17,25},{25,1},{2,10},{10... | collective-permute-start | bytes 61448 | tf_op jit(solution)/shard_map/ppermute | solution.py:37
  43.7 3.7 %collective-permute-start.3 = (bf16[32,320]{1,0:T(8,128)(2,1)S(1)}, bf16[32,320]{1,0:T(8,128)(2,1)S(1)}, u32[]{:S(2)}, u32[]{:S(2)}) collective-permute-start(bf16[32,320]{1,0:T(8,128)(2,1)S(1)} %get-tuple-element.9), channel_id=1, source_target_pairs={{0,24},{8,0},{16,8},{24,16},{1,25},{9,1},{17,9},{25,17},{2,26},{10... | collective-permute-start | bytes 61448 | tf_op jit(solution)/shard_map/ppermute | solution.py:37
  47.4 0.8 fusion.2
  48.2 0.7 pad.16.gains
  48.9 0.0 collective-permute-done.2.before
  48.9 0.6 collective-permute-done.3.after
  49.4 6.9 %conv_stack.1 = (bf16[256,320]{1,0:T(8,128)(2,1)S(1)}, bf16[16,64,320]{2,1,0:T(8,128)(2,1)}) custom-call(s32[1]{0:T(128)} %bitcast.core, bf16[32,8,320]{2,1,0:T(8,128)(2,1)S(1)} %reshape.33.own, bf16[32,8,320]{2,1,0:T(8,128)(2,1)S(1)} %collective-permute-done.other, bf16[64,320]{1,0:T(8,128)(2,1)S(1)} %reshape.34.edge, ...), custom_call_target="tpu_custom_call" | custom-call | flops 1946419200 | bytes 5000000 | tf_op jit(solution)/shard_map/conv_stack/pallas_call | solution.py:182
  56.3 7.2 %all-to-all-start.2 = ((bf16[16,64,320]{2,1,0:T(8,128)(2,1)}), bf16[16,64,320]{2,1,0:T(8,128)(2,1)S(1)}, u32[]{:S(2)}, u32[]{:S(2)}) async-start(bf16[16,64,320]{2,1,0:T(8,128)(2,1)} %get-tuple-element.11), calls=%async_computation.2 | async-start | bytes 1572864 | tf_op jit(solution)/shard_map/all_to_all | solution.py:41
  63.5 0.0 copy-done
  63.5 0.0 copy-done.1
  63.6 2.0 %collective-permute-start.4 = (bf16[272,320]{1,0:T(8,128)(2,1)S(1)}, bf16[272,320]{1,0:T(8,128)(2,1)S(1)}, u32[]{:S(2)}, u32[]{:S(2)}) collective-permute-start(bf16[272,320]{1,0:T(8,128)(2,1)S(1)} %fusion.1), channel_id=1, source_target_pairs={{0,68},{1,69},{2,198},{3,199},{4,256},{5,257},{6,386},{7,387},{32,... | collective-permute-start | bytes 522248 | tf_op jit(solution)/shard_map/ppermute | solution.py:37
  65.6 21.1 %collective-permute-done.4 = bf16[272,320]{1,0:T(8,128)(2,1)S(1)} collective-permute-done((bf16[272,320]{1,0:T(8,128)(2,1)S(1)}, bf16[272,320]{1,0:T(8,128)(2,1)S(1)}, u32[]{:S(2)}, u32[]{:S(2)}) %collective-permute-start.4) | collective-permute-done | bytes 174112 | tf_op jit(solution)/shard_map/ppermute | solution.py:37
  86.7 1.9 %collective-permute-start.5 = (bf16[272,320]{1,0:T(8,128)(2,1)S(1)}, bf16[272,320]{1,0:T(8,128)(2,1)S(1)}, u32[]{:S(2)}, u32[]{:S(2)}) collective-permute-start(bf16[272,320]{1,0:T(8,128)(2,1)S(1)} %collective-permute-done.4), channel_id=1, source_target_pairs={{0,32},{32,0},{1,33},{33,1},{2,34},{34,2},{3,35},{35,3},{4,36},{36... | collective-permute-start | bytes 522248 | tf_op jit(solution)/shard_map/ppermute | solution.py:45
  88.6 1.4 collective-permute-done.5
  90.1 0.0 all-to-all-done.2
  90.1 0.8 heads.1
  90.8 2.0 %collective-permute-start.6 = (bf16[1024,256]{1,0:T(8,128)(2,1)S(1)}, bf16[1024,256]{1,0:T(8,128)(2,1)S(1)}, u32[]{:S(2)}, u32[]{:S(2)}) collective-permute-start(bf16[1024,256]{1,0:T(8,128)(2,1)S(1)} %get-tuple-element.13.pair), channel_id=1, source_target_pairs={{0,32},{32,0},{1,33},{33,1},{2,34},{34,2},{3,35},{35,3},{4,36},{36... | collective-permute-start | bytes 1572872 | tf_op jit(solution)/shard_map/ppermute | solution.py:45
  92.9 1.7 %collective-permute-done.6.pair_far = bf16[1024,256]{1,0:T(8,128)(2,1)S(1)} collective-permute-done((bf16[1024,256]{1,0:T(8,128)(2,1)S(1)}, bf16[1024,256]{1,0:T(8,128)(2,1)S(1)}, u32[]{:S(2)}, u32[]{:S(2)}) %collective-permute-start.6) | collective-permute-done | bytes 524320 | tf_op jit(solution)/shard_map/ppermute | solution.py:45
  94.6 5.1 %attend.1 = bf16[32,80,128]{2,1,0:T(8,128)(2,1)} custom-call(bf16[1024,128]{1,0:T(8,128)(2,1)S(1)} %get-tuple-element.12.query, bf16[1024,256]{1,0:T(8,128)(2,1)S(1)} %get-tuple-element.13.pair, bf16[1024,256]{1,0:T(8,128)(2,1)S(1)} %collective-permute-done.6.pair_far, bf16[1024,320]{1,0:T(8,128)(2,1)S(1)} %bitcast.11, ...), custom_call_target="tpu_custom_call" | custom-call | flops 1157627904 | bytes 3000000 | tf_op jit(solution)/shard_map/attend/pallas_call | solution.py:299
  99.8 8.0 %all-to-all-start.3 = ((bf16[32,80,128]{2,1,0:T(8,128)(2,1)}), bf16[32,80,128]{2,1,0:T(8,128)(2,1)S(1)}, u32[]{:S(2)}, u32[]{:S(2)}) async-start(bf16[32,80,128]{2,1,0:T(8,128)(2,1)} %attend.1), calls=%async_computation.3 | async-start | bytes 1310720 | tf_op jit(solution)/shard_map/all_to_all | solution.py:41
  107.7 0.9 tiled.1
  108.7 10.1 %all-to-all-done.3.terms = bf16[32,80,128]{2,1,0:T(8,128)(2,1)S(1)} async-done(((bf16[32,80,128]{2,1,0:T(8,128)(2,1)}), bf16[32,80,128]{2,1,0:T(8,128)(2,1)S(1)}, u32[]{:S(2)}, u32[]{:S(2)}) %all-to-all-start.3) | async-done | bytes 655392 | tf_op jit(solution)/shard_map/all_to_all | solution.py:41
  118.8 6.7 %all-to-all-start.1 = ((bf16[16,40,128]{2,1,0:T(8,128)(2,1)}), bf16[16,40,128]{2,1,0:T(8,128)(2,1)S(1)}, u32[]{:S(2)}, u32[]{:S(2)}) async-start(bf16[16,40,128]{2,1,0:T(8,128)(2,1)} %tiled.1), calls=%async_computation.1 | async-start | bytes 327680 | tf_op jit(solution)/shard_map/all_to_all | solution.py:41
  125.5 0.1 sum_heads.1
  125.6 8.9 %collective-permute-start.7 = (bf16[32,2,320]{2,1,0:T(2,128)(2,1)S(1)}, bf16[32,2,320]{2,1,0:T(2,128)(2,1)S(1)}, u32[]{:S(2)}, u32[]{:S(2)}) collective-permute-start(bf16[32,2,320]{2,1,0:T(2,128)(2,1)S(1)} %sum_heads.1), channel_id=1, source_target_pairs={{0,0},{1,32},{2,64},{3,96},{4,128},{5,160},{6,192},{7,224},{8,8},{... | collective-permute-start | bytes 122888 | tf_op jit(solution)/shard_map/ppermute | solution.py:37
  134.5 6.2 %all-to-all-done.1.source = bf16[16,40,128]{2,1,0:T(8,128)(2,1)S(1)} async-done(((bf16[16,40,128]{2,1,0:T(8,128)(2,1)}), bf16[16,40,128]{2,1,0:T(8,128)(2,1)S(1)}, u32[]{:S(2)}, u32[]{:S(2)}) %all-to-all-start.1) | async-done | bytes 163872 | tf_op jit(solution)/shard_map/all_to_all | solution.py:41
  140.8 0.8 copied.1
  141.5 5.1 %collective-permute-done.7 = bf16[32,2,320]{2,1,0:T(2,128)(2,1)S(1)} collective-permute-done((bf16[32,2,320]{2,1,0:T(2,128)(2,1)S(1)}, bf16[32,2,320]{2,1,0:T(2,128)(2,1)S(1)}, u32[]{:S(2)}, u32[]{:S(2)}) %collective-permute-start.7) | collective-permute-done | bytes 40992 | tf_op jit(solution)/shard_map/ppermute | solution.py:37
  146.6 0.6 copy.13
  (4 shorter events, 0.1 us)
Async XLA Ops:
  0.6 31.6 %all-to-all-start = ((bf16[16,4,4,320]{3,2,1,0:T(4,128)(2,1)}), bf16[16,4,4,320]{3,2,1,0:T(4,128)(2,1)S(1)}, u32[]{:S(2)}, u32[]{:S(2)}) async-start(bf16[16,4,4,320]{3,2,1,0:T(4,128)(2,1)} %param.6), calls=%async_computation | async-start | bytes 393216 | tf_op jit(solution)/shard_map/all_to_all | solution.py:41
  32.4 7.5 %collective-permute-start = (bf16[32,8,320]{2,1,0:T(8,128)(2,1)S(1)}, bf16[32,8,320]{2,1,0:T(8,128)(2,1)S(1)}, u32[]{:S(2)}, u32[]{:S(2)}) collective-permute-start(bf16[32,8,320]{2,1,0:T(8,128)(2,1)S(1)} %reshape.33.own), channel_id=1, source_target_pairs={{0,32},{32,0},{1,33},{33,1},{2,34},{34,2},{3,35},{35,3},{4,36},{36... | collective-permute-start | bytes 491528 | tf_op jit(solution)/shard_map/ppermute | solution.py:45
  34.4 5.4 %collective-permute-start.1 = (bf16[32,2,320]{2,1,0:T(2,128)(2,1)S(1)}, bf16[32,2,320]{2,1,0:T(2,128)(2,1)S(1)}, u32[]{:S(2)}, u32[]{:S(2)}) collective-permute-start(bf16[32,2,320]{2,1,0:T(2,128)(2,1)S(1)} %broadcast_select_fusion.2), channel_id=1, source_target_pairs={{0,416},{32,128},{128,32},{160,256},{256,160},{288,384},{384,288},... | collective-permute-start | bytes 122888 | tf_op jit(solution)/shard_map/ppermute | solution.py:37
  40.1 23.4 %copy-start = (bf16[3,64,320]{2,1,0:T(8,128)(2,1)S(1)}, bf16[3,64,320]{2,1,0:T(8,128)(2,1)}, u32[]{:S(2)}) copy-start(bf16[3,64,320]{2,1,0:T(8,128)(2,1)} %param.9) | copy-start | bytes 368644
  40.2 23.4 %copy-start.1 = (bf16[64,320]{1,0:T(8,128)(2,1)S(1)}, bf16[64,320]{1,0:T(8,128)(2,1)}, u32[]{:S(2)}) copy-start(bf16[64,320]{1,0:T(8,128)(2,1)} %param.11) | copy-start | bytes 122884
  40.2 8.7 %collective-permute-start.2 = (bf16[32,320]{1,0:T(8,128)(2,1)S(1)}, bf16[32,320]{1,0:T(8,128)(2,1)S(1)}, u32[]{:S(2)}, u32[]{:S(2)}) collective-permute-start(bf16[32,320]{1,0:T(8,128)(2,1)S(1)} %get-tuple-element.8), channel_id=1, source_target_pairs={{0,8},{8,16},{16,24},{24,0},{1,9},{9,17},{17,25},{25,1},{2,10},{10... | collective-permute-start | bytes 61448 | tf_op jit(solution)/shard_map/ppermute | solution.py:37
  43.7 5.7 %collective-permute-start.3 = (bf16[32,320]{1,0:T(8,128)(2,1)S(1)}, bf16[32,320]{1,0:T(8,128)(2,1)S(1)}, u32[]{:S(2)}, u32[]{:S(2)}) collective-permute-start(bf16[32,320]{1,0:T(8,128)(2,1)S(1)} %get-tuple-element.9), channel_id=1, source_target_pairs={{0,24},{8,0},{16,8},{24,16},{1,25},{9,1},{17,9},{25,17},{2,26},{10... | collective-permute-start | bytes 61448 | tf_op jit(solution)/shard_map/ppermute | solution.py:37
  56.3 33.8 %all-to-all-start.2 = ((bf16[16,64,320]{2,1,0:T(8,128)(2,1)}), bf16[16,64,320]{2,1,0:T(8,128)(2,1)S(1)}, u32[]{:S(2)}, u32[]{:S(2)}) async-start(bf16[16,64,320]{2,1,0:T(8,128)(2,1)} %get-tuple-element.11), calls=%async_computation.2 | async-start | bytes 1572864 | tf_op jit(solution)/shard_map/all_to_all | solution.py:41
  63.6 23.1 %collective-permute-start.4 = (bf16[272,320]{1,0:T(8,128)(2,1)S(1)}, bf16[272,320]{1,0:T(8,128)(2,1)S(1)}, u32[]{:S(2)}, u32[]{:S(2)}) collective-permute-start(bf16[272,320]{1,0:T(8,128)(2,1)S(1)} %fusion.1), channel_id=1, source_target_pairs={{0,68},{1,69},{2,198},{3,199},{4,256},{5,257},{6,386},{7,387},{32,... | collective-permute-start | bytes 522248 | tf_op jit(solution)/shard_map/ppermute | solution.py:37
  86.7 3.3 %collective-permute-start.5 = (bf16[272,320]{1,0:T(8,128)(2,1)S(1)}, bf16[272,320]{1,0:T(8,128)(2,1)S(1)}, u32[]{:S(2)}, u32[]{:S(2)}) collective-permute-start(bf16[272,320]{1,0:T(8,128)(2,1)S(1)} %collective-permute-done.4), channel_id=1, source_target_pairs={{0,32},{32,0},{1,33},{33,1},{2,34},{34,2},{3,35},{35,3},{4,36},{36... | collective-permute-start | bytes 522248 | tf_op jit(solution)/shard_map/ppermute | solution.py:45
  90.8 3.8 %collective-permute-start.6 = (bf16[1024,256]{1,0:T(8,128)(2,1)S(1)}, bf16[1024,256]{1,0:T(8,128)(2,1)S(1)}, u32[]{:S(2)}, u32[]{:S(2)}) collective-permute-start(bf16[1024,256]{1,0:T(8,128)(2,1)S(1)} %get-tuple-element.13.pair), channel_id=1, source_target_pairs={{0,32},{32,0},{1,33},{33,1},{2,34},{34,2},{3,35},{35,3},{4,36},{36... | collective-permute-start | bytes 1572872 | tf_op jit(solution)/shard_map/ppermute | solution.py:45
  99.8 19.0 %all-to-all-start.3 = ((bf16[32,80,128]{2,1,0:T(8,128)(2,1)}), bf16[32,80,128]{2,1,0:T(8,128)(2,1)S(1)}, u32[]{:S(2)}, u32[]{:S(2)}) async-start(bf16[32,80,128]{2,1,0:T(8,128)(2,1)} %attend.1), calls=%async_computation.3 | async-start | bytes 1310720 | tf_op jit(solution)/shard_map/all_to_all | solution.py:41
  118.8 22.0 %all-to-all-start.1 = ((bf16[16,40,128]{2,1,0:T(8,128)(2,1)}), bf16[16,40,128]{2,1,0:T(8,128)(2,1)S(1)}, u32[]{:S(2)}, u32[]{:S(2)}) async-start(bf16[16,40,128]{2,1,0:T(8,128)(2,1)} %tiled.1), calls=%async_computation.1 | async-start | bytes 327680 | tf_op jit(solution)/shard_map/all_to_all | solution.py:41
  125.6 21.0 %collective-permute-start.7 = (bf16[32,2,320]{2,1,0:T(2,128)(2,1)S(1)}, bf16[32,2,320]{2,1,0:T(2,128)(2,1)S(1)}, u32[]{:S(2)}, u32[]{:S(2)}) collective-permute-start(bf16[32,2,320]{2,1,0:T(2,128)(2,1)S(1)} %sum_heads.1), channel_id=1, source_target_pairs={{0,0},{1,32},{2,64},{3,96},{4,128},{5,160},{6,192},{7,224},{8,8},{... | collective-permute-start | bytes 122888 | tf_op jit(solution)/shard_map/ppermute | solution.py:37

commit v8 on v7

--- a/solution.py
+++ b/solution.py
@@ -168,8 +168,8 @@
     same = ((place >> 4) == (index >> 3) * 2 + (index & 1)) & (
         ((place >> 1) & 3) == ((index >> 2) & 1) * 2 + ((index >> 1) & 1)
     )
-    pooled = dot(jnp.where(same, 0.25, 0.0).astype(BF), fresh).astype(BF)
-    pool[...] = pooled
+    pooled = dot(jnp.where(same, 0.25, 0.0).astype(BF), fresh)
+    pool[...] = dense(pooled).astype(BF)
     copies = [pltpu.make_async_copy(pool, pool_out.at[slot], sent.at[slot]) for slot in range(16)]
     for copy in copies:
         copy.start()
@@ -183,7 +183,7 @@
         conv_kernel,
         out_shape=(
             jax.ShapeDtypeStruct((256, C), BF),
-            jax.ShapeDtypeStruct((16, 64, C), BF),
+            jax.ShapeDtypeStruct((16, 160, 128), BF),
         ),
         out_specs=(pl.BlockSpec(memory_space=pltpu.VMEM), pl.BlockSpec(memory_space=pltpu.HBM)),
         in_specs=[pl.BlockSpec(memory_space=pltpu.SMEM)]
@@ -196,7 +196,7 @@
             pltpu.VMEM((256, 3 * C), BF),
             pltpu.VMEM((2, 3, 3, C, C), BF),
             pltpu.SemaphoreType.DMA((6,)),
-            pltpu.VMEM((64, C), BF),
+            pltpu.VMEM((160, 128), BF),
             pltpu.SemaphoreType.DMA((16,)),
         ],
         cost_estimate=pl.CostEstimate(
@@ -237,7 +237,15 @@
         return jnp.concatenate([near[start : start + 64], far[start : start + 64]], 0)
 
     matrix = jnp.concatenate([both(0), both(64), both(128)], 0)
-    projected = dot_t(tokens[...], matrix)
+    wide = jnp.concatenate(
+        [tokens[:, 0:64].reshape(1024, 128), tokens[:, 64:128].reshape(1024, 128)], 1
+    )
+    tail = tokens[:, 128:160].reshape(512, 128)
+    none = jnp.zeros((384, 64), BF)
+    upper = dot_t(tail, jnp.concatenate([matrix[:, 256:C], none], 1)).reshape(16, 32, 384)
+    lower = dot_t(tail, jnp.concatenate([none, matrix[:, 256:C]], 1)).reshape(16, 32, 384)
+    projected = dot_t(wide, matrix[:, 0:256])
+    projected = projected + jnp.concatenate([upper, lower], 1).reshape(1024, 384)
     query_gain = near[256:257, 0:128].astype(F32) + far[257:258, 0:128].astype(F32)
     key_gain = near[258:259, 0:128].astype(F32) + far[259:260, 0:128].astype(F32)
     query_out[...] = norm(projected[:, 0:128], query_gain * (128 ** (-0.5) * math.log2(math.e)))
@@ -281,7 +289,9 @@
         attended = dot(shifted.astype(BF), pair[:, 128:256])
         attended = attended + dot(shifted_far.astype(BF), pair_far[:, 128:256])
         attended = (attended / total).astype(BF)
-        terms = dot(attended, head_out) + tokens[rows].astype(F32) * 0.0625
+        terms = dot(attended, head_out) + undense(
+            tokens[pl.ds(step * 4, 4)].astype(F32)
+        ).reshape(256, C) * 0.0625
         for column in range(8):
             parts = [
                 terms[y * 64 + column * 8 : y * 64 + column * 8 + 8] for y in range(4)
@@ -384,7 +394,7 @@
 
     fresh, pooled = conv_stack(core, own, other, edge, before, after, conv_weight, conv_gain)
 
-    tokens = exchange(pooled, ("x", "y")).reshape(1024, C)
+    tokens = exchange(pooled, ("x", "y"))
     feature_tiles = tiled(fresh)
     features = exchange(feature_tiles, DEPTH)
 

time: 148 us -> 148 us (level)
  no operation moved by 1% of the time
where the time goes in v8:
time: 148 us; the launch traced here: 147 us
  waiting for transfers between devices  65.9 us (45%)
  starting transfers between devices  63 us (43%)
  Pallas kernels  14.9 us (10%)
  local copies, waits for them, and re-layouts  1.54 us (1%)
    all_to_all x4, starting transfers between devices, exchange(): return lax.all_to_all(array, axes, split_axis=0, concat_axis=0, tiled=True)  36.8 us
    all_to_all x4, waiting for transfers between devices, exchange(): return lax.all_to_all(array, axes, split_axis=0, concat_axis=0, tiled=True)  32.8 us
    ppermute x5, waiting for transfers between devices, move(): return lax.ppermute(array, axes, pairs)  30 us
    ppermute x5, starting transfers between devices, move(): return lax.ppermute(array, axes, pairs)  20.4 us
    pallas_call x1, Pallas kernels, conv_stack(): pl.pallas_call(conv_kernel, out_shape=(jax.ShapeDtypeStruct((256, C), BF)...  6.92 us
    ppermute x3, starting transfers between devices, swap(): return lax.ppermute(array, 'c', [(0, 1), (1, 0)])  5.87 us
    pallas_call x1, Pallas kernels, attend(): pl.pallas_call(attend_kernel, out_shape=jax.ShapeDtypeStruct((32, 80, 128...  5.09 us
    ppermute x3, waiting for transfers between devices, swap(): return lax.ppermute(array, 'c', [(0, 1), (1, 0)])  3.18 us
  transfers between devices with their start and end apart: 12, of which 9 were waited for; matrix products, arithmetic and copies ran while one was open for 1% of the time, Pallas kernels for 1%

profile of v8, /device:TPU:16, one launch (start us, length us, event | category | flops | bytes accessed | tf_op | source)
XLA Modules:
  0.0 147.1 jit_solution(1455440507827447086)
XLA Ops:
  0.6 15.2 %all-to-all-start = ((bf16[16,4,4,320]{3,2,1,0:T(4,128)(2,1)}), bf16[16,4,4,320]{3,2,1,0:T(4,128)(2,1)S(1)}, u32[]{:S(2)}, u32[]{:S(2)}) async-start(bf16[16,4,4,320]{3,2,1,0:T(4,128)(2,1)} %param.6), calls=%async_computation | async-start | bytes 393216 | tf_op jit(solution)/shard_map/all_to_all | solution.py:41
  15.9 16.4 %all-to-all-done = bf16[16,4,4,320]{3,2,1,0:T(4,128)(2,1)S(1)} async-done(((bf16[16,4,4,320]{3,2,1,0:T(4,128)(2,1)}), bf16[16,4,4,320]{3,2,1,0:T(4,128)(2,1)S(1)}, u32[]{:S(2)}, u32[]{:S(2)}) %all-to-all-start) | async-done | bytes 163872 | tf_op jit(solution)/shard_map/all_to_all | solution.py:41
  32.2 0.1 copy.11
  32.3 0.1 reshape.30.own
  32.4 1.9 %collective-permute-start = (bf16[32,8,320]{2,1,0:T(8,128)(2,1)S(1)}, bf16[32,8,320]{2,1,0:T(8,128)(2,1)S(1)}, u32[]{:S(2)}, u32[]{:S(2)}) collective-permute-start(bf16[32,8,320]{2,1,0:T(8,128)(2,1)S(1)} %reshape.30.own), channel_id=1, source_target_pairs={{0,32},{32,0},{1,33},{33,1},{2,34},{34,2},{3,35},{35,3},{4,36},{36... | collective-permute-start | bytes 491528 | tf_op jit(solution)/shard_map/ppermute | solution.py:45
  34.3 0.1 broadcast_select_fusion.2
  34.4 2.5 %collective-permute-start.1 = (bf16[32,2,320]{2,1,0:T(2,128)(2,1)S(1)}, bf16[32,2,320]{2,1,0:T(2,128)(2,1)S(1)}, u32[]{:S(2)}, u32[]{:S(2)}) collective-permute-start(bf16[32,2,320]{2,1,0:T(2,128)(2,1)S(1)} %broadcast_select_fusion.2), channel_id=1, source_target_pairs={{0,416},{32,128},{128,32},{160,256},{256,160},{288,384},{384,288},... | collective-permute-start | bytes 122888 | tf_op jit(solution)/shard_map/ppermute | solution.py:37
  36.9 2.9 %collective-permute-done.1 = bf16[32,2,320]{2,1,0:T(2,128)(2,1)S(1)} collective-permute-done((bf16[32,2,320]{2,1,0:T(2,128)(2,1)S(1)}, bf16[32,2,320]{2,1,0:T(2,128)(2,1)S(1)}, u32[]{:S(2)}, u32[]{:S(2)}) %collective-permute-start.1) | collective-permute-done | bytes 40992 | tf_op jit(solution)/shard_map/ppermute | solution.py:37
  39.9 0.0 collective-permute-done.other
  39.9 0.0 copy-start
  39.9 0.0 copy-start.1
  39.9 0.2 border.1
  40.2 3.4 %collective-permute-start.2 = (bf16[32,320]{1,0:T(8,128)(2,1)S(1)}, bf16[32,320]{1,0:T(8,128)(2,1)S(1)}, u32[]{:S(2)}, u32[]{:S(2)}) collective-permute-start(bf16[32,320]{1,0:T(8,128)(2,1)S(1)} %get-tuple-element.8), channel_id=1, source_target_pairs={{0,8},{8,16},{16,24},{24,0},{1,9},{9,17},{17,25},{25,1},{2,10},{10... | collective-permute-start | bytes 61448 | tf_op jit(solution)/shard_map/ppermute | solution.py:37
  43.6 3.7 %collective-permute-start.3 = (bf16[32,320]{1,0:T(8,128)(2,1)S(1)}, bf16[32,320]{1,0:T(8,128)(2,1)S(1)}, u32[]{:S(2)}, u32[]{:S(2)}) collective-permute-start(bf16[32,320]{1,0:T(8,128)(2,1)S(1)} %get-tuple-element.9), channel_id=1, source_target_pairs={{0,24},{8,0},{16,8},{24,16},{1,25},{9,1},{17,9},{25,17},{2,26},{10... | collective-permute-start | bytes 61448 | tf_op jit(solution)/shard_map/ppermute | solution.py:37
  47.2 0.8 fusion.2
  48.0 0.7 pad.16.gains
  48.7 0.0 collective-permute-done.2.before
  48.7 0.6 collective-permute-done.3.after
  49.3 6.9 %conv_stack.1 = (bf16[256,320]{1,0:T(8,128)(2,1)S(1)}, bf16[16,160,128]{2,1,0:T(8,128)(2,1)}) custom-call(s32[1]{0:T(128)} %bitcast.core, bf16[32,8,320]{2,1,0:T(8,128)(2,1)S(1)} %reshape.30.own, bf16[32,8,320]{2,1,0:T(8,128)(2,1)S(1)} %collective-permute-done.other, bf16[64,320]{1,0:T(8,128)(2,1)S(1)} %reshape.31.edge, ...), custom_call_target="tpu_custom_call" | custom-call | flops 1946419200 | bytes 5000000 | tf_op jit(solution)/shard_map/conv_stack/pallas_call | solution.py:182
  56.2 7.2 %all-to-all-start.2 = ((bf16[16,160,128]{2,1,0:T(8,128)(2,1)}), bf16[16,160,128]{2,1,0:T(8,128)(2,1)S(1)}, u32[]{:S(2)}, u32[]{:S(2)}) async-start(bf16[16,160,128]{2,1,0:T(8,128)(2,1)} %get-tuple-element.11), calls=%async_computation.2 | async-start | bytes 1310720 | tf_op jit(solution)/shard_map/all_to_all | solution.py:41
  63.4 0.0 copy-done
  63.4 0.0 copy-done.1
  63.5 2.0 %collective-permute-start.4 = (bf16[272,320]{1,0:T(8,128)(2,1)S(1)}, bf16[272,320]{1,0:T(8,128)(2,1)S(1)}, u32[]{:S(2)}, u32[]{:S(2)}) collective-permute-start(bf16[272,320]{1,0:T(8,128)(2,1)S(1)} %fusion.1), channel_id=1, source_target_pairs={{0,68},{1,69},{2,198},{3,199},{4,256},{5,257},{6,386},{7,387},{32,... | collective-permute-start | bytes 522248 | tf_op jit(solution)/shard_map/ppermute | solution.py:37
  65.5 21.3 %collective-permute-done.4 = bf16[272,320]{1,0:T(8,128)(2,1)S(1)} collective-permute-done((bf16[272,320]{1,0:T(8,128)(2,1)S(1)}, bf16[272,320]{1,0:T(8,128)(2,1)S(1)}, u32[]{:S(2)}, u32[]{:S(2)}) %collective-permute-start.4) | collective-permute-done | bytes 174112 | tf_op jit(solution)/shard_map/ppermute | solution.py:37
  86.9 1.9 %collective-permute-start.5 = (bf16[272,320]{1,0:T(8,128)(2,1)S(1)}, bf16[272,320]{1,0:T(8,128)(2,1)S(1)}, u32[]{:S(2)}, u32[]{:S(2)}) collective-permute-start(bf16[272,320]{1,0:T(8,128)(2,1)S(1)} %collective-permute-done.4), channel_id=1, source_target_pairs={{0,32},{32,0},{1,33},{33,1},{2,34},{34,2},{3,35},{35,3},{4,36},{36... | collective-permute-start | bytes 522248 | tf_op jit(solution)/shard_map/ppermute | solution.py:45
  88.8 1.4 collective-permute-done.5
  90.2 0.0 all-to-all-done.2.tokens
  90.3 0.7 heads.1
  91.0 2.0 %collective-permute-start.6 = (bf16[1024,256]{1,0:T(8,128)(2,1)S(1)}, bf16[1024,256]{1,0:T(8,128)(2,1)S(1)}, u32[]{:S(2)}, u32[]{:S(2)}) collective-permute-start(bf16[1024,256]{1,0:T(8,128)(2,1)S(1)} %get-tuple-element.13.pair), channel_id=1, source_target_pairs={{0,32},{32,0},{1,33},{33,1},{2,34},{34,2},{3,35},{35,3},{4,36},{36... | collective-permute-start | bytes 1572872 | tf_op jit(solution)/shard_map/ppermute | solution.py:45
  93.1 1.8 %collective-permute-done.6.pair_far = bf16[1024,256]{1,0:T(8,128)(2,1)S(1)} collective-permute-done((bf16[1024,256]{1,0:T(8,128)(2,1)S(1)}, bf16[1024,256]{1,0:T(8,128)(2,1)S(1)}, u32[]{:S(2)}, u32[]{:S(2)}) %collective-permute-start.6) | collective-permute-done | bytes 524320 | tf_op jit(solution)/shard_map/ppermute | solution.py:45
  94.8 5.1 %attend.1 = bf16[32,80,128]{2,1,0:T(8,128)(2,1)} custom-call(bf16[1024,128]{1,0:T(8,128)(2,1)S(1)} %get-tuple-element.12.query, bf16[1024,256]{1,0:T(8,128)(2,1)S(1)} %get-tuple-element.13.pair, bf16[1024,256]{1,0:T(8,128)(2,1)S(1)} %collective-permute-done.6.pair_far, bf16[16,160,128]{2,1,0:T(8,128)(2,1)S(1)} %all-to-all-done.2.tokens, ...), custom_call_target="tpu_custom_call" | custom-call | flops 1157627904 | bytes 3000000 | tf_op jit(solution)/shard_map/attend/pallas_call | solution.py:309
  99.9 7.1 %all-to-all-start.3 = ((bf16[32,80,128]{2,1,0:T(8,128)(2,1)}), bf16[32,80,128]{2,1,0:T(8,128)(2,1)S(1)}, u32[]{:S(2)}, u32[]{:S(2)}) async-start(bf16[32,80,128]{2,1,0:T(8,128)(2,1)} %attend.1), calls=%async_computation.3 | async-start | bytes 1310720 | tf_op jit(solution)/shard_map/all_to_all | solution.py:41
  107.0 0.9 tiled.1
  107.9 10.1 %all-to-all-done.3.terms = bf16[32,80,128]{2,1,0:T(8,128)(2,1)S(1)} async-done(((bf16[32,80,128]{2,1,0:T(8,128)(2,1)}), bf16[32,80,128]{2,1,0:T(8,128)(2,1)S(1)}, u32[]{:S(2)}, u32[]{:S(2)}) %all-to-all-start.3) | async-done | bytes 655392 | tf_op jit(solution)/shard_map/all_to_all | solution.py:41
  118.1 7.3 %all-to-all-start.1 = ((bf16[16,40,128]{2,1,0:T(8,128)(2,1)}), bf16[16,40,128]{2,1,0:T(8,128)(2,1)S(1)}, u32[]{:S(2)}, u32[]{:S(2)}) async-start(bf16[16,40,128]{2,1,0:T(8,128)(2,1)} %tiled.1), calls=%async_computation.1 | async-start | bytes 327680 | tf_op jit(solution)/shard_map/all_to_all | solution.py:41
  125.3 0.1 sum_heads.1
  125.5 8.9 %collective-permute-start.7 = (bf16[32,2,320]{2,1,0:T(2,128)(2,1)S(1)}, bf16[32,2,320]{2,1,0:T(2,128)(2,1)S(1)}, u32[]{:S(2)}, u32[]{:S(2)}) collective-permute-start(bf16[32,2,320]{2,1,0:T(2,128)(2,1)S(1)} %sum_heads.1), channel_id=1, source_target_pairs={{0,0},{1,32},{2,64},{3,96},{4,128},{5,160},{6,192},{7,224},{8,8},{... | collective-permute-start | bytes 122888 | tf_op jit(solution)/shard_map/ppermute | solution.py:37
  134.4 6.2 %all-to-all-done.1.source = bf16[16,40,128]{2,1,0:T(8,128)(2,1)S(1)} async-done(((bf16[16,40,128]{2,1,0:T(8,128)(2,1)}), bf16[16,40,128]{2,1,0:T(8,128)(2,1)S(1)}, u32[]{:S(2)}, u32[]{:S(2)}) %all-to-all-start.1) | async-done | bytes 163872 | tf_op jit(solution)/shard_map/all_to_all | solution.py:41
  140.6 0.8 copied.1
  141.4 5.1 %collective-permute-done.7 = bf16[32,2,320]{2,1,0:T(2,128)(2,1)S(1)} collective-permute-done((bf16[32,2,320]{2,1,0:T(2,128)(2,1)S(1)}, bf16[32,2,320]{2,1,0:T(2,128)(2,1)S(1)}, u32[]{:S(2)}, u32[]{:S(2)}) %collective-permute-start.7) | collective-permute-done | bytes 40992 | tf_op jit(solution)/shard_map/ppermute | solution.py:37
  146.5 0.6 copy.13
  (4 shorter events, 0.1 us)
Async XLA Ops:
  0.6 31.6 %all-to-all-start = ((bf16[16,4,4,320]{3,2,1,0:T(4,128)(2,1)}), bf16[16,4,4,320]{3,2,1,0:T(4,128)(2,1)S(1)}, u32[]{:S(2)}, u32[]{:S(2)}) async-start(bf16[16,4,4,320]{3,2,1,0:T(4,128)(2,1)} %param.6), calls=%async_computation | async-start | bytes 393216 | tf_op jit(solution)/shard_map/all_to_all | solution.py:41
  32.4 7.5 %collective-permute-start = (bf16[32,8,320]{2,1,0:T(8,128)(2,1)S(1)}, bf16[32,8,320]{2,1,0:T(8,128)(2,1)S(1)}, u32[]{:S(2)}, u32[]{:S(2)}) collective-permute-start(bf16[32,8,320]{2,1,0:T(8,128)(2,1)S(1)} %reshape.30.own), channel_id=1, source_target_pairs={{0,32},{32,0},{1,33},{33,1},{2,34},{34,2},{3,35},{35,3},{4,36},{36... | collective-permute-start | bytes 491528 | tf_op jit(solution)/shard_map/ppermute | solution.py:45
  34.4 5.4 %collective-permute-start.1 = (bf16[32,2,320]{2,1,0:T(2,128)(2,1)S(1)}, bf16[32,2,320]{2,1,0:T(2,128)(2,1)S(1)}, u32[]{:S(2)}, u32[]{:S(2)}) collective-permute-start(bf16[32,2,320]{2,1,0:T(2,128)(2,1)S(1)} %broadcast_select_fusion.2), channel_id=1, source_target_pairs={{0,416},{32,128},{128,32},{160,256},{256,160},{288,384},{384,288},... | collective-permute-start | bytes 122888 | tf_op jit(solution)/shard_map/ppermute | solution.py:37
  39.9 23.6 %copy-start = (bf16[3,64,320]{2,1,0:T(8,128)(2,1)S(1)}, bf16[3,64,320]{2,1,0:T(8,128)(2,1)}, u32[]{:S(2)}) copy-start(bf16[3,64,320]{2,1,0:T(8,128)(2,1)} %param.9) | copy-start | bytes 368644
  39.9 23.5 %copy-start.1 = (bf16[64,320]{1,0:T(8,128)(2,1)S(1)}, bf16[64,320]{1,0:T(8,128)(2,1)}, u32[]{:S(2)}) copy-start(bf16[64,320]{1,0:T(8,128)(2,1)} %param.11) | copy-start | bytes 122884
  40.2 8.6 %collective-permute-start.2 = (bf16[32,320]{1,0:T(8,128)(2,1)S(1)}, bf16[32,320]{1,0:T(8,128)(2,1)S(1)}, u32[]{:S(2)}, u32[]{:S(2)}) collective-permute-start(bf16[32,320]{1,0:T(8,128)(2,1)S(1)} %get-tuple-element.8), channel_id=1, source_target_pairs={{0,8},{8,16},{16,24},{24,0},{1,9},{9,17},{17,25},{25,1},{2,10},{10... | collective-permute-start | bytes 61448 | tf_op jit(solution)/shard_map/ppermute | solution.py:37
  43.6 5.7 %collective-permute-start.3 = (bf16[32,320]{1,0:T(8,128)(2,1)S(1)}, bf16[32,320]{1,0:T(8,128)(2,1)S(1)}, u32[]{:S(2)}, u32[]{:S(2)}) collective-permute-start(bf16[32,320]{1,0:T(8,128)(2,1)S(1)} %get-tuple-element.9), channel_id=1, source_target_pairs={{0,24},{8,0},{16,8},{24,16},{1,25},{9,1},{17,9},{25,17},{2,26},{10... | collective-permute-start | bytes 61448 | tf_op jit(solution)/shard_map/ppermute | solution.py:37
  56.2 34.0 %all-to-all-start.2 = ((bf16[16,160,128]{2,1,0:T(8,128)(2,1)}), bf16[16,160,128]{2,1,0:T(8,128)(2,1)S(1)}, u32[]{:S(2)}, u32[]{:S(2)}) async-start(bf16[16,160,128]{2,1,0:T(8,128)(2,1)} %get-tuple-element.11), calls=%async_computation.2 | async-start | bytes 1310720 | tf_op jit(solution)/shard_map/all_to_all | solution.py:41
  63.5 23.4 %collective-permute-start.4 = (bf16[272,320]{1,0:T(8,128)(2,1)S(1)}, bf16[272,320]{1,0:T(8,128)(2,1)S(1)}, u32[]{:S(2)}, u32[]{:S(2)}) collective-permute-start(bf16[272,320]{1,0:T(8,128)(2,1)S(1)} %fusion.1), channel_id=1, source_target_pairs={{0,68},{1,69},{2,198},{3,199},{4,256},{5,257},{6,386},{7,387},{32,... | collective-permute-start | bytes 522248 | tf_op jit(solution)/shard_map/ppermute | solution.py:37
  86.9 3.3 %collective-permute-start.5 = (bf16[272,320]{1,0:T(8,128)(2,1)S(1)}, bf16[272,320]{1,0:T(8,128)(2,1)S(1)}, u32[]{:S(2)}, u32[]{:S(2)}) collective-permute-start(bf16[272,320]{1,0:T(8,128)(2,1)S(1)} %collective-permute-done.4), channel_id=1, source_target_pairs={{0,32},{32,0},{1,33},{33,1},{2,34},{34,2},{3,35},{35,3},{4,36},{36... | collective-permute-start | bytes 522248 | tf_op jit(solution)/shard_map/ppermute | solution.py:45
  91.0 3.8 %collective-permute-start.6 = (bf16[1024,256]{1,0:T(8,128)(2,1)S(1)}, bf16[1024,256]{1,0:T(8,128)(2,1)S(1)}, u32[]{:S(2)}, u32[]{:S(2)}) collective-permute-start(bf16[1024,256]{1,0:T(8,128)(2,1)S(1)} %get-tuple-element.13.pair), channel_id=1, source_target_pairs={{0,32},{32,0},{1,33},{33,1},{2,34},{34,2},{3,35},{35,3},{4,36},{36... | collective-permute-start | bytes 1572872 | tf_op jit(solution)/shard_map/ppermute | solution.py:45
  99.9 18.2 %all-to-all-start.3 = ((bf16[32,80,128]{2,1,0:T(8,128)(2,1)}), bf16[32,80,128]{2,1,0:T(8,128)(2,1)S(1)}, u32[]{:S(2)}, u32[]{:S(2)}) async-start(bf16[32,80,128]{2,1,0:T(8,128)(2,1)} %attend.1), calls=%async_computation.3 | async-start | bytes 1310720 | tf_op jit(solution)/shard_map/all_to_all | solution.py:41
  118.1 22.5 %all-to-all-start.1 = ((bf16[16,40,128]{2,1,0:T(8,128)(2,1)}), bf16[16,40,128]{2,1,0:T(8,128)(2,1)S(1)}, u32[]{:S(2)}, u32[]{:S(2)}) async-start(bf16[16,40,128]{2,1,0:T(8,128)(2,1)} %tiled.1), calls=%async_computation.1 | async-start | bytes 327680 | tf_op jit(solution)/shard_map/all_to_all | solution.py:41
  125.5 21.0 %collective-permute-start.7 = (bf16[32,2,320]{2,1,0:T(2,128)(2,1)S(1)}, bf16[32,2,320]{2,1,0:T(2,128)(2,1)S(1)}, u32[]{:S(2)}, u32[]{:S(2)}) collective-permute-start(bf16[32,2,320]{2,1,0:T(2,128)(2,1)S(1)} %sum_heads.1), channel_id=1, source_target_pairs={{0,0},{1,32},{2,64},{3,96},{4,128},{5,160},{6,192},{7,224},{8,8},{... | collective-permute-start | bytes 122888 | tf_op jit(solution)/shard_map/ppermute | solution.py:37
